TPU v7x, 32 devices: a whole 2x2x4 slice. The times are simulated.
32 devices in a mesh: groups: 2 (over y), wide: 8 (over z, x), narrow: 2 (over core).
Axes of the slice: x: 2, y: 2, z: 4, core: 2. Of those that a mesh axis runs over, the one named last changes fastest.
Arguments:
- pieces: bfloat16 [2, 1024, 8192], P(None, ('groups', 'wide'), 'narrow'), parts along dimension 1, may hold values from -6 to 6
- destination: int32 [512], P('wide'), may hold values from 0 to 511, as said below
- first_offset: int32 [512], P('wide'), may hold values from 0 to 6144, as said below
- valid_length: int32 [512], P('wide'), may hold values from 2048 to 8192
- midpoint_factor: float32 [1024, 128], P(('groups', 'wide')), parts along dimension 0, may hold values from -0.3 to 0.3
- offset_factor: float32 [16384, 128], P(('groups', 'narrow')), parts along dimension 0, may hold values from -6 to 6
- threshold: float32 [16384], P(('groups', 'narrow')), parts along dimension 0, may hold values from 0.3 to 3
Outputs:
- sparse: bfloat16 [2, 1024, 8192], P(None, ('groups', 'wide'), 'narrow'), parts along dimension 1
- new_midpoint: float32 [1024, 128], P(('groups', 'wide')), parts along dimension 0
- new_offset: float32 [16384, 128], P(('groups', 'narrow')), parts along dimension 0
There are 2 independent parts, one for each index of `groups`. A program takes and returns all parts, laid end to end along the dimension named above; an argument that names none is the same for every part. Nothing has to cross between parts.
Inputs may be any that keep to these rules, and one draw needn't show every extreme that they name: destination is a permutation of the midpoint rows; the 64 segments of one device (aligned blocks) name at most 16 rows of any aligned block of 64 midpoint rows, and exactly 16 rows of some block. first_offset + valid_length <= 8192.
All inputs are finite; a program needn't handle non-finite values.
Results may differ from a plain program's by a relative error of at most 0.005.
Values may be sent and summed in bfloat16 or wider, within the bound.
No kernel may reach another device: no remote copies, remote signals or barrier semaphores. Data moves between devices by JAX's collectives and lax.ppermute only.
A program may use at most 64 MiB of HBM per device.

v0:
```python
from functools import partial

import jax
import jax.numpy as jnp
from jax import lax
from jax.experimental import pallas as pl
from jax.experimental.pallas import tpu as pltpu
from jax.sharding import PartitionSpec as P


epsilon = 1e-06
F32 = jnp.float32
BF16 = jnp.bfloat16
PAD = 8
NEAR = 2


def turned(rows):
    half = rows.shape[1] // 2
    return jnp.concatenate([rows[:, half:], -rows[:, :half]], 1)


def unturned(rows):
    half = rows.shape[1] // 2
    return jnp.concatenate([-rows[:, half:], rows[:, :half]], 1)


def both_halves(norm):
    half = norm.shape[1] // 2
    once = norm[:, :half] + norm[:, half:]
    return jnp.concatenate([once, once], 1)


def parts_of(piece_real, piece_imag, left_low, right_low, level):
    rows = left_low.shape[0]
    pair = jnp.concatenate([left_low, turned(left_low)], 0)
    model = lax.dot_general(pair, right_low, (((1,), (1,)), ((), ())), preferred_element_type=F32)
    real = piece_real.astype(F32) - model[:rows]
    imag = piece_imag.astype(F32) - model[rows:]
    kept = level * lax.rsqrt(jnp.maximum(real * real + imag * imag, level * level))
    return pair, real, imag, kept


def live_mask(begin, end, first_col, count):
    column = lax.broadcasted_iota(jnp.int32, (begin.shape[0], count), 1)
    return (column >= begin - first_col) & (column < end - first_col)


def masked_error(real, imag, kept, inside):
    share = jnp.where(inside, kept, 0.0)
    return jnp.concatenate([(real * share).astype(BF16), (imag * share).astype(BF16)], 0)


def header_body(rows_ref, dest_ref, first_ref, valid_ref, out_ref):
    count, tall, width = out_ref.shape
    rows = tall - PAD
    first = first_ref[...]
    top = jnp.concatenate([dest_ref[...], first], 1).astype(F32)
    end = (first + valid_ref[...]).astype(F32)
    low = jnp.concatenate([end, jnp.zeros_like(end)], 1)
    numbers = jnp.concatenate([top, low, jnp.zeros((PAD - 2, width), F32)], 0)
    for target in range(count):
        out_ref[target, :rows] = rows_ref[...]
        out_ref[target, rows:] = numbers


def split_body(target_ref, piece_ref, *out_refs):
    cols = out_refs[0].shape[2]
    for index, out_ref in enumerate(out_refs):
        start = pl.multiple_of(target_ref[index] * cols, cols)
        out_ref[...] = piece_ref[:, :, pl.ds(start, cols)]


def rows_body(base_ref, piece_ref, left_ref, right_ref, level_ref, begin_ref, end_ref, grad_ref, acc_ref, norm_ref):
    rows, width = left_ref.shape
    block = column_block(right_ref.shape[0])
    low = left_ref[...].astype(BF16)
    begin = begin_ref[...]
    end = end_ref[...]
    acc_ref[...] = jnp.zeros_like(acc_ref)
    norm_ref[...] = jnp.zeros_like(norm_ref)

    @pl.loop(0, right_ref.shape[0] // block)
    def _(step):
        start = step * block
        at = pl.ds(pl.multiple_of(start, block), block)
        right = right_ref[at, :]
        right_low = right.astype(BF16)
        _, real, imag, kept = parts_of(piece_ref[0, :, at], piece_ref[1, :, at], low, right_low, level_ref[:, at])
        error = masked_error(real, imag, kept, live_mask(begin, end, base_ref[0] + start, block))
        acc_ref[...] += jnp.dot(error, right_low, preferred_element_type=F32)
        norm_ref[...] += jnp.sum((right * right).reshape(-1, 8, width), 0)

    grad_ref[:rows] = acc_ref[:rows] + unturned(acc_ref[rows:])
    grad_ref[rows:] = jnp.broadcast_to(jnp.sum(norm_ref[...], 0, keepdims=True), (PAD, width))


def step_body(mine_ref, *refs):
    *other_refs, move_ref, out_ref = refs
    total = mine_ref[...]
    for other_ref in other_refs:
        total = total + other_ref[...]
    rows = total.shape[0] - PAD
    move = (total[:rows] / (both_halves(total[rows : rows + 1]) + epsilon)).astype(BF16)
    move_ref[...] = move
    for target in range(out_ref.shape[0]):
        out_ref[target] = move


def cols_body(counts, second, base_ref, source_ref, *refs):
    piece_refs, refs = refs[: len(counts)], refs[len(counts) :]
    if second:
        left_ref, move_ref, header_ref, right_ref, level_ref, change_ref, out_ref, acc_ref, part_ref = refs
    else:
        left_ref, header_ref, right_ref, level_ref, next_ref, low_ref, acc_ref = refs
    sources, tall, width = header_ref.shape
    rows = tall - PAD
    cols = right_ref.shape[0]
    right = right_ref[...]
    right_low = right.astype(BF16)
    level = level_ref[...]
    acc_ref[...] = jnp.zeros_like(acc_ref)
    if second:
        part_ref[...] = jnp.zeros_like(part_ref)

    def one(piece_real, piece_imag, source):
        at = pl.ds(pl.multiple_of(source * rows, rows), rows)
        left = left_ref[at, :]
        if second:
            left = left + move_ref[at, :].astype(F32)
        numbers = header_ref[source, rows:, :]
        standing = numbers.T.astype(jnp.int32)
        begin = standing[rows : 2 * rows, 0:1]
        end = standing[:rows, 1:2]
        pair, real, imag, kept = parts_of(piece_real, piece_imag, left.astype(BF16), right_low, level)
        error = masked_error(real, imag, kept, live_mask(begin, end, base_ref[0], cols))
        acc_ref[...] += lax.dot_general(pair, error, (((0,), (0,)), ((), ())), preferred_element_type=F32)
        if second:
            part = jnp.dot(error, right_low, preferred_element_type=F32)
            part = (part[:rows] + unturned(part[rows:])).astype(BF16)
            named = numbers[0:1, :rows].astype(jnp.int32)
            row = lax.broadcasted_iota(jnp.int32, (sources * rows, rows), 0)
            place = jnp.where(row == named, 1.0, 0.0).astype(BF16)
            part_ref[...] += jnp.dot(place, part, preferred_element_type=F32)

    index = 0
    for count, piece_ref in zip(counts, piece_refs):
        if count == 1:
            one(piece_ref[0], piece_ref[1], source_ref[index])
        else:

            @pl.loop(0, count)
            def _(slot, piece_ref=piece_ref, index=index):
                one(piece_ref[slot, 0], piece_ref[slot, 1], source_ref[index + slot])

        index += count

    left = left_ref[...]
    if second:
        left = left + move_ref[...].astype(F32)
    left_norm = both_halves(jnp.sum(left * left, 0, keepdims=True))
    after = right + acc_ref[...].T / (left_norm + epsilon)
    if not second:
        next_ref[...] = after
        low_ref[...] = after.astype(BF16)
        return
    change_ref[...] = (after - right_low.astype(F32)).astype(BF16)
    norm = jnp.sum(right * right, 0, keepdims=True)
    high = norm.astype(BF16).astype(F32)
    tail = jnp.concatenate([high, norm - high, jnp.zeros((PAD - 2, width), F32)], 0).astype(BF16)
    for target in range(sources):
        out_ref[target, :rows] = part_ref[target * rows : (target + 1) * rows].astype(BF16)
        out_ref[target, rows:] = tail


def sparse_body(counts, base_ref, source_ref, piece_ref, left_ref, move_ref, level_ref, begin_ref, end_ref, *refs):
    right_refs, out_ref = refs[:-1], refs[-1]
    low = (left_ref[...] + move_ref[...].astype(F32)).astype(BF16)
    begin = begin_ref[...]
    end = end_ref[...]

    def one(right, source):
        cols = right.shape[0]
        start = source * cols
        at = pl.ds(pl.multiple_of(start, cols), cols)
        _, real, imag, kept = parts_of(piece_ref[0, :, at], piece_ref[1, :, at], low, right, level_ref[:, at])
        share = jnp.where(live_mask(begin, end, base_ref[0] + start, cols), 1.0 - kept, 0.0)
        out_ref[0, :, at] = (real * share).astype(BF16)
        out_ref[1, :, at] = (imag * share).astype(BF16)

    index = 0
    for count, right_ref in zip(counts, right_refs):
        if count == 1:
            one(right_ref[...], source_ref[index])
        else:
            wide = max(1, 128 // right_ref.shape[1])
            block = wide * right_ref.shape[1]

            @pl.loop(0, count // wide)
            def _(slot, right_ref=right_ref):
                one(right_ref[pl.ds(slot * wide, wide)].reshape(block, right_ref.shape[2]), slot)

        index += count


def join_body(counts, source_ref, *refs):
    low_refs, change_refs, out_ref = refs[: len(counts)], refs[len(counts) : -1], refs[-1]
    index = 0
    for count, low_ref, change_ref in zip(counts, low_refs, change_refs):
        if count == 1:
            cols = low_ref.shape[0]
            at = pl.ds(pl.multiple_of(source_ref[index] * cols, cols), cols)
            out_ref[at, :] = low_ref[...].astype(F32) + change_ref[...].astype(F32)
        else:
            total = low_ref[...].astype(F32) + change_ref[...].astype(F32)
            out_ref[...] = total.reshape(out_ref.shape)
        index += count


VMEM = pl.BlockSpec(memory_space=pltpu.VMEM)
SMEM = pl.BlockSpec(memory_space=pltpu.SMEM)


def call(body, shapes, scalars, arrays, scratch=()):
    return pl.pallas_call(
        body,
        in_specs=[SMEM] * len(scalars) + [VMEM] * len(arrays),
        out_specs=jax.tree.map(lambda _: VMEM, shapes),
        out_shape=shapes,
        scratch_shapes=list(scratch),
    )(*scalars, *arrays)


def column_block(count):
    block = min(512, count)
    while count % block:
        block //= 2
    return block


def rows_at(table, index):
    return table.at[index].get(mode="promise_in_bounds")


def exchange(blocks):
    return lax.all_to_all(blocks, "wide", split_axis=0, concat_axis=0, tiled=True)


def other_narrow(value):
    count = lax.axis_size("narrow")
    return [lax.ppermute(value, "narrow", [(i, (i + k) % count) for i in range(count)]) for k in range(1, count)]


def small_wide():
    count = lax.axis_size("wide")
    return count % NEAR == 0 and count <= 4 * NEAR


def shift(value, far, near):
    outer = lax.axis_size("wide") // NEAR
    pairs = [
        (z * NEAR + x, (z + far) % outer * NEAR + (x + near) % NEAR) for z in range(outer) for x in range(NEAR)
    ]
    return lax.ppermute(value, "wide", pairs)


def device_at(far, near):
    outer = lax.axis_size("wide") // NEAR
    me = lax.axis_index("wide")
    return (me // NEAR + far) % outer * NEAR + (me % NEAR + near) % NEAR


def far_first(outer):
    return sorted(range(1, outer), key=lambda far: -min(far, outer - far))


def send_parts(pieces):
    count = lax.axis_size("wide")
    _, rows, cols = pieces.shape
    part = cols // count
    if not small_wide():
        blocks = exchange(jnp.transpose(pieces.reshape(2, rows, count, part), (2, 0, 1, 3)))
        return [blocks], (count,), jnp.arange(count, dtype=jnp.int32)
    outer = count // NEAR
    ways = [(far, near) for far in far_first(outer) for near in range(NEAR)] + [(0, near) for near in range(NEAR)]
    ways = [way for way in ways if way != (0, 0)] + [(0, 0)]
    targets = jnp.stack([device_at(*way) for way in ways]).astype(jnp.int32)
    shapes = [jax.ShapeDtypeStruct((2, rows, part), pieces.dtype)] * count
    parts = call(split_body, shapes, [targets], [pieces])
    arrived = [block if way == (0, 0) else shift(block, *way) for way, block in zip(ways, parts)]
    sources = jnp.stack([device_at(-far, -near) for far, near in ways]).astype(jnp.int32)
    return arrived, (1,) * count, sources


def gather_parts(block):
    count = lax.axis_size("wide")
    if not small_wide():
        blocks = exchange(jnp.broadcast_to(block[None], (count,) + block.shape))
        return [blocks], (count,), jnp.arange(count, dtype=jnp.int32)
    outer = count // NEAR
    held = [(block, 0, 0)]
    held += [(shift(block, 0, near), 0, near) for near in range(1, NEAR)]
    first = [(shift(block, far, 0), far) for far in range(1, outer)]
    for arrived, far in first:
        held.append((arrived, far, 0))
        held += [(shift(arrived, 0, near), far, near) for near in range(1, NEAR)]
    sources = jnp.stack([device_at(-far, -near) for _, far, near in held]).astype(jnp.int32)
    return [value for value, _, _ in held], (1,) * count, sources


def body(pieces, destination, first_offset, valid_length, midpoint_factor, offset_factor, threshold):
    count = lax.axis_size("wide")
    _, rows, cols = pieces.shape
    width = offset_factor.shape[1]
    part = cols // count
    total = count * rows
    me = lax.axis_index("wide")
    base = lax.axis_index("narrow") * cols
    base_all = jnp.full((1,), base, jnp.int32)
    base_part = jnp.full((1,), base + me * part, jnp.int32)
    level = threshold[None, :]
    begin = first_offset[:, None]
    end = begin + valid_length[:, None]

    header = call(
        header_body,
        jax.ShapeDtypeStruct((count, rows + PAD, width), F32),
        [],
        [midpoint_factor, destination[None], first_offset[None], valid_length[None]],
    )
    headers = exchange(header)
    blocks, block_counts, block_sources = send_parts(pieces)

    all_rows = headers[:, :rows].reshape(total, width)
    left_mine = rows_at(all_rows, destination)
    row_grad = call(
        rows_body,
        jax.ShapeDtypeStruct((rows + PAD, width), F32),
        [base_all],
        [pieces, left_mine, offset_factor, level, begin, end],
        [pltpu.VMEM((2 * rows, width), F32), pltpu.VMEM((8, width), F32)],
    )
    move_mine, moves = call(
        step_body,
        [jax.ShapeDtypeStruct((rows, width), BF16), jax.ShapeDtypeStruct((count, rows, width), BF16)],
        [],
        [row_grad] + other_narrow(row_grad),
    )
    move_all = exchange(moves).reshape(total, width)

    dest_all = headers[:, rows, :rows].astype(jnp.int32).reshape(total)
    left_all = rows_at(all_rows, dest_all)
    right_part = lax.dynamic_slice_in_dim(offset_factor, me * part, part, 0)
    level_part = lax.dynamic_slice_in_dim(level, me * part, part, 1)
    right_one, right_low = call(
        partial(cols_body, block_counts, False),
        [jax.ShapeDtypeStruct((part, width), F32), jax.ShapeDtypeStruct((part, width), BF16)],
        [base_part, block_sources],
        [*blocks, left_all, headers, right_part, level_part],
        [pltpu.VMEM((width, part), F32)],
    )
    lows, counts, sources = gather_parts(right_low)

    change, outgoing = call(
        partial(cols_body, block_counts, True),
        [jax.ShapeDtypeStruct((part, width), BF16), jax.ShapeDtypeStruct((count, rows + PAD, width), BF16)],
        [base_part, block_sources],
        [*blocks, left_all, move_all, headers, right_one, level_part],
        [pltpu.VMEM((width, part), F32), pltpu.VMEM((total, width), F32)],
    )
    changes, _, _ = gather_parts(change)

    my_rows = me * rows + jnp.arange(rows, dtype=jnp.int32)
    order = jnp.arange(total, dtype=jnp.int32)
    my_segments = jnp.sum(jnp.where(dest_all[None, :] == my_rows[:, None], order[None, :], 0), 1)
    first_step = rows_at(move_all, my_segments).astype(F32)
    arrived = exchange(outgoing)
    summed = jnp.sum(arrived.astype(F32), 0)
    for other in other_narrow(summed):
        summed = summed + other
    norm_two = both_halves(summed[rows : rows + 1] + summed[rows + 1 : rows + 2])
    new_midpoint = midpoint_factor + first_step + summed[:rows] / (norm_two + epsilon)

    sparse = call(
        partial(sparse_body, counts),
        jax.ShapeDtypeStruct(pieces.shape, BF16),
        [base_all, sources],
        [pieces, left_mine, move_mine, level, begin, end, *lows],
    )
    new_offset = call(
        partial(join_body, counts), jax.ShapeDtypeStruct((cols, width), F32), [sources], [*lows, *changes]
    )
    return sparse, new_midpoint, new_offset


def solution(mesh):
    placed = (
        P(None, ("groups", "wide"), "narrow"),
        P("wide"),
        P("wide"),
        P("wide"),
        P(("groups", "wide"), None),
        P(("groups", "narrow"), None),
        P(("groups", "narrow")),
    )
    return jax.shard_map(
        body,
        mesh=mesh,
        in_specs=placed,
        out_specs=(
            P(None, ("groups", "wide"), "narrow"),
            P(("groups", "wide"), None),
            P(("groups", "narrow"), None),
        ),
        check_vma=False,
    )
```

profile of v0, /device:TPU:0, one launch (start us, length us, event | category | flops | bytes accessed | tf_op | source)
XLA Modules:
  0.0 110.0 jit_solution(11113720692497629656)
XLA Ops:
  1.4 2.3 %shard_map.97 = (bf16[2,64,512]{2,1,0:T(8,128)(2,1)}, bf16[2,64,512]{2,1,0:T(8,128)(2,1)}, bf16[2,64,512]{2,1,0:T(8,128)(2,1)}, bf16[2,64,512]{2,1,0:T(8,128)(2,...) custom-call(s32[8]{0:T(128)} %stack.80.target_ref, ...), custom_call_target="tpu_custom_call" | custom-call | tf_op jit(solution)/shard_map/pallas_call | solution.py:225
  3.7 4.1 %collective-permute-start.1 = (bf16[2,64,512]{2,1,0:T(8,128)(2,1)}, bf16[2,64,512]{2,1,0:T(8,128)(2,1)S(1)}, u32[]{:S(2)}, u32[]{:S(2)}) collective-permute-start(bf16[2,64,512]{2,1,0:T(8,128)(2,1)} %get-tuple-element.18), channel_id=1, source_target_pairs={{0,8},{2,10},{4,12},{6,14},{8,0},{10,2},{12,4},{14,6},{1,9},{3,11}... | collective-permute-start | bytes 393224 | tf_op jit(solution)/shard_map/ppermute | solution.py:264
  7.7 1.3 %collective-permute-start.2 = (bf16[2,64,512]{2,1,0:T(8,128)(2,1)}, bf16[2,64,512]{2,1,0:T(8,128)(2,1)S(1)}, u32[]{:S(2)}, u32[]{:S(2)}) collective-permute-start(bf16[2,64,512]{2,1,0:T(8,128)(2,1)} %get-tuple-element.19), channel_id=1, source_target_pairs={{0,10},{2,8},{4,14},{6,12},{8,2},{10,0},{12,6},{14,4},{1,11},{3,9}... | collective-permute-start | bytes 393224 | tf_op jit(solution)/shard_map/ppermute | solution.py:264
  9.0 1.6 %collective-permute-start.3 = (bf16[2,64,512]{2,1,0:T(8,128)(2,1)}, bf16[2,64,512]{2,1,0:T(8,128)(2,1)S(1)}, u32[]{:S(2)}, u32[]{:S(2)}) collective-permute-start(bf16[2,64,512]{2,1,0:T(8,128)(2,1)} %get-tuple-element.20), channel_id=1, source_target_pairs={{0,4},{2,6},{4,8},{6,10},{8,12},{10,14},{12,0},{14,2},{1,5},{3,7},... | collective-permute-start | bytes 393224 | tf_op jit(solution)/shard_map/ppermute | solution.py:264
  10.6 1.5 %collective-permute-start.4 = (bf16[2,64,512]{2,1,0:T(8,128)(2,1)}, bf16[2,64,512]{2,1,0:T(8,128)(2,1)S(1)}, u32[]{:S(2)}, u32[]{:S(2)}) collective-permute-start(bf16[2,64,512]{2,1,0:T(8,128)(2,1)} %get-tuple-element.21), channel_id=1, source_target_pairs={{0,6},{2,4},{4,10},{6,8},{8,14},{10,12},{12,2},{14,0},{1,7},{3,5},... | collective-permute-start | bytes 393224 | tf_op jit(solution)/shard_map/ppermute | solution.py:264
  12.1 2.2 %collective-permute-start.5 = (bf16[2,64,512]{2,1,0:T(8,128)(2,1)}, bf16[2,64,512]{2,1,0:T(8,128)(2,1)S(1)}, u32[]{:S(2)}, u32[]{:S(2)}) collective-permute-start(bf16[2,64,512]{2,1,0:T(8,128)(2,1)} %get-tuple-element.22), channel_id=1, source_target_pairs={{0,12},{2,14},{4,0},{6,2},{8,4},{10,6},{12,8},{14,10},{1,13},{3,15... | collective-permute-start | bytes 393224 | tf_op jit(solution)/shard_map/ppermute | solution.py:264
  14.4 1.6 %shard_map.94 = f32[8,72,128]{2,1,0:T(8,128)} custom-call(f32[64,128]{1,0:T(8,128)} %rows_ref.1, s32[1,64]{1,0:T(1,128)} %bitcast.47, s32[1,64]{1,0:T(1,128)} %bitcast.45, s32[1,64]{1,0:T(1,128)} %bitcast.48), custom_call_target="tpu_custom_call" | custom-call | tf_op jit(solution)/shard_map/pallas_call | solution.py:225
  15.9 3.4 %all-to-all-start = ((f32[8,72,128]{2,1,0:T(8,128)}), f32[8,72,128]{2,1,0:T(8,128)S(1)}, u32[]{:S(2)}, u32[]{:S(2)}) async-start(f32[8,72,128]{2,1,0:T(8,128)} %shard_map.94), calls=%async_computation | async-start | bytes 589824 | tf_op jit(solution)/shard_map/all_to_all | solution.py:246
  19.4 1.7 %constant_dynamic-slice_fusion.refs_10_ = f32[512,128]{1,0:T(8,128)} fusion(f32[4096,128]{1,0:T(8,128)} %right_ref.1, s32[]{:T(128)S(6)} %select_n.241), kind=kLoop, calls=%fused_computation.20 | loop fusion | bytes 524292 | tf_op jit(solution)/shard_map/dynamic_slice | solution.py:353
  21.2 1.4 %dynamic-slice.3 = f32[512]{0:T(512)} dynamic-slice(f32[4096]{0:T(1024)} %param.13, s32[]{:T(128)S(6)} %select_n.241), dynamic_slice_sizes={512} | dynamic-slice | bytes 4100 | tf_op jit(solution)/shard_map/dynamic-slice
  24.6 10.1 %all-to-all-done.refs_9_.refs_10_ = f32[8,72,128]{2,1,0:T(8,128)S(1)} async-done(((f32[8,72,128]{2,1,0:T(8,128)}), f32[8,72,128]{2,1,0:T(8,128)S(1)}, u32[]{:S(2)}, u32[]{:S(2)}) %all-to-all-start) | async-done | bytes 294944 | tf_op jit(solution)/shard_map/all_to_all | solution.py:246
  34.7 4.5 %collective-permute-start.6 = (bf16[2,64,512]{2,1,0:T(8,128)(2,1)}, bf16[2,64,512]{2,1,0:T(8,128)(2,1)S(1)}, u32[]{:S(2)}, u32[]{:S(2)}) collective-permute-start(bf16[2,64,512]{2,1,0:T(8,128)(2,1)} %get-tuple-element.23), channel_id=1, source_target_pairs={{0,14},{2,12},{4,2},{6,0},{8,6},{10,4},{12,10},{14,8},{1,15},{3,13... | collective-permute-start | bytes 393224 | tf_op jit(solution)/shard_map/ppermute | solution.py:264
  41.0 6.0 %shard_map.95.mine_ref = f32[72,128]{1,0:T(8,128)} custom-call(s32[1]{0:T(128)} %bitcast.base_ref, bf16[2,64,4096]{2,1,0:T(8,128)(2,1)} %piece_ref.5, f32[64,128]{1,0:T(8,128)} %gather_fusion, f32[4096,128]{1,0:T(8,128)} %right_ref.1, f32[1,4096]{1,0:T(1,128)} %bitcast.39, s32[64,1]{1,0:T(8,128)} %copy.14.begin_ref, s32[64,1]{1,0:T(8,128)} %copy.15.end_ref), custom_call_target="tpu_custom_call" | custom-call | tf_op jit(solution)/shard_map/pallas_call | solution.py:225
  47.0 1.6 %gather_fusion.1 = f32[512,128]{1,0:T(8,128)} fusion(f32[512,128]{1,0:T(8,128)S(1)} %bitcast.36, s32[1024]{0:T(1024)S(1)} %pad_clamp_fusion.1), kind=kCustom, calls=%fused_computation.1 | custom fusion | bytes 526336 | tf_op jit(solution)/shard_map/gather | solution.py:242
  49.5 4.7 %shard_map.98 = (f32[512,128]{1,0:T(8,128)}, bf16[512,128]{1,0:T(8,128)(2,1)}) custom-call(s32[1]{0:T(128)} %bitcast.16.base_ref, s32[8]{0:T(128)} %stack.72.source_ref, bf16[2,64,512]{2,1,0:T(8,128)(2,1)} %copy-done.3, bf16[2,64,512]{2,1,0:T(8,128)(2,1)} %copy-done.4, bf16[2,64,512]{2,1,0:T(8,128)(2,1)} %copy-done.5, bf16[2,64,512]{2,1,0:T(8,128)(2,1)} %copy-done.6, ...), custom_call_target="tpu_custom_call" | custom-call | tf_op jit(solution)/shard_map/pallas_call | solution.py:225
  54.8 1.6 %shard_map.96 = (bf16[64,128]{1,0:T(8,128)(2,1)}, bf16[8,64,128]{2,1,0:T(8,128)(2,1)}) custom-call(f32[72,128]{1,0:T(8,128)} %shard_map.95.mine_ref, f32[72,128]{1,0:T(8,128)} %copy-done.25), custom_call_target="tpu_custom_call" | custom-call | tf_op jit(solution)/shard_map/pallas_call | solution.py:225
  56.5 6.0 %all-to-all-start.1 = ((bf16[8,64,128]{2,1,0:T(8,128)(2,1)}), bf16[8,64,128]{2,1,0:T(8,128)(2,1)S(1)}, u32[]{:S(2)}, u32[]{:S(2)}) async-start(bf16[8,64,128]{2,1,0:T(8,128)(2,1)} %get-tuple-element.27), calls=%async_computation.1 | async-start | bytes 262144 | tf_op jit(solution)/shard_map/all_to_all | solution.py:246
  63.1 2.9 %collective-permute-start.11 = (bf16[512,128]{1,0:T(8,128)(2,1)}, bf16[512,128]{1,0:T(8,128)(2,1)S(1)}, u32[]{:S(2)}, u32[]{:S(2)}) collective-permute-start(bf16[512,128]{1,0:T(8,128)(2,1)} %get-tuple-element.26.refs_0_), channel_id=1, source_target_pairs={{0,8},{2,10},{4,12},{6,14},{8,0},{10,2},{12,4},{14,6},{1,9},{3,11}... | collective-permute-start | bytes 393224 | tf_op jit(solution)/shard_map/ppermute | solution.py:264
  66.0 1.5 %collective-permute-start.13 = (bf16[512,128]{1,0:T(8,128)(2,1)}, bf16[512,128]{1,0:T(8,128)(2,1)S(1)}, u32[]{:S(2)}, u32[]{:S(2)}) collective-permute-start(bf16[512,128]{1,0:T(8,128)(2,1)} %get-tuple-element.26.refs_0_), channel_id=1, source_target_pairs={{0,12},{2,14},{4,0},{6,2},{8,4},{10,6},{12,8},{14,10},{1,13},{3,15... | collective-permute-start | bytes 393224 | tf_op jit(solution)/shard_map/ppermute | solution.py:264
  67.5 1.5 %collective-permute-start.8 = (bf16[512,128]{1,0:T(8,128)(2,1)}, bf16[512,128]{1,0:T(8,128)(2,1)S(1)}, u32[]{:S(2)}, u32[]{:S(2)}) collective-permute-start(bf16[512,128]{1,0:T(8,128)(2,1)} %get-tuple-element.26.refs_0_), channel_id=1, source_target_pairs={{0,2},{2,0},{4,6},{6,4},{8,10},{10,8},{12,14},{14,12},{1,3},{3,1},... | collective-permute-start | bytes 393224 | tf_op jit(solution)/shard_map/ppermute | solution.py:264
  70.3 2.2 %all-to-all-done.1 = bf16[8,64,128]{2,1,0:T(8,128)(2,1)S(1)} async-done(((bf16[8,64,128]{2,1,0:T(8,128)(2,1)}), bf16[8,64,128]{2,1,0:T(8,128)(2,1)S(1)}, u32[]{:S(2)}, u32[]{:S(2)}) %all-to-all-start.1) | async-done | bytes 131104 | tf_op jit(solution)/shard_map/all_to_all | solution.py:246
  73.2 6.0 %shard_map.100 = (bf16[512,128]{1,0:T(8,128)(2,1)}, bf16[8,72,128]{2,1,0:T(8,128)(2,1)}) custom-call(s32[1]{0:T(128)} %bitcast.16.base_ref, s32[8]{0:T(128)} %stack.72.source_ref, bf16[2,64,512]{2,1,0:T(8,128)(2,1)} %copy-done.3, bf16[2,64,512]{2,1,0:T(8,128)(2,1)} %copy-done.4, bf16[2,64,512]{2,1,0:T(8,128)(2,1)} %copy-done.5, ...), custom_call_target="tpu_custom_call" | custom-call | tf_op jit(solution)/shard_map/pallas_call | solution.py:225
  79.2 5.9 %all-to-all-start.2 = ((bf16[8,72,128]{2,1,0:T(8,128)(2,1)}), bf16[8,72,128]{2,1,0:T(8,128)(2,1)S(1)}, u32[]{:S(2)}, u32[]{:S(2)}) async-start(bf16[8,72,128]{2,1,0:T(8,128)(2,1)} %get-tuple-element.29), calls=%async_computation.2 | async-start | bytes 294912 | tf_op jit(solution)/shard_map/all_to_all | solution.py:246
  85.2 2.1 %collective-permute-start.12 = (bf16[512,128]{1,0:T(8,128)(2,1)S(1)}, bf16[512,128]{1,0:T(8,128)(2,1)S(1)}, u32[]{:S(2)}, u32[]{:S(2)}) collective-permute-start(bf16[512,128]{1,0:T(8,128)(2,1)S(1)} %collective-permute-done.11.refs_4_), channel_id=1, source_target_pairs={{0,2},{2,0},{4,6},{6,4},{8,10},{10,8},{12,14},{14,12},{1,3},{3,1},... | collective-permute-start | bytes 393224 | tf_op jit(solution)/shard_map/ppermute | solution.py:264
  87.4 1.9 %collective-permute-start.17 = (bf16[512,128]{1,0:T(8,128)(2,1)}, bf16[512,128]{1,0:T(8,128)(2,1)S(1)}, u32[]{:S(2)}, u32[]{:S(2)}) collective-permute-start(bf16[512,128]{1,0:T(8,128)(2,1)} %get-tuple-element.30.refs_8_), channel_id=1, source_target_pairs={{0,4},{2,6},{4,8},{6,10},{8,12},{10,14},{12,0},{14,2},{1,5},{3,7},... | collective-permute-start | bytes 393224 | tf_op jit(solution)/shard_map/ppermute | solution.py:264
  89.4 2.4 %collective-permute-start.19 = (bf16[512,128]{1,0:T(8,128)(2,1)}, bf16[512,128]{1,0:T(8,128)(2,1)S(1)}, u32[]{:S(2)}, u32[]{:S(2)}) collective-permute-start(bf16[512,128]{1,0:T(8,128)(2,1)} %get-tuple-element.30.refs_8_), channel_id=1, source_target_pairs={{0,8},{2,10},{4,12},{6,14},{8,0},{10,2},{12,4},{14,6},{1,9},{3,11}... | collective-permute-start | bytes 393224 | tf_op jit(solution)/shard_map/ppermute | solution.py:264
  91.7 1.5 %collective-permute-start.21 = (bf16[512,128]{1,0:T(8,128)(2,1)}, bf16[512,128]{1,0:T(8,128)(2,1)S(1)}, u32[]{:S(2)}, u32[]{:S(2)}) collective-permute-start(bf16[512,128]{1,0:T(8,128)(2,1)} %get-tuple-element.30.refs_8_), channel_id=1, source_target_pairs={{0,12},{2,14},{4,0},{6,2},{8,4},{10,6},{12,8},{14,10},{1,13},{3,15... | collective-permute-start | bytes 393224 | tf_op jit(solution)/shard_map/ppermute | solution.py:264
  93.2 1.5 %collective-permute-start.16 = (bf16[512,128]{1,0:T(8,128)(2,1)}, bf16[512,128]{1,0:T(8,128)(2,1)S(1)}, u32[]{:S(2)}, u32[]{:S(2)}) collective-permute-start(bf16[512,128]{1,0:T(8,128)(2,1)} %get-tuple-element.30.refs_8_), channel_id=1, source_target_pairs={{0,2},{2,0},{4,6},{6,4},{8,10},{10,8},{12,14},{14,12},{1,3},{3,1},... | collective-permute-start | bytes 393224 | tf_op jit(solution)/shard_map/ppermute | solution.py:264
  94.7 1.7 %collective-permute-start.18 = (bf16[512,128]{1,0:T(8,128)(2,1)S(1)}, bf16[512,128]{1,0:T(8,128)(2,1)S(1)}, u32[]{:S(2)}, u32[]{:S(2)}) collective-permute-start(bf16[512,128]{1,0:T(8,128)(2,1)S(1)} %collective-permute-done.17.refs_10_), channel_id=1, source_target_pairs={{0,2},{2,0},{4,6},{6,4},{8,10},{10,8},{12,14},{14,12},{1,3},{3,1},... | collective-permute-start | bytes 393224 | tf_op jit(solution)/shard_map/ppermute | solution.py:264
  97.3 1.9 %collective-permute-start.20 = (bf16[512,128]{1,0:T(8,128)(2,1)S(1)}, bf16[512,128]{1,0:T(8,128)(2,1)S(1)}, u32[]{:S(2)}, u32[]{:S(2)}) collective-permute-start(bf16[512,128]{1,0:T(8,128)(2,1)S(1)} %collective-permute-done.19.refs_12_), channel_id=1, source_target_pairs={{0,2},{2,0},{4,6},{6,4},{8,10},{10,8},{12,14},{14,12},{1,3},{3,1},... | collective-permute-start | bytes 393224 | tf_op jit(solution)/shard_map/ppermute | solution.py:264
  100.4 3.6 %shard_map.99 = bf16[2,64,4096]{2,1,0:T(8,128)(2,1)} custom-call(s32[1]{0:T(128)} %bitcast.base_ref, s32[8]{0:T(128)} %stack.71.source_ref, bf16[2,64,4096]{2,1,0:T(8,128)(2,1)} %piece_ref.5, f32[64,128]{1,0:T(8,128)} %gather_fusion, bf16[64,128]{1,0:T(8,128)(2,1)} %get-tuple-element.17.move_ref, f32[1,4096]{1,0:T(1,128)} %bitcast.40, ...), custom_call_target="tpu_custom_call" | custom-call | tf_op jit(solution)/shard_map/pallas_call | solution.py:225
  106.0 3.1 %shard_map.101 = f32[4096,128]{1,0:T(8,128)} custom-call(s32[8]{0:T(128)} %stack.71.source_ref, bf16[512,128]{1,0:T(8,128)(2,1)} %get-tuple-element.26.refs_0_, bf16[512,128]{1,0:T(8,128)(2,1)} %copy-done.11, bf16[512,128]{1,0:T(8,128)(2,1)} %copy-done.8, bf16[512,128]{1,0:T(8,128)(2,1)} %copy-done.12, bf16[512,128]{1,0:T(8,128)(2,1)} %copy-done.9, ...), custom_call_target="tpu_custom_call" | custom-call | tf_op jit(solution)/shard_map/pallas_call | solution.py:225
  (116 shorter events, 13.6 us)
Async XLA Ops:
  0.6 20.4 %copy-start.26 = (s32[64]{0:T(128)S(1)}, s32[64]{0:T(128)}, u32[]{:S(2)}) copy-start(s32[64]{0:T(128)} %param.9) | copy-start | bytes 772
  0.6 20.4 %copy-start.28 = (s32[64]{0:T(128)S(1)}, s32[64]{0:T(128)}, u32[]{:S(2)}) copy-start(s32[64]{0:T(128)} %param.10) | copy-start | bytes 772
  0.7 20.4 %copy-start.27 = (s32[64]{0:T(128)S(1)}, s32[64]{0:T(128)}, u32[]{:S(2)}) copy-start(s32[64]{0:T(128)} %param.8) | copy-start | bytes 772
  3.7 31.0 %collective-permute-start.1 = (bf16[2,64,512]{2,1,0:T(8,128)(2,1)}, bf16[2,64,512]{2,1,0:T(8,128)(2,1)S(1)}, u32[]{:S(2)}, u32[]{:S(2)}) collective-permute-start(bf16[2,64,512]{2,1,0:T(8,128)(2,1)} %get-tuple-element.18), channel_id=1, source_target_pairs={{0,8},{2,10},{4,12},{6,14},{8,0},{10,2},{12,4},{14,6},{1,9},{3,11}... | collective-permute-start | bytes 393224 | tf_op jit(solution)/shard_map/ppermute | solution.py:264
  7.7 31.5 %collective-permute-start.2 = (bf16[2,64,512]{2,1,0:T(8,128)(2,1)}, bf16[2,64,512]{2,1,0:T(8,128)(2,1)S(1)}, u32[]{:S(2)}, u32[]{:S(2)}) collective-permute-start(bf16[2,64,512]{2,1,0:T(8,128)(2,1)} %get-tuple-element.19), channel_id=1, source_target_pairs={{0,10},{2,8},{4,14},{6,12},{8,2},{10,0},{12,6},{14,4},{1,11},{3,9}... | collective-permute-start | bytes 393224 | tf_op jit(solution)/shard_map/ppermute | solution.py:264
  9.0 38.0 %collective-permute-start.3 = (bf16[2,64,512]{2,1,0:T(8,128)(2,1)}, bf16[2,64,512]{2,1,0:T(8,128)(2,1)S(1)}, u32[]{:S(2)}, u32[]{:S(2)}) collective-permute-start(bf16[2,64,512]{2,1,0:T(8,128)(2,1)} %get-tuple-element.20), channel_id=1, source_target_pairs={{0,4},{2,6},{4,8},{6,10},{8,12},{10,14},{12,0},{14,2},{1,5},{3,7},... | collective-permute-start | bytes 393224 | tf_op jit(solution)/shard_map/ppermute | solution.py:264
  10.6 38.1 %collective-permute-start.4 = (bf16[2,64,512]{2,1,0:T(8,128)(2,1)}, bf16[2,64,512]{2,1,0:T(8,128)(2,1)S(1)}, u32[]{:S(2)}, u32[]{:S(2)}) collective-permute-start(bf16[2,64,512]{2,1,0:T(8,128)(2,1)} %get-tuple-element.21), channel_id=1, source_target_pairs={{0,6},{2,4},{4,10},{6,8},{8,14},{10,12},{12,2},{14,0},{1,7},{3,5},... | collective-permute-start | bytes 393224 | tf_op jit(solution)/shard_map/ppermute | solution.py:264
  12.1 36.6 %collective-permute-start.5 = (bf16[2,64,512]{2,1,0:T(8,128)(2,1)}, bf16[2,64,512]{2,1,0:T(8,128)(2,1)S(1)}, u32[]{:S(2)}, u32[]{:S(2)}) collective-permute-start(bf16[2,64,512]{2,1,0:T(8,128)(2,1)} %get-tuple-element.22), channel_id=1, source_target_pairs={{0,12},{2,14},{4,0},{6,2},{8,4},{10,6},{12,8},{14,10},{1,13},{3,15... | collective-permute-start | bytes 393224 | tf_op jit(solution)/shard_map/ppermute | solution.py:264
  15.9 18.7 %all-to-all-start = ((f32[8,72,128]{2,1,0:T(8,128)}), f32[8,72,128]{2,1,0:T(8,128)S(1)}, u32[]{:S(2)}, u32[]{:S(2)}) async-start(f32[8,72,128]{2,1,0:T(8,128)} %shard_map.94), calls=%async_computation | async-start | bytes 589824 | tf_op jit(solution)/shard_map/all_to_all | solution.py:246
  34.7 14.0 %collective-permute-start.6 = (bf16[2,64,512]{2,1,0:T(8,128)(2,1)}, bf16[2,64,512]{2,1,0:T(8,128)(2,1)S(1)}, u32[]{:S(2)}, u32[]{:S(2)}) collective-permute-start(bf16[2,64,512]{2,1,0:T(8,128)(2,1)} %get-tuple-element.23), channel_id=1, source_target_pairs={{0,14},{2,12},{4,2},{6,0},{8,6},{10,4},{12,10},{14,8},{1,15},{3,13... | collective-permute-start | bytes 393224 | tf_op jit(solution)/shard_map/ppermute | solution.py:264
  39.3 9.5 %collective-permute-start.7 = (bf16[2,64,512]{2,1,0:T(8,128)(2,1)}, bf16[2,64,512]{2,1,0:T(8,128)(2,1)S(1)}, u32[]{:S(2)}, u32[]{:S(2)}) collective-permute-start(bf16[2,64,512]{2,1,0:T(8,128)(2,1)} %get-tuple-element.24), channel_id=1, source_target_pairs={{0,2},{2,0},{4,6},{6,4},{8,10},{10,8},{12,14},{14,12},{1,3},{3,1},... | collective-permute-start | bytes 393224 | tf_op jit(solution)/shard_map/ppermute | solution.py:264
  47.0 7.2 %collective-permute-start = (f32[72,128]{1,0:T(8,128)}, f32[72,128]{1,0:T(8,128)S(1)}, u32[]{:S(2)}, u32[]{:S(2)}) collective-permute-start(f32[72,128]{1,0:T(8,128)} %shard_map.95.mine_ref), channel_id=1, source_target_pairs={{0,1},{1,0},{2,3},{3,2},{4,5},{5,4},{6,7},{7,6},{8,9},{9,8},{10,11... | collective-permute-start | bytes 110600 | tf_op jit(solution)/shard_map/ppermute | solution.py:251
  54.2 14.7 %collective-permute-start.9 = (bf16[512,128]{1,0:T(8,128)(2,1)}, bf16[512,128]{1,0:T(8,128)(2,1)S(1)}, u32[]{:S(2)}, u32[]{:S(2)}) collective-permute-start(bf16[512,128]{1,0:T(8,128)(2,1)} %get-tuple-element.26.refs_0_), channel_id=1, source_target_pairs={{0,4},{2,6},{4,8},{6,10},{8,12},{10,14},{12,0},{14,2},{1,5},{3,7},... | collective-permute-start | bytes 393224 | tf_op jit(solution)/shard_map/ppermute | solution.py:264
  56.5 16.1 %all-to-all-start.1 = ((bf16[8,64,128]{2,1,0:T(8,128)(2,1)}), bf16[8,64,128]{2,1,0:T(8,128)(2,1)S(1)}, u32[]{:S(2)}, u32[]{:S(2)}) async-start(bf16[8,64,128]{2,1,0:T(8,128)(2,1)} %get-tuple-element.27), calls=%async_computation.1 | async-start | bytes 262144 | tf_op jit(solution)/shard_map/all_to_all | solution.py:246
  63.1 22.1 %collective-permute-start.11 = (bf16[512,128]{1,0:T(8,128)(2,1)}, bf16[512,128]{1,0:T(8,128)(2,1)S(1)}, u32[]{:S(2)}, u32[]{:S(2)}) collective-permute-start(bf16[512,128]{1,0:T(8,128)(2,1)} %get-tuple-element.26.refs_0_), channel_id=1, source_target_pairs={{0,8},{2,10},{4,12},{6,14},{8,0},{10,2},{12,4},{14,6},{1,9},{3,11}... | collective-permute-start | bytes 393224 | tf_op jit(solution)/shard_map/ppermute | solution.py:264
  66.0 21.3 %collective-permute-start.13 = (bf16[512,128]{1,0:T(8,128)(2,1)}, bf16[512,128]{1,0:T(8,128)(2,1)S(1)}, u32[]{:S(2)}, u32[]{:S(2)}) collective-permute-start(bf16[512,128]{1,0:T(8,128)(2,1)} %get-tuple-element.26.refs_0_), channel_id=1, source_target_pairs={{0,12},{2,14},{4,0},{6,2},{8,4},{10,6},{12,8},{14,10},{1,13},{3,15... | collective-permute-start | bytes 393224 | tf_op jit(solution)/shard_map/ppermute | solution.py:264
  67.5 21.9 %collective-permute-start.8 = (bf16[512,128]{1,0:T(8,128)(2,1)}, bf16[512,128]{1,0:T(8,128)(2,1)S(1)}, u32[]{:S(2)}, u32[]{:S(2)}) collective-permute-start(bf16[512,128]{1,0:T(8,128)(2,1)} %get-tuple-element.26.refs_0_), channel_id=1, source_target_pairs={{0,2},{2,0},{4,6},{6,4},{8,10},{10,8},{12,14},{14,12},{1,3},{3,1},... | collective-permute-start | bytes 393224 | tf_op jit(solution)/shard_map/ppermute | solution.py:264
  68.9 30.9 %copy-start.8 = (bf16[512,128]{1,0:T(8,128)(2,1)}, bf16[512,128]{1,0:T(8,128)(2,1)S(1)}, u32[]{:S(2)}) copy-start(bf16[512,128]{1,0:T(8,128)(2,1)S(1)} %collective-permute-done.9.refs_2_) | copy-start | bytes 393220
  68.9 22.8 %collective-permute-start.10 = (bf16[512,128]{1,0:T(8,128)(2,1)S(1)}, bf16[512,128]{1,0:T(8,128)(2,1)S(1)}, u32[]{:S(2)}, u32[]{:S(2)}) collective-permute-start(bf16[512,128]{1,0:T(8,128)(2,1)S(1)} %collective-permute-done.9.refs_2_), channel_id=1, source_target_pairs={{0,2},{2,0},{4,6},{6,4},{8,10},{10,8},{12,14},{14,12},{1,3},{3,1},... | collective-permute-start | bytes 393224 | tf_op jit(solution)/shard_map/ppermute | solution.py:264
  79.2 24.8 %copy-start.2 = (bf16[8,64,128]{2,1,0:T(8,128)(2,1)S(1)}, bf16[8,64,128]{2,1,0:T(8,128)(2,1)}, u32[]{:S(2)}) copy-start(bf16[8,64,128]{2,1,0:T(8,128)(2,1)} %copy-done.1) | copy-start | bytes 393220
  79.2 20.5 %all-to-all-start.2 = ((bf16[8,72,128]{2,1,0:T(8,128)(2,1)}), bf16[8,72,128]{2,1,0:T(8,128)(2,1)S(1)}, u32[]{:S(2)}, u32[]{:S(2)}) async-start(bf16[8,72,128]{2,1,0:T(8,128)(2,1)} %get-tuple-element.29), calls=%async_computation.2 | async-start | bytes 294912 | tf_op jit(solution)/shard_map/all_to_all | solution.py:246
  85.2 14.6 %copy-start.9 = (bf16[512,128]{1,0:T(8,128)(2,1)}, bf16[512,128]{1,0:T(8,128)(2,1)S(1)}, u32[]{:S(2)}) copy-start(bf16[512,128]{1,0:T(8,128)(2,1)S(1)} %collective-permute-done.11.refs_4_) | copy-start | bytes 393220
  85.2 8.0 %collective-permute-start.12 = (bf16[512,128]{1,0:T(8,128)(2,1)S(1)}, bf16[512,128]{1,0:T(8,128)(2,1)S(1)}, u32[]{:S(2)}, u32[]{:S(2)}) collective-permute-start(bf16[512,128]{1,0:T(8,128)(2,1)S(1)} %collective-permute-done.11.refs_4_), channel_id=1, source_target_pairs={{0,2},{2,0},{4,6},{6,4},{8,10},{10,8},{12,14},{14,12},{1,3},{3,1},... | collective-permute-start | bytes 393224 | tf_op jit(solution)/shard_map/ppermute | solution.py:264
  87.3 12.4 %collective-permute-start.14 = (bf16[512,128]{1,0:T(8,128)(2,1)S(1)}, bf16[512,128]{1,0:T(8,128)(2,1)S(1)}, u32[]{:S(2)}, u32[]{:S(2)}) collective-permute-start(bf16[512,128]{1,0:T(8,128)(2,1)S(1)} %collective-permute-done.13.refs_6_), channel_id=1, source_target_pairs={{0,2},{2,0},{4,6},{6,4},{8,10},{10,8},{12,14},{14,12},{1,3},{3,1},... | collective-permute-start | bytes 393224 | tf_op jit(solution)/shard_map/ppermute | solution.py:264
  87.4 7.3 %collective-permute-start.17 = (bf16[512,128]{1,0:T(8,128)(2,1)}, bf16[512,128]{1,0:T(8,128)(2,1)S(1)}, u32[]{:S(2)}, u32[]{:S(2)}) collective-permute-start(bf16[512,128]{1,0:T(8,128)(2,1)} %get-tuple-element.30.refs_8_), channel_id=1, source_target_pairs={{0,4},{2,6},{4,8},{6,10},{8,12},{10,14},{12,0},{14,2},{1,5},{3,7},... | collective-permute-start | bytes 393224 | tf_op jit(solution)/shard_map/ppermute | solution.py:264
  89.4 7.9 %collective-permute-start.19 = (bf16[512,128]{1,0:T(8,128)(2,1)}, bf16[512,128]{1,0:T(8,128)(2,1)S(1)}, u32[]{:S(2)}, u32[]{:S(2)}) collective-permute-start(bf16[512,128]{1,0:T(8,128)(2,1)} %get-tuple-element.30.refs_8_), channel_id=1, source_target_pairs={{0,8},{2,10},{4,12},{6,14},{8,0},{10,2},{12,4},{14,6},{1,9},{3,11}... | collective-permute-start | bytes 393224 | tf_op jit(solution)/shard_map/ppermute | solution.py:264
  91.7 7.5 %collective-permute-start.21 = (bf16[512,128]{1,0:T(8,128)(2,1)}, bf16[512,128]{1,0:T(8,128)(2,1)S(1)}, u32[]{:S(2)}, u32[]{:S(2)}) collective-permute-start(bf16[512,128]{1,0:T(8,128)(2,1)} %get-tuple-element.30.refs_8_), channel_id=1, source_target_pairs={{0,12},{2,14},{4,0},{6,2},{8,4},{10,6},{12,8},{14,10},{1,13},{3,15... | collective-permute-start | bytes 393224 | tf_op jit(solution)/shard_map/ppermute | solution.py:264
  93.2 11.4 %collective-permute-start.16 = (bf16[512,128]{1,0:T(8,128)(2,1)}, bf16[512,128]{1,0:T(8,128)(2,1)S(1)}, u32[]{:S(2)}, u32[]{:S(2)}) collective-permute-start(bf16[512,128]{1,0:T(8,128)(2,1)} %get-tuple-element.30.refs_8_), channel_id=1, source_target_pairs={{0,2},{2,0},{4,6},{6,4},{8,10},{10,8},{12,14},{14,12},{1,3},{3,1},... | collective-permute-start | bytes 393224 | tf_op jit(solution)/shard_map/ppermute | solution.py:264
  94.7 9.9 %collective-permute-start.18 = (bf16[512,128]{1,0:T(8,128)(2,1)S(1)}, bf16[512,128]{1,0:T(8,128)(2,1)S(1)}, u32[]{:S(2)}, u32[]{:S(2)}) collective-permute-start(bf16[512,128]{1,0:T(8,128)(2,1)S(1)} %collective-permute-done.17.refs_10_), channel_id=1, source_target_pairs={{0,2},{2,0},{4,6},{6,4},{8,10},{10,8},{12,14},{14,12},{1,3},{3,1},... | collective-permute-start | bytes 393224 | tf_op jit(solution)/shard_map/ppermute | solution.py:264
  97.3 7.3 %collective-permute-start.20 = (bf16[512,128]{1,0:T(8,128)(2,1)S(1)}, bf16[512,128]{1,0:T(8,128)(2,1)S(1)}, u32[]{:S(2)}, u32[]{:S(2)}) collective-permute-start(bf16[512,128]{1,0:T(8,128)(2,1)S(1)} %collective-permute-done.19.refs_12_), channel_id=1, source_target_pairs={{0,2},{2,0},{4,6},{6,4},{8,10},{10,8},{12,14},{14,12},{1,3},{3,1},... | collective-permute-start | bytes 393224 | tf_op jit(solution)/shard_map/ppermute | solution.py:264
  99.3 5.4 %collective-permute-start.22 = (bf16[512,128]{1,0:T(8,128)(2,1)S(1)}, bf16[512,128]{1,0:T(8,128)(2,1)S(1)}, u32[]{:S(2)}, u32[]{:S(2)}) collective-permute-start(bf16[512,128]{1,0:T(8,128)(2,1)S(1)} %collective-permute-done.21.refs_14_), channel_id=1, source_target_pairs={{0,2},{2,0},{4,6},{6,4},{8,10},{10,8},{12,14},{14,12},{1,3},{3,1},... | collective-permute-start | bytes 393224 | tf_op jit(solution)/shard_map/ppermute | solution.py:264
  99.7 9.4 %collective-permute-start.15 = (f32[72,128]{1,0:T(8,128)S(1)}, f32[72,128]{1,0:T(8,128)S(1)}, u32[]{:S(2)}, u32[]{:S(2)}) collective-permute-start(f32[72,128]{1,0:T(8,128)S(1)} %convert_reduce_fusion), channel_id=1, source_target_pairs={{0,1},{1,0},{2,3},{3,2},{4,5},{5,4},{6,7},{7,6},{8,9},{9,8},{10,11... | collective-permute-start | bytes 110600 | tf_op jit(solution)/shard_map/ppermute | solution.py:251
  (23 other events, 112.0 us)
where the time goes:
time: 111 us; the launch traced here: 110 us
  starting transfers between devices  51.1 us (46%)
  Pallas kernels  28.8 us (26%)
  local copies, waits for them, and re-layouts  13.8 us (12%)
  waiting for transfers between devices  13.2 us (12%)
  other arithmetic  1.8 us (2%)
  between operations  1.25 us (1%)
    ppermute x21, starting transfers between devices, shift(): return lax.ppermute(value, 'wide', pairs)  35.7 us
    pallas_call x8, Pallas kernels, call(): pl.pallas_call(body, in_specs=[SMEM] * len(scalars) + [VMEM] * len(arrays...  28.8 us
    all_to_all x3, starting transfers between devices, exchange(): lax.all_to_all(blocks, 'wide', split_axis=0, concat_axis=0, tiled=True)  15.3 us
    all_to_all x3, waiting for transfers between devices, exchange(): lax.all_to_all(blocks, 'wide', split_axis=0, concat_axis=0, tiled=True)  12.3 us
    unnamed x58, local copies, waits for them, and re-layouts  3.89 us
    gather x3, local copies, waits for them, and re-layouts, rows_at(): return table.at[index].get(mode='promise_in_bounds')  3.48 us
  transfers between devices with their start and end apart: 26, of which 3 were waited for; matrix products, arithmetic and copies ran while one was open for 9% of the time, Pallas kernels for 24%

commit v1 on v0

v1 whole, which is shorter than its diff:
```python
from functools import partial

import jax
import jax.numpy as jnp
from jax import lax
from jax.experimental import pallas as pl
from jax.experimental.pallas import tpu as pltpu
from jax.sharding import PartitionSpec as P


epsilon = 1e-06
F32 = jnp.float32
BF16 = jnp.bfloat16
PAD = 8
NEAR = 2


def turned(rows):
    half = rows.shape[1] // 2
    return jnp.concatenate([rows[:, half:], -rows[:, :half]], 1)


def unturned(rows):
    half = rows.shape[1] // 2
    return jnp.concatenate([-rows[:, half:], rows[:, :half]], 1)


def both_halves(norm):
    half = norm.shape[1] // 2
    once = norm[:, :half] + norm[:, half:]
    return jnp.concatenate([once, once], 1)


def parts_of(piece_real, piece_imag, left_low, right_low, level):
    rows = left_low.shape[0]
    pair = jnp.concatenate([left_low, turned(left_low)], 0)
    model = lax.dot_general(pair, right_low, (((1,), (1,)), ((), ())), preferred_element_type=F32)
    real = piece_real.astype(F32) - model[:rows]
    imag = piece_imag.astype(F32) - model[rows:]
    kept = level * lax.rsqrt(jnp.maximum(real * real + imag * imag, level * level))
    return pair, real, imag, kept


def live_mask(begin, end, first_col, count):
    column = lax.broadcasted_iota(jnp.int32, (begin.shape[0], count), 1)
    return (column >= begin - first_col) & (column < end - first_col)


def masked_error(real, imag, kept, inside):
    share = jnp.where(inside, kept, 0.0)
    return jnp.concatenate([(real * share).astype(BF16), (imag * share).astype(BF16)], 0)


def row_numbers(dest_ref, first_ref, valid_ref, width):
    first = first_ref[...]
    top = jnp.concatenate([dest_ref[...], first], 1).astype(F32)
    end = (first + valid_ref[...]).astype(F32)
    low = jnp.concatenate([end, jnp.zeros_like(end)], 1)
    return jnp.concatenate([top, low, jnp.zeros((PAD - 2, width), F32)], 0)


def standing_numbers(numbers, rows):
    columns = numbers.T.astype(jnp.int32)
    return columns[:rows, 0:1], columns[rows : 2 * rows, 0:1], columns[:rows, 1:2]


def three_ways(table):
    high = table.astype(BF16)
    rest = table - high.astype(F32)
    middle = rest.astype(BF16)
    return [high, middle, (rest - middle.astype(F32)).astype(BF16)]


def picked(dest, ways):
    row = lax.broadcasted_iota(jnp.int32, (dest.shape[0], ways[0].shape[0]), 1)
    place = jnp.where(row == dest, 1.0, 0.0).astype(BF16)
    parts = [jnp.dot(place, way, preferred_element_type=F32) for way in ways]
    return parts[0] + parts[1] + parts[2]


def prep_body(ways, rows_ref, dest_ref, first_ref, valid_ref, *refs):
    piece_ref, header_ref, numbers_ref, *part_refs = refs if ways else (None, *refs)
    count, tall, width = header_ref.shape
    rows = tall - PAD
    numbers = row_numbers(dest_ref, first_ref, valid_ref, width)
    numbers_ref[...] = numbers
    for target in range(count):
        header_ref[target, :rows] = rows_ref[...]
        header_ref[target, rows:] = numbers
    for way, part_ref in zip(ways, part_refs):
        cols = part_ref.shape[2]
        part_ref[...] = piece_ref[:, :, pl.ds(pl.multiple_of(device_at(*way) * cols, cols), cols)]


def rows_body(piece_ref, header_ref, numbers_ref, right_ref, level_ref, *refs):
    grad_ref, left_ref, own_ref, acc_ref, norm_ref = refs
    rows, width = left_ref.shape
    cols = right_ref.shape[0]
    part = own_ref.shape[0]
    block = column_block(cols)
    base = lax.axis_index("narrow") * cols
    dest, begin, end = standing_numbers(numbers_ref[...], rows)
    left = picked(dest, three_ways(header_ref[:, :rows].reshape(-1, width)))
    left_ref[...] = left
    low = left.astype(BF16)
    own_ref[...] = right_ref[pl.ds(pl.multiple_of(lax.axis_index("wide") * part, part), part), :]
    acc_ref[...] = jnp.zeros_like(acc_ref)
    norm_ref[...] = jnp.zeros_like(norm_ref)

    @pl.loop(0, cols // block)
    def _(step):
        start = step * block
        at = pl.ds(pl.multiple_of(start, block), block)
        right = right_ref[at, :]
        right_low = right.astype(BF16)
        _, real, imag, kept = parts_of(piece_ref[0, :, at], piece_ref[1, :, at], low, right_low, level_ref[:, at])
        error = masked_error(real, imag, kept, live_mask(begin, end, base + start, block))
        acc_ref[...] += jnp.dot(error, right_low, preferred_element_type=F32)
        norm_ref[...] += jnp.sum((right * right).reshape(-1, 8, width), 0)

    grad_ref[:rows] = acc_ref[:rows] + unturned(acc_ref[rows:])
    grad_ref[rows:] = jnp.broadcast_to(jnp.sum(norm_ref[...], 0, keepdims=True), (PAD, width))


def step_body(mine_ref, *refs):
    *other_refs, move_ref, out_ref = refs
    total = mine_ref[...]
    for other_ref in other_refs:
        total = total + other_ref[...]
    rows = total.shape[0] - PAD
    move = (total[:rows] / (both_halves(total[rows : rows + 1]) + epsilon)).astype(BF16)
    move_ref[...] = move
    for target in range(out_ref.shape[0]):
        out_ref[target] = move


def cols_body(ways, second, header_ref, right_ref, level_ref, *refs):
    many = len(ways) or 1
    piece_refs, refs = refs[:many], refs[many:]
    if second:
        left_ref, move_ref, change_ref, out_ref, acc_ref, part_ref = refs
        part_ref[...] = jnp.zeros_like(part_ref)
    else:
        next_ref, low_ref, left_ref, acc_ref = refs
        table = three_ways(header_ref[:, : header_ref.shape[1] - PAD].reshape(-1, header_ref.shape[2]))
    sources, tall, width = header_ref.shape
    rows = tall - PAD
    part = right_ref.shape[0]
    right = right_ref[...]
    right_low = right.astype(BF16)
    me = lax.axis_index("wide")
    base = lax.axis_index("narrow") * (sources * part) + me * part
    if level_ref.shape[1] == part:
        level = level_ref[...]
    else:
        level = level_ref[:, pl.ds(pl.multiple_of(me * part, part), part)]
    acc_ref[...] = jnp.zeros_like(acc_ref)

    def one(piece_real, piece_imag, source):
        at = pl.ds(pl.multiple_of(source * rows, rows), rows)
        numbers = header_ref[source, rows:, :]
        dest, begin, end = standing_numbers(numbers, rows)
        if second:
            left = left_ref[at, :] + move_ref[at, :].astype(F32)
        else:
            left = picked(dest, table)
            left_ref[at, :] = left
        pair, real, imag, kept = parts_of(piece_real, piece_imag, left.astype(BF16), right_low, level)
        error = masked_error(real, imag, kept, live_mask(begin, end, base, part))
        acc_ref[...] += lax.dot_general(pair, error, (((0,), (0,)), ((), ())), preferred_element_type=F32)
        if second:
            grad = jnp.dot(error, right_low, preferred_element_type=F32)
            grad = (grad[:rows] + unturned(grad[rows:])).astype(BF16)
            named = numbers[0:1, :rows].astype(jnp.int32)
            row = lax.broadcasted_iota(jnp.int32, (sources * rows, rows), 0)
            place = jnp.where(row == named, 1.0, 0.0).astype(BF16)
            part_ref[...] += jnp.dot(place, grad, preferred_element_type=F32)

    for way, piece_ref in zip(ways, piece_refs):
        one(piece_ref[0], piece_ref[1], device_at(-way[0], -way[1]))
    if not ways:

        @pl.loop(0, sources)
        def _(source):
            one(piece_refs[0][source, 0], piece_refs[0][source, 1], source)

    left = left_ref[...]
    if second:
        left = left + move_ref[...].astype(F32)
    left_norm = both_halves(jnp.sum(left * left, 0, keepdims=True))
    after = right + acc_ref[...].T / (left_norm + epsilon)
    if not second:
        next_ref[...] = after
        low_ref[...] = after.astype(BF16)
        return
    change_ref[...] = (after - right_low.astype(F32)).astype(BF16)
    norm = jnp.sum(right * right, 0, keepdims=True)
    high = norm.astype(BF16).astype(F32)
    tail = jnp.concatenate([high, norm - high, jnp.zeros((PAD - 2, width), F32)], 0).astype(BF16)
    for target in range(sources):
        out_ref[target, :rows] = part_ref[target * rows : (target + 1) * rows].astype(BF16)
        out_ref[target, rows:] = tail


def sparse_body(ways, piece_ref, numbers_ref, left_ref, move_ref, level_ref, *refs):
    right_refs, out_ref = refs[:-1], refs[-1]
    low = (left_ref[...] + move_ref[...].astype(F32)).astype(BF16)
    _, begin, end = standing_numbers(numbers_ref[...], low.shape[0])
    base = lax.axis_index("narrow") * piece_ref.shape[2]

    def one(right, source):
        cols = right.shape[0]
        start = source * cols
        at = pl.ds(pl.multiple_of(start, cols), cols)
        _, real, imag, kept = parts_of(piece_ref[0, :, at], piece_ref[1, :, at], low, right, level_ref[:, at])
        share = jnp.where(live_mask(begin, end, base + start, cols), 1.0 - kept, 0.0)
        out_ref[0, :, at] = (real * share).astype(BF16)
        out_ref[1, :, at] = (imag * share).astype(BF16)

    for way, right_ref in zip(ways, right_refs):
        one(right_ref[...], device_at(-way[0], -way[1]))
    if not ways:
        block = column_block(right_refs[0].shape[0])

        @pl.loop(0, right_refs[0].shape[0] // block)
        def _(step):
            one(right_refs[0][pl.ds(pl.multiple_of(step * block, block), block), :], step)


def join_body(ways, header_ref, move_ref, rows_ref, mine_ref, *refs):
    narrow = lax.axis_size("narrow") - 1
    other_refs, refs = refs[:narrow], refs[narrow:]
    many = len(ways) or 1
    low_refs, change_refs, (out_ref, rows_out_ref) = refs[:many], refs[many : 2 * many], refs[2 * many :]
    for way, low_ref, change_ref in zip(ways, low_refs, change_refs):
        cols = low_ref.shape[0]
        at = pl.ds(pl.multiple_of(device_at(-way[0], -way[1]) * cols, cols), cols)
        out_ref[at, :] = low_ref[...].astype(F32) + change_ref[...].astype(F32)
    if not ways:
        out_ref[...] = low_refs[0][...].astype(F32) + change_refs[0][...].astype(F32)

    total = mine_ref[...]
    for other_ref in other_refs:
        total = total + other_ref[...]
    rows = total.shape[0] - PAD
    norm = both_halves(total[rows : rows + 1] + total[rows + 1 : rows + 2])
    my_row = lax.axis_index("wide") * rows + lax.broadcasted_iota(jnp.int32, (rows, rows), 0)
    first = jnp.zeros(rows_ref.shape, F32)
    for source in range(header_ref.shape[0]):
        named = header_ref[source, rows : rows + 1, :rows].astype(jnp.int32)
        place = jnp.where(my_row == named, 1.0, 0.0).astype(BF16)
        first = first + jnp.dot(place, move_ref[source], preferred_element_type=F32)
    rows_out_ref[...] = rows_ref[...] + first + total[:rows] / (norm + epsilon)


VMEM = pl.BlockSpec(memory_space=pltpu.VMEM)


def call(body, shapes, arrays, scratch=()):
    return pl.pallas_call(
        body,
        in_specs=[VMEM] * len(arrays),
        out_specs=jax.tree.map(lambda _: VMEM, shapes),
        out_shape=shapes,
        scratch_shapes=list(scratch),
    )(*arrays)


def column_block(count):
    block = min(512, count)
    while count % block:
        block //= 2
    return block


def exchange(blocks):
    return lax.all_to_all(blocks, "wide", split_axis=0, concat_axis=0, tiled=True)


def other_narrow(value):
    count = lax.axis_size("narrow")
    return [lax.ppermute(value, "narrow", [(i, (i + k) % count) for i in range(count)]) for k in range(1, count)]


def small_wide():
    count = lax.axis_size("wide")
    return count % NEAR == 0 and count <= 4 * NEAR


def shift(value, far, near):
    outer = lax.axis_size("wide") // NEAR
    pairs = [
        (z * NEAR + x, (z + far) % outer * NEAR + (x + near) % NEAR) for z in range(outer) for x in range(NEAR)
    ]
    return lax.ppermute(value, "wide", pairs)


def device_at(far, near):
    outer = lax.axis_size("wide") // NEAR
    me = lax.axis_index("wide")
    return (me // NEAR + far) % outer * NEAR + (me % NEAR + near) % NEAR


def part_ways():
    if not small_wide():
        return ()
    outer = lax.axis_size("wide") // NEAR
    far_first = sorted(range(1, outer), key=lambda far: -min(far, outer - far))
    ways = [(far, near) for far in far_first for near in range(NEAR)]
    return (*ways, *((0, near) for near in range(1, NEAR)), (0, 0))


def gather_ways():
    if not small_wide():
        return ()
    return tuple((far, near) for far in range(lax.axis_size("wide") // NEAR) for near in range(NEAR))


def gather_parts(block):
    count = lax.axis_size("wide")
    ways = gather_ways()
    if not ways:
        return [exchange(jnp.broadcast_to(block[None], (count,) + block.shape)).reshape(-1, block.shape[1])]
    held = {(far, 0): shift(block, far, 0) for far, near in ways if far and not near}
    held |= {(0, near): shift(block, 0, near) for near in range(1, NEAR)}
    held[0, 0] = block
    return [held[way] if way in held else shift(held[way[0], 0], 0, way[1]) for way in ways]


def program(pieces, destination, first_offset, valid_length, midpoint_factor, offset_factor, threshold):
    count = lax.axis_size("wide")
    _, rows, cols = pieces.shape
    width = offset_factor.shape[1]
    part = cols // count
    total = count * rows
    level = threshold[None, :]
    own_level = level
    if part % 128:
        own_level = lax.dynamic_slice_in_dim(level, lax.axis_index("wide") * part, part, 1)

    ways = part_ways()
    shape = jax.ShapeDtypeStruct
    header, numbers, *parts = call(
        partial(prep_body, ways),
        [shape((count, rows + PAD, width), F32), shape((PAD, width), F32)]
        + [shape((2, rows, part), pieces.dtype)] * len(ways),
        [midpoint_factor, destination[None], first_offset[None], valid_length[None]] + [pieces] * bool(ways),
    )
    headers = exchange(header)
    if ways:
        blocks = [block if way == (0, 0) else shift(block, *way) for way, block in zip(ways, parts)]
    else:
        blocks = [exchange(jnp.transpose(pieces.reshape(2, rows, count, part), (2, 0, 1, 3)))]

    row_grad, left_mine, own_right = call(
        rows_body,
        [shape((rows + PAD, width), F32), shape((rows, width), F32), shape((part, width), F32)],
        [pieces, headers, numbers, offset_factor, level],
        [pltpu.VMEM((2 * rows, width), F32), pltpu.VMEM((8, width), F32)],
    )
    move_mine, moves = call(
        step_body, [shape((rows, width), BF16), shape((count, rows, width), BF16)], [row_grad] + other_narrow(row_grad)
    )
    moves = exchange(moves)

    right_one, right_low, left_all = call(
        partial(cols_body, ways, False),
        [shape((part, width), F32), shape((part, width), BF16), shape((total, width), F32)],
        [headers, own_right, own_level, *blocks],
        [pltpu.VMEM((width, part), F32)],
    )
    lows = gather_parts(right_low)

    change, outgoing = call(
        partial(cols_body, ways, True),
        [shape((part, width), BF16), shape((count, rows + PAD, width), BF16)],
        [headers, right_one, own_level, *blocks, left_all, moves.reshape(total, width)],
        [pltpu.VMEM((width, part), F32), pltpu.VMEM((total, width), F32)],
    )
    changes = gather_parts(change)
    arrived = exchange(outgoing)
    summed = jnp.sum(arrived.astype(F32), 0)

    sparse = call(
        partial(sparse_body, gather_ways()),
        shape(pieces.shape, BF16),
        [pieces, numbers, left_mine, move_mine, level, *lows],
    )
    new_offset, new_midpoint = call(
        partial(join_body, gather_ways()),
        [shape((cols, width), F32), shape((rows, width), F32)],
        [headers, moves, midpoint_factor, summed, *other_narrow(summed), *lows, *changes],
    )
    return sparse, new_midpoint, new_offset


def solution(mesh):
    placed = (
        P(None, ("groups", "wide"), "narrow"),
        P("wide"),
        P("wide"),
        P("wide"),
        P(("groups", "wide"), None),
        P(("groups", "narrow"), None),
        P(("groups", "narrow")),
    )
    return jax.shard_map(
        program,
        mesh=mesh,
        in_specs=placed,
        out_specs=(
            P(None, ("groups", "wide"), "narrow"),
            P(("groups", "wide"), None),
            P(("groups", "narrow"), None),
        ),
        check_vma=False,
    )
```

time: 111 us -> 112 us (level)
  waiting for transfers between devices: 13.2 us -> 30 us
  local copies, waits for them, and re-layouts: 13.8 us -> 4.45 us
  starting transfers between devices: 51.1 us -> 45.8 us
  other arithmetic: 1.8 us -> 0.02 us
    ppermute x21, waiting for transfers between devices: 0.94 us -> 16.3 us  [shift(): return lax.ppermute(value, 'wide', pairs)]
    ppermute x21, starting transfers between devices: 35.7 us -> 30.3 us  [shift(): return lax.ppermute(value, 'wide', pairs)]
    gather x3 -> x0, local copies, waits for them, and re-layouts: 3.48 us -> none  [rows_at(): return table.at[index].get(mode='promise_in_bounds')]
    another operation x4 -> x0, local copies, waits for them, and re-layouts: 3.18 us -> none
    dynamic_slice x1 -> x0, local copies, waits for them, and re-layouts: 1.67 us -> none  [body(): right_part = lax.dynamic_slice_in_dim(offset_factor, me * part, part, 0)]
    ppermute x2, waiting for transfers between devices: 0.01 us -> 1.42 us  [other_narrow(): lax.ppermute(value, 'narrow', [(i, (i + k) % count) for i in range(count)])]
    pallas_call x8 -> x7, Pallas kernels: 28.8 us -> 29.8 us  [call(): pl.pallas_call(body, in_specs=[VMEM] * len(arrays), out_specs=jax.tree.ma...]
    unnamed x58 -> x62, local copies, waits for them, and re-layouts: 3.89 us -> 4.45 us
  transfers between devices with their start and end apart: 26 -> 26, of which waited for: 3 -> 10; matrix products, arithmetic and copies ran while one was open for 9% -> 0% of each run, Pallas kernels for 24% -> 22%
where the time goes in v1:
time: 112 us; the launch traced here: 111 us
  starting transfers between devices  45.8 us (41%)
  waiting for transfers between devices  30 us (27%)
  Pallas kernels  29.8 us (27%)
  local copies, waits for them, and re-layouts  4.45 us (4%)
    ppermute x21, starting transfers between devices, shift(): return lax.ppermute(value, 'wide', pairs)  30.3 us
    pallas_call x7, Pallas kernels, call(): pl.pallas_call(body, in_specs=[VMEM] * len(arrays), out_specs=jax.tree.ma...  29.8 us
    ppermute x21, waiting for transfers between devices, shift(): return lax.ppermute(value, 'wide', pairs)  16.3 us
    all_to_all x3, starting transfers between devices, exchange(): lax.all_to_all(blocks, 'wide', split_axis=0, concat_axis=0, tiled=True)  15.4 us
    all_to_all x3, waiting for transfers between devices, exchange(): lax.all_to_all(blocks, 'wide', split_axis=0, concat_axis=0, tiled=True)  12.2 us
    unnamed x62, local copies, waits for them, and re-layouts  4.45 us
  transfers between devices with their start and end apart: 26, of which 10 were waited for; matrix products, arithmetic and copies ran while one was open for 0% of the time, Pallas kernels for 22%

profile of v1, /device:TPU:0, one launch (start us, length us, event | category | flops | bytes accessed | tf_op | source)
XLA Modules:
  0.0 111.0 jit_solution(14876858301496671878)
XLA Ops:
  0.6 2.4 %shard_map.94 = (f32[8,72,128]{2,1,0:T(8,128)}, f32[8,128]{1,0:T(8,128)}, bf16[2,64,512]{2,1,0:T(8,128)(2,1)}, bf16[2,64,512]{2,1,0:T(8,128)(2,1)}, bf16[2,64,51...) custom-call(f32[64,128]{1,0:T(8,128)} %rows_ref.3, ...), custom_call_target="tpu_custom_call" | custom-call | tf_op jit(solution)/shard_map/pallas_call | solution.py:260
  3.0 7.4 %all-to-all-start = ((f32[8,72,128]{2,1,0:T(8,128)}), f32[8,72,128]{2,1,0:T(8,128)S(1)}, u32[]{:S(2)}, u32[]{:S(2)}) async-start(f32[8,72,128]{2,1,0:T(8,128)} %get-tuple-element.26), calls=%async_computation | async-start | bytes 589824 | tf_op jit(solution)/shard_map/all_to_all | solution.py:277
  10.5 2.9 %collective-permute-start.1 = (bf16[2,64,512]{2,1,0:T(8,128)(2,1)}, bf16[2,64,512]{2,1,0:T(8,128)(2,1)S(1)}, u32[]{:S(2)}, u32[]{:S(2)}) collective-permute-start(bf16[2,64,512]{2,1,0:T(8,128)(2,1)} %get-tuple-element.31), channel_id=1, source_target_pairs={{0,8},{2,10},{4,12},{6,14},{8,0},{10,2},{12,4},{14,6},{1,9},{3,11}... | collective-permute-start | bytes 393224 | tf_op jit(solution)/shard_map/ppermute | solution.py:295
  13.4 1.5 %collective-permute-start.2 = (bf16[2,64,512]{2,1,0:T(8,128)(2,1)}, bf16[2,64,512]{2,1,0:T(8,128)(2,1)S(1)}, u32[]{:S(2)}, u32[]{:S(2)}) collective-permute-start(bf16[2,64,512]{2,1,0:T(8,128)(2,1)} %get-tuple-element.32), channel_id=1, source_target_pairs={{0,10},{2,8},{4,14},{6,12},{8,2},{10,0},{12,6},{14,4},{1,11},{3,9}... | collective-permute-start | bytes 393224 | tf_op jit(solution)/shard_map/ppermute | solution.py:295
  14.8 12.2 %all-to-all-done.header_ref = f32[8,72,128]{2,1,0:T(8,128)S(1)} async-done(((f32[8,72,128]{2,1,0:T(8,128)}), f32[8,72,128]{2,1,0:T(8,128)S(1)}, u32[]{:S(2)}, u32[]{:S(2)}) %all-to-all-start) | async-done | bytes 294944 | tf_op jit(solution)/shard_map/all_to_all | solution.py:277
  27.8 6.4 %shard_map.95 = (f32[72,128]{1,0:T(8,128)}, f32[64,128]{1,0:T(8,128)}, f32[512,128]{1,0:T(8,128)}) custom-call(bf16[2,64,4096]{2,1,0:T(8,128)(2,1)} %piece_ref.3, f32[8,72,128]{2,1,0:T(8,128)} %copy-done, f32[8,128]{1,0:T(8,128)} %get-tuple-element.25.numbers_ref, f32[4096,128]{1,0:T(8,128)} %right_ref.1, f32[1,4096]{1,0:T(1,128)} %bitcast.6), custom_call_target="tpu_custom_call" | custom-call | tf_op jit(solution)/shard_map/pallas_call | solution.py:260
  34.2 1.4 %collective-permute-done.refs_0_ = f32[72,128]{1,0:T(8,128)S(1)} collective-permute-done((f32[72,128]{1,0:T(8,128)}, f32[72,128]{1,0:T(8,128)S(1)}, u32[]{:S(2)}, u32[]{:S(2)}) %collective-permute-start) | collective-permute-done | bytes 36896 | tf_op jit(solution)/shard_map/ppermute | solution.py:282
  36.2 1.6 %shard_map.96 = (bf16[64,128]{1,0:T(8,128)(2,1)}, bf16[8,64,128]{2,1,0:T(8,128)(2,1)}) custom-call(f32[72,128]{1,0:T(8,128)} %get-tuple-element.28.mine_ref, f32[72,128]{1,0:T(8,128)} %copy-done.24), custom_call_target="tpu_custom_call" | custom-call | tf_op jit(solution)/shard_map/pallas_call | solution.py:260
  37.8 3.4 %all-to-all-start.1 = ((bf16[8,64,128]{2,1,0:T(8,128)(2,1)}), bf16[8,64,128]{2,1,0:T(8,128)(2,1)S(1)}, u32[]{:S(2)}, u32[]{:S(2)}) async-start(bf16[8,64,128]{2,1,0:T(8,128)(2,1)} %get-tuple-element.40), calls=%async_computation.1 | async-start | bytes 262144 | tf_op jit(solution)/shard_map/all_to_all | solution.py:277
  41.2 1.9 %collective-permute-start.3 = (bf16[2,64,512]{2,1,0:T(8,128)(2,1)S(1)}, bf16[2,64,512]{2,1,0:T(8,128)(2,1)S(1)}, u32[]{:S(2)}, u32[]{:S(2)}) collective-permute-start(bf16[2,64,512]{2,1,0:T(8,128)(2,1)S(1)} %copy-done.30), channel_id=1, source_target_pairs={{0,4},{2,6},{4,8},{6,10},{8,12},{10,14},{12,0},{14,2},{1,5},{3,7},... | collective-permute-start | bytes 393224 | tf_op jit(solution)/shard_map/ppermute | solution.py:295
  43.1 2.4 %collective-permute-start.4 = (bf16[2,64,512]{2,1,0:T(8,128)(2,1)S(1)}, bf16[2,64,512]{2,1,0:T(8,128)(2,1)S(1)}, u32[]{:S(2)}, u32[]{:S(2)}) collective-permute-start(bf16[2,64,512]{2,1,0:T(8,128)(2,1)S(1)} %copy-done.29), channel_id=1, source_target_pairs={{0,6},{2,4},{4,10},{6,8},{8,14},{10,12},{12,2},{14,0},{1,7},{3,5},... | collective-permute-start | bytes 393224 | tf_op jit(solution)/shard_map/ppermute | solution.py:295
  45.5 2.3 %collective-permute-start.5 = (bf16[2,64,512]{2,1,0:T(8,128)(2,1)S(1)}, bf16[2,64,512]{2,1,0:T(8,128)(2,1)S(1)}, u32[]{:S(2)}, u32[]{:S(2)}) collective-permute-start(bf16[2,64,512]{2,1,0:T(8,128)(2,1)S(1)} %copy-done.28), channel_id=1, source_target_pairs={{0,12},{2,14},{4,0},{6,2},{8,4},{10,6},{12,8},{14,10},{1,13},{3,15... | collective-permute-start | bytes 393224 | tf_op jit(solution)/shard_map/ppermute | solution.py:295
  48.1 1.9 %collective-permute-start.7 = (bf16[2,64,512]{2,1,0:T(8,128)(2,1)S(1)}, bf16[2,64,512]{2,1,0:T(8,128)(2,1)S(1)}, u32[]{:S(2)}, u32[]{:S(2)}) collective-permute-start(bf16[2,64,512]{2,1,0:T(8,128)(2,1)S(1)} %copy-done.26), channel_id=1, source_target_pairs={{0,2},{2,0},{4,6},{6,4},{8,10},{10,8},{12,14},{14,12},{1,3},{3,1},... | collective-permute-start | bytes 393224 | tf_op jit(solution)/shard_map/ppermute | solution.py:295
  50.0 1.6 %collective-permute-done.3.refs_2_ = bf16[2,64,512]{2,1,0:T(8,128)(2,1)S(1)} collective-permute-done((bf16[2,64,512]{2,1,0:T(8,128)(2,1)S(1)}, bf16[2,64,512]{2,1,0:T(8,128)(2,1)S(1)}, u32[]{:S(2)}, u32[]{:S(2)}) %collective-permute-start.3) | collective-permute-done | bytes 131104 | tf_op jit(solution)/shard_map/ppermute | solution.py:295
  51.6 3.7 %collective-permute-done.4.refs_3_ = bf16[2,64,512]{2,1,0:T(8,128)(2,1)S(1)} collective-permute-done((bf16[2,64,512]{2,1,0:T(8,128)(2,1)S(1)}, bf16[2,64,512]{2,1,0:T(8,128)(2,1)S(1)}, u32[]{:S(2)}, u32[]{:S(2)}) %collective-permute-start.4) | collective-permute-done | bytes 131104 | tf_op jit(solution)/shard_map/ppermute | solution.py:295
  56.4 2.9 %collective-permute-done.6.refs_5_ = bf16[2,64,512]{2,1,0:T(8,128)(2,1)S(1)} collective-permute-done((bf16[2,64,512]{2,1,0:T(8,128)(2,1)S(1)}, bf16[2,64,512]{2,1,0:T(8,128)(2,1)S(1)}, u32[]{:S(2)}, u32[]{:S(2)}) %collective-permute-start.6) | collective-permute-done | bytes 131104 | tf_op jit(solution)/shard_map/ppermute | solution.py:295
  60.1 6.5 %shard_map.97 = (f32[512,128]{1,0:T(8,128)}, bf16[512,128]{1,0:T(8,128)(2,1)}, f32[512,128]{1,0:T(8,128)}) custom-call(f32[8,72,128]{2,1,0:T(8,128)} %copy-done, f32[512,128]{1,0:T(8,128)} %get-tuple-element.30.right_ref, f32[1,4096]{1,0:T(1,128)} %bitcast.7, bf16[2,64,512]{2,1,0:T(8,128)(2,1)} %copy-done.9, bf16[2,64,512]{2,1,0:T(8,128)(2,1)} %copy-done.10, ...), custom_call_target="tpu_custom_call" | custom-call | tf_op jit(solution)/shard_map/pallas_call | solution.py:260
  66.6 1.4 %collective-permute-start.13 = (bf16[512,128]{1,0:T(8,128)(2,1)}, bf16[512,128]{1,0:T(8,128)(2,1)S(1)}, u32[]{:S(2)}, u32[]{:S(2)}) collective-permute-start(bf16[512,128]{1,0:T(8,128)(2,1)} %get-tuple-element.39.refs_0_.refs_1_), channel_id=1, source_target_pairs={{0,12},{2,14},{4,0},{6,2},{8,4},{10,6},{12,8},{14,10},{1,13},{3,15... | collective-permute-start | bytes 393224 | tf_op jit(solution)/shard_map/ppermute | solution.py:295
  68.0 1.3 %collective-permute-start.11 = (bf16[512,128]{1,0:T(8,128)(2,1)}, bf16[512,128]{1,0:T(8,128)(2,1)S(1)}, u32[]{:S(2)}, u32[]{:S(2)}) collective-permute-start(bf16[512,128]{1,0:T(8,128)(2,1)} %get-tuple-element.39.refs_0_.refs_1_), channel_id=1, source_target_pairs={{0,8},{2,10},{4,12},{6,14},{8,0},{10,2},{12,4},{14,6},{1,9},{3,11}... | collective-permute-start | bytes 393224 | tf_op jit(solution)/shard_map/ppermute | solution.py:295
  69.3 1.3 %collective-permute-start.9 = (bf16[512,128]{1,0:T(8,128)(2,1)}, bf16[512,128]{1,0:T(8,128)(2,1)S(1)}, u32[]{:S(2)}, u32[]{:S(2)}) collective-permute-start(bf16[512,128]{1,0:T(8,128)(2,1)} %get-tuple-element.39.refs_0_.refs_1_), channel_id=1, source_target_pairs={{0,4},{2,6},{4,8},{6,10},{8,12},{10,14},{12,0},{14,2},{1,5},{3,7},... | collective-permute-start | bytes 393224 | tf_op jit(solution)/shard_map/ppermute | solution.py:295
  71.9 5.9 %shard_map.99 = (bf16[512,128]{1,0:T(8,128)(2,1)}, bf16[8,72,128]{2,1,0:T(8,128)(2,1)}) custom-call(f32[8,72,128]{2,1,0:T(8,128)} %copy-done, f32[512,128]{1,0:T(8,128)} %get-tuple-element.41.right_ref, f32[1,4096]{1,0:T(1,128)} %bitcast.8, bf16[2,64,512]{2,1,0:T(8,128)(2,1)} %copy-done.9, bf16[2,64,512]{2,1,0:T(8,128)(2,1)} %copy-done.10, ...), custom_call_target="tpu_custom_call" | custom-call | tf_op jit(solution)/shard_map/pallas_call | solution.py:260
  77.8 4.6 %all-to-all-start.2 = ((bf16[8,72,128]{2,1,0:T(8,128)(2,1)}), bf16[8,72,128]{2,1,0:T(8,128)(2,1)S(1)}, u32[]{:S(2)}, u32[]{:S(2)}) async-start(bf16[8,72,128]{2,1,0:T(8,128)(2,1)} %get-tuple-element.43), calls=%async_computation.2 | async-start | bytes 294912 | tf_op jit(solution)/shard_map/all_to_all | solution.py:277
  82.4 2.1 %collective-permute-start.14 = (bf16[512,128]{1,0:T(8,128)(2,1)S(1)}, bf16[512,128]{1,0:T(8,128)(2,1)S(1)}, u32[]{:S(2)}, u32[]{:S(2)}) collective-permute-start(bf16[512,128]{1,0:T(8,128)(2,1)S(1)} %collective-permute-done.13.refs_6_.refs_7_), channel_id=1, source_target_pairs={{0,2},{2,0},{4,6},{6,4},{8,10},{10,8},{12,14},{14,12},{1,3},{3,1},... | collective-permute-start | bytes 393224 | tf_op jit(solution)/shard_map/ppermute | solution.py:295
  84.6 3.7 %collective-permute-start.21 = (bf16[512,128]{1,0:T(8,128)(2,1)}, bf16[512,128]{1,0:T(8,128)(2,1)S(1)}, u32[]{:S(2)}, u32[]{:S(2)}) collective-permute-start(bf16[512,128]{1,0:T(8,128)(2,1)} %get-tuple-element.44.refs_9_), channel_id=1, source_target_pairs={{0,12},{2,14},{4,0},{6,2},{8,4},{10,6},{12,8},{14,10},{1,13},{3,15... | collective-permute-start | bytes 393224 | tf_op jit(solution)/shard_map/ppermute | solution.py:295
  88.4 1.1 collective-permute-start.17
  89.8 1.5 %collective-permute-start.10 = (bf16[512,128]{1,0:T(8,128)(2,1)S(1)}, bf16[512,128]{1,0:T(8,128)(2,1)S(1)}, u32[]{:S(2)}, u32[]{:S(2)}) collective-permute-start(bf16[512,128]{1,0:T(8,128)(2,1)S(1)} %collective-permute-done.9.refs_2_.refs_3_), channel_id=1, source_target_pairs={{0,2},{2,0},{4,6},{6,4},{8,10},{10,8},{12,14},{14,12},{1,3},{3,1},... | collective-permute-start | bytes 393224 | tf_op jit(solution)/shard_map/ppermute | solution.py:295
  91.3 1.5 %collective-permute-done.12.refs_5_.refs_6_ = bf16[512,128]{1,0:T(8,128)(2,1)S(1)} collective-permute-done((bf16[512,128]{1,0:T(8,128)(2,1)S(1)}, bf16[512,128]{1,0:T(8,128)(2,1)S(1)}, u32[]{:S(2)}, u32[]{:S(2)}) %collective-permute-start.12) | collective-permute-done | bytes 131104 | tf_op jit(solution)/shard_map/ppermute | solution.py:295
  92.8 1.2 %collective-permute-start.16 = (bf16[512,128]{1,0:T(8,128)(2,1)}, bf16[512,128]{1,0:T(8,128)(2,1)S(1)}, u32[]{:S(2)}, u32[]{:S(2)}) collective-permute-start(bf16[512,128]{1,0:T(8,128)(2,1)} %get-tuple-element.44.refs_9_), channel_id=1, source_target_pairs={{0,2},{2,0},{4,6},{6,4},{8,10},{10,8},{12,14},{14,12},{1,3},{3,1},... | collective-permute-start | bytes 393224 | tf_op jit(solution)/shard_map/ppermute | solution.py:295
  94.9 4.9 %collective-permute-done.19.refs_13_ = bf16[512,128]{1,0:T(8,128)(2,1)S(1)} collective-permute-done((bf16[512,128]{1,0:T(8,128)(2,1)}, bf16[512,128]{1,0:T(8,128)(2,1)S(1)}, u32[]{:S(2)}, u32[]{:S(2)}) %collective-permute-start.19) | collective-permute-done | bytes 131104 | tf_op jit(solution)/shard_map/ppermute | solution.py:295
  99.8 1.5 %collective-permute-start.20 = (bf16[512,128]{1,0:T(8,128)(2,1)S(1)}, bf16[512,128]{1,0:T(8,128)(2,1)S(1)}, u32[]{:S(2)}, u32[]{:S(2)}) collective-permute-start(bf16[512,128]{1,0:T(8,128)(2,1)S(1)} %collective-permute-done.19.refs_13_), channel_id=1, source_target_pairs={{0,2},{2,0},{4,6},{6,4},{8,10},{10,8},{12,14},{14,12},{1,3},{3,1},... | collective-permute-start | bytes 393224 | tf_op jit(solution)/shard_map/ppermute | solution.py:295
  102.5 3.6 %shard_map.98 = bf16[2,64,4096]{2,1,0:T(8,128)(2,1)} custom-call(bf16[2,64,4096]{2,1,0:T(8,128)(2,1)} %piece_ref.3, f32[8,128]{1,0:T(8,128)} %get-tuple-element.25.numbers_ref, f32[64,128]{1,0:T(8,128)} %get-tuple-element.27.left_ref, bf16[64,128]{1,0:T(8,128)(2,1)} %get-tuple-element.29.move_ref, f32[1,4096]{1,0:T(1,128)} %bitcast.9, ...), custom_call_target="tpu_custom_call" | custom-call | tf_op jit(solution)/shard_map/pallas_call | solution.py:260
  107.6 3.4 %shard_map.100 = (f32[4096,128]{1,0:T(8,128)}, f32[64,128]{1,0:T(8,128)}) custom-call(f32[8,72,128]{2,1,0:T(8,128)} %copy-done, bf16[8,64,128]{2,1,0:T(8,128)(2,1)} %copy-done.1, f32[64,128]{1,0:T(8,128)} %rows_ref.3, f32[72,128]{1,0:T(8,128)} %copy-done.16, f32[72,128]{1,0:T(8,128)} %copy-done.25, bf16[512,128]{1,0:T(8,128)(2,1)} %get-tuple-element.39.refs_0_.refs_1_, ...), custom_call_target="tpu_custom_call" | custom-call | tf_op jit(solution)/shard_map/pallas_call | solution.py:260
  (90 shorter events, 8.5 us)
Async XLA Ops:
  3.0 38.2 %copy-start.30 = (bf16[2,64,512]{2,1,0:T(8,128)(2,1)S(1)}, bf16[2,64,512]{2,1,0:T(8,128)(2,1)}, u32[]{:S(2)}) copy-start(bf16[2,64,512]{2,1,0:T(8,128)(2,1)} %get-tuple-element.33) | copy-start | bytes 393220
  3.0 40.1 %copy-start.29 = (bf16[2,64,512]{2,1,0:T(8,128)(2,1)S(1)}, bf16[2,64,512]{2,1,0:T(8,128)(2,1)}, u32[]{:S(2)}) copy-start(bf16[2,64,512]{2,1,0:T(8,128)(2,1)} %get-tuple-element.34) | copy-start | bytes 393220
  3.0 42.5 %copy-start.28 = (bf16[2,64,512]{2,1,0:T(8,128)(2,1)S(1)}, bf16[2,64,512]{2,1,0:T(8,128)(2,1)}, u32[]{:S(2)}) copy-start(bf16[2,64,512]{2,1,0:T(8,128)(2,1)} %get-tuple-element.35) | copy-start | bytes 393220
  3.0 44.9 %copy-start.27 = (bf16[2,64,512]{2,1,0:T(8,128)(2,1)S(1)}, bf16[2,64,512]{2,1,0:T(8,128)(2,1)}, u32[]{:S(2)}) copy-start(bf16[2,64,512]{2,1,0:T(8,128)(2,1)} %get-tuple-element.36) | copy-start | bytes 393220
  3.0 45.1 %copy-start.26 = (bf16[2,64,512]{2,1,0:T(8,128)(2,1)S(1)}, bf16[2,64,512]{2,1,0:T(8,128)(2,1)}, u32[]{:S(2)}) copy-start(bf16[2,64,512]{2,1,0:T(8,128)(2,1)} %get-tuple-element.37) | copy-start | bytes 393220
  3.0 24.0 %all-to-all-start = ((f32[8,72,128]{2,1,0:T(8,128)}), f32[8,72,128]{2,1,0:T(8,128)S(1)}, u32[]{:S(2)}, u32[]{:S(2)}) async-start(f32[8,72,128]{2,1,0:T(8,128)} %get-tuple-element.26), calls=%async_computation | async-start | bytes 589824 | tf_op jit(solution)/shard_map/all_to_all | solution.py:277
  10.5 37.4 %collective-permute-start.1 = (bf16[2,64,512]{2,1,0:T(8,128)(2,1)}, bf16[2,64,512]{2,1,0:T(8,128)(2,1)S(1)}, u32[]{:S(2)}, u32[]{:S(2)}) collective-permute-start(bf16[2,64,512]{2,1,0:T(8,128)(2,1)} %get-tuple-element.31), channel_id=1, source_target_pairs={{0,8},{2,10},{4,12},{6,14},{8,0},{10,2},{12,4},{14,6},{1,9},{3,11}... | collective-permute-start | bytes 393224 | tf_op jit(solution)/shard_map/ppermute | solution.py:295
  13.4 34.7 %collective-permute-start.2 = (bf16[2,64,512]{2,1,0:T(8,128)(2,1)}, bf16[2,64,512]{2,1,0:T(8,128)(2,1)S(1)}, u32[]{:S(2)}, u32[]{:S(2)}) collective-permute-start(bf16[2,64,512]{2,1,0:T(8,128)(2,1)} %get-tuple-element.32), channel_id=1, source_target_pairs={{0,10},{2,8},{4,14},{6,12},{8,2},{10,0},{12,6},{14,4},{1,11},{3,9}... | collective-permute-start | bytes 393224 | tf_op jit(solution)/shard_map/ppermute | solution.py:295
  34.2 1.4 %collective-permute-start = (f32[72,128]{1,0:T(8,128)}, f32[72,128]{1,0:T(8,128)S(1)}, u32[]{:S(2)}, u32[]{:S(2)}) collective-permute-start(f32[72,128]{1,0:T(8,128)} %get-tuple-element.28.mine_ref), channel_id=1, source_target_pairs={{0,1},{1,0},{2,3},{3,2},{4,5},{5,4},{6,7},{7,6},{8,9},{9,8},{10,11... | collective-permute-start | bytes 110600 | tf_op jit(solution)/shard_map/ppermute | solution.py:282
  37.8 33.4 %all-to-all-start.1 = ((bf16[8,64,128]{2,1,0:T(8,128)(2,1)}), bf16[8,64,128]{2,1,0:T(8,128)(2,1)S(1)}, u32[]{:S(2)}, u32[]{:S(2)}) async-start(bf16[8,64,128]{2,1,0:T(8,128)(2,1)} %get-tuple-element.40), calls=%async_computation.1 | async-start | bytes 262144 | tf_op jit(solution)/shard_map/all_to_all | solution.py:277
  41.2 10.4 %collective-permute-start.3 = (bf16[2,64,512]{2,1,0:T(8,128)(2,1)S(1)}, bf16[2,64,512]{2,1,0:T(8,128)(2,1)S(1)}, u32[]{:S(2)}, u32[]{:S(2)}) collective-permute-start(bf16[2,64,512]{2,1,0:T(8,128)(2,1)S(1)} %copy-done.30), channel_id=1, source_target_pairs={{0,4},{2,6},{4,8},{6,10},{8,12},{10,14},{12,0},{14,2},{1,5},{3,7},... | collective-permute-start | bytes 393224 | tf_op jit(solution)/shard_map/ppermute | solution.py:295
  43.1 12.2 %collective-permute-start.4 = (bf16[2,64,512]{2,1,0:T(8,128)(2,1)S(1)}, bf16[2,64,512]{2,1,0:T(8,128)(2,1)S(1)}, u32[]{:S(2)}, u32[]{:S(2)}) collective-permute-start(bf16[2,64,512]{2,1,0:T(8,128)(2,1)S(1)} %copy-done.29), channel_id=1, source_target_pairs={{0,6},{2,4},{4,10},{6,8},{8,14},{10,12},{12,2},{14,0},{1,7},{3,5},... | collective-permute-start | bytes 393224 | tf_op jit(solution)/shard_map/ppermute | solution.py:295
  45.5 10.9 %collective-permute-start.5 = (bf16[2,64,512]{2,1,0:T(8,128)(2,1)S(1)}, bf16[2,64,512]{2,1,0:T(8,128)(2,1)S(1)}, u32[]{:S(2)}, u32[]{:S(2)}) collective-permute-start(bf16[2,64,512]{2,1,0:T(8,128)(2,1)S(1)} %copy-done.28), channel_id=1, source_target_pairs={{0,12},{2,14},{4,0},{6,2},{8,4},{10,6},{12,8},{14,10},{1,13},{3,15... | collective-permute-start | bytes 393224 | tf_op jit(solution)/shard_map/ppermute | solution.py:295
  47.9 11.5 %collective-permute-start.6 = (bf16[2,64,512]{2,1,0:T(8,128)(2,1)S(1)}, bf16[2,64,512]{2,1,0:T(8,128)(2,1)S(1)}, u32[]{:S(2)}, u32[]{:S(2)}) collective-permute-start(bf16[2,64,512]{2,1,0:T(8,128)(2,1)S(1)} %copy-done.27), channel_id=1, source_target_pairs={{0,14},{2,12},{4,2},{6,0},{8,6},{10,4},{12,10},{14,8},{1,15},{3,13... | collective-permute-start | bytes 393224 | tf_op jit(solution)/shard_map/ppermute | solution.py:295
  48.1 11.3 %collective-permute-start.7 = (bf16[2,64,512]{2,1,0:T(8,128)(2,1)S(1)}, bf16[2,64,512]{2,1,0:T(8,128)(2,1)S(1)}, u32[]{:S(2)}, u32[]{:S(2)}) collective-permute-start(bf16[2,64,512]{2,1,0:T(8,128)(2,1)S(1)} %copy-done.26), channel_id=1, source_target_pairs={{0,2},{2,0},{4,6},{6,4},{8,10},{10,8},{12,14},{14,12},{1,3},{3,1},... | collective-permute-start | bytes 393224 | tf_op jit(solution)/shard_map/ppermute | solution.py:295
  66.6 15.8 %collective-permute-start.13 = (bf16[512,128]{1,0:T(8,128)(2,1)}, bf16[512,128]{1,0:T(8,128)(2,1)S(1)}, u32[]{:S(2)}, u32[]{:S(2)}) collective-permute-start(bf16[512,128]{1,0:T(8,128)(2,1)} %get-tuple-element.39.refs_0_.refs_1_), channel_id=1, source_target_pairs={{0,12},{2,14},{4,0},{6,2},{8,4},{10,6},{12,8},{14,10},{1,13},{3,15... | collective-permute-start | bytes 393224 | tf_op jit(solution)/shard_map/ppermute | solution.py:295
  68.0 16.5 %collective-permute-start.11 = (bf16[512,128]{1,0:T(8,128)(2,1)}, bf16[512,128]{1,0:T(8,128)(2,1)S(1)}, u32[]{:S(2)}, u32[]{:S(2)}) collective-permute-start(bf16[512,128]{1,0:T(8,128)(2,1)} %get-tuple-element.39.refs_0_.refs_1_), channel_id=1, source_target_pairs={{0,8},{2,10},{4,12},{6,14},{8,0},{10,2},{12,4},{14,6},{1,9},{3,11}... | collective-permute-start | bytes 393224 | tf_op jit(solution)/shard_map/ppermute | solution.py:295
  69.3 19.1 %collective-permute-start.9 = (bf16[512,128]{1,0:T(8,128)(2,1)}, bf16[512,128]{1,0:T(8,128)(2,1)S(1)}, u32[]{:S(2)}, u32[]{:S(2)}) collective-permute-start(bf16[512,128]{1,0:T(8,128)(2,1)} %get-tuple-element.39.refs_0_.refs_1_), channel_id=1, source_target_pairs={{0,4},{2,6},{4,8},{6,10},{8,12},{10,14},{12,0},{14,2},{1,5},{3,7},... | collective-permute-start | bytes 393224 | tf_op jit(solution)/shard_map/ppermute | solution.py:295
  70.6 17.8 %collective-permute-start.8 = (bf16[512,128]{1,0:T(8,128)(2,1)}, bf16[512,128]{1,0:T(8,128)(2,1)S(1)}, u32[]{:S(2)}, u32[]{:S(2)}) collective-permute-start(bf16[512,128]{1,0:T(8,128)(2,1)} %get-tuple-element.39.refs_0_.refs_1_), channel_id=1, source_target_pairs={{0,2},{2,0},{4,6},{6,4},{8,10},{10,8},{12,14},{14,12},{1,3},{3,1},... | collective-permute-start | bytes 393224 | tf_op jit(solution)/shard_map/ppermute | solution.py:295
  77.8 24.0 %all-to-all-start.2 = ((bf16[8,72,128]{2,1,0:T(8,128)(2,1)}), bf16[8,72,128]{2,1,0:T(8,128)(2,1)S(1)}, u32[]{:S(2)}, u32[]{:S(2)}) async-start(bf16[8,72,128]{2,1,0:T(8,128)(2,1)} %get-tuple-element.43), calls=%async_computation.2 | async-start | bytes 294912 | tf_op jit(solution)/shard_map/all_to_all | solution.py:277
  82.4 19.5 %copy-start.2 = (bf16[512,128]{1,0:T(8,128)(2,1)}, bf16[512,128]{1,0:T(8,128)(2,1)S(1)}, u32[]{:S(2)}) copy-start(bf16[512,128]{1,0:T(8,128)(2,1)S(1)} %collective-permute-done.13.refs_6_.refs_7_) | copy-start | bytes 393220
  82.4 7.4 %collective-permute-start.14 = (bf16[512,128]{1,0:T(8,128)(2,1)S(1)}, bf16[512,128]{1,0:T(8,128)(2,1)S(1)}, u32[]{:S(2)}, u32[]{:S(2)}) collective-permute-start(bf16[512,128]{1,0:T(8,128)(2,1)S(1)} %collective-permute-done.13.refs_6_.refs_7_), channel_id=1, source_target_pairs={{0,2},{2,0},{4,6},{6,4},{8,10},{10,8},{12,14},{14,12},{1,3},{3,1},... | collective-permute-start | bytes 393224 | tf_op jit(solution)/shard_map/ppermute | solution.py:295
  84.5 8.3 %collective-permute-start.12 = (bf16[512,128]{1,0:T(8,128)(2,1)S(1)}, bf16[512,128]{1,0:T(8,128)(2,1)S(1)}, u32[]{:S(2)}, u32[]{:S(2)}) collective-permute-start(bf16[512,128]{1,0:T(8,128)(2,1)S(1)} %collective-permute-done.11.refs_4_.refs_5_), channel_id=1, source_target_pairs={{0,2},{2,0},{4,6},{6,4},{8,10},{10,8},{12,14},{14,12},{1,3},{3,1},... | collective-permute-start | bytes 393224 | tf_op jit(solution)/shard_map/ppermute | solution.py:295
  84.6 9.4 %collective-permute-start.21 = (bf16[512,128]{1,0:T(8,128)(2,1)}, bf16[512,128]{1,0:T(8,128)(2,1)S(1)}, u32[]{:S(2)}, u32[]{:S(2)}) collective-permute-start(bf16[512,128]{1,0:T(8,128)(2,1)} %get-tuple-element.44.refs_9_), channel_id=1, source_target_pairs={{0,12},{2,14},{4,0},{6,2},{8,4},{10,6},{12,8},{14,10},{1,13},{3,15... | collective-permute-start | bytes 393224 | tf_op jit(solution)/shard_map/ppermute | solution.py:295
  88.4 11.4 %collective-permute-start.19 = (bf16[512,128]{1,0:T(8,128)(2,1)}, bf16[512,128]{1,0:T(8,128)(2,1)S(1)}, u32[]{:S(2)}, u32[]{:S(2)}) collective-permute-start(bf16[512,128]{1,0:T(8,128)(2,1)} %get-tuple-element.44.refs_9_), channel_id=1, source_target_pairs={{0,8},{2,10},{4,12},{6,14},{8,0},{10,2},{12,4},{14,6},{1,9},{3,11}... | collective-permute-start | bytes 393224 | tf_op jit(solution)/shard_map/ppermute | solution.py:295
  88.4 12.9 %collective-permute-start.17 = (bf16[512,128]{1,0:T(8,128)(2,1)}, bf16[512,128]{1,0:T(8,128)(2,1)S(1)}, u32[]{:S(2)}, u32[]{:S(2)}) collective-permute-start(bf16[512,128]{1,0:T(8,128)(2,1)} %get-tuple-element.44.refs_9_), channel_id=1, source_target_pairs={{0,4},{2,6},{4,8},{6,10},{8,12},{10,14},{12,0},{14,2},{1,5},{3,7},... | collective-permute-start | bytes 393224 | tf_op jit(solution)/shard_map/ppermute | solution.py:295
  89.8 12.0 %collective-permute-start.10 = (bf16[512,128]{1,0:T(8,128)(2,1)S(1)}, bf16[512,128]{1,0:T(8,128)(2,1)S(1)}, u32[]{:S(2)}, u32[]{:S(2)}) collective-permute-start(bf16[512,128]{1,0:T(8,128)(2,1)S(1)} %collective-permute-done.9.refs_2_.refs_3_), channel_id=1, source_target_pairs={{0,2},{2,0},{4,6},{6,4},{8,10},{10,8},{12,14},{14,12},{1,3},{3,1},... | collective-permute-start | bytes 393224 | tf_op jit(solution)/shard_map/ppermute | solution.py:295
  92.8 13.3 %collective-permute-start.16 = (bf16[512,128]{1,0:T(8,128)(2,1)}, bf16[512,128]{1,0:T(8,128)(2,1)S(1)}, u32[]{:S(2)}, u32[]{:S(2)}) collective-permute-start(bf16[512,128]{1,0:T(8,128)(2,1)} %get-tuple-element.44.refs_9_), channel_id=1, source_target_pairs={{0,2},{2,0},{4,6},{6,4},{8,10},{10,8},{12,14},{14,12},{1,3},{3,1},... | collective-permute-start | bytes 393224 | tf_op jit(solution)/shard_map/ppermute | solution.py:295
  94.1 12.1 %collective-permute-start.22 = (bf16[512,128]{1,0:T(8,128)(2,1)S(1)}, bf16[512,128]{1,0:T(8,128)(2,1)S(1)}, u32[]{:S(2)}, u32[]{:S(2)}) collective-permute-start(bf16[512,128]{1,0:T(8,128)(2,1)S(1)} %collective-permute-done.21.refs_15_), channel_id=1, source_target_pairs={{0,2},{2,0},{4,6},{6,4},{8,10},{10,8},{12,14},{14,12},{1,3},{3,1},... | collective-permute-start | bytes 393224 | tf_op jit(solution)/shard_map/ppermute | solution.py:295
  99.8 6.4 %collective-permute-start.20 = (bf16[512,128]{1,0:T(8,128)(2,1)S(1)}, bf16[512,128]{1,0:T(8,128)(2,1)S(1)}, u32[]{:S(2)}, u32[]{:S(2)}) collective-permute-start(bf16[512,128]{1,0:T(8,128)(2,1)S(1)} %collective-permute-done.19.refs_13_), channel_id=1, source_target_pairs={{0,2},{2,0},{4,6},{6,4},{8,10},{10,8},{12,14},{14,12},{1,3},{3,1},... | collective-permute-start | bytes 393224 | tf_op jit(solution)/shard_map/ppermute | solution.py:295
  101.3 5.1 %collective-permute-start.18 = (bf16[512,128]{1,0:T(8,128)(2,1)S(1)}, bf16[512,128]{1,0:T(8,128)(2,1)S(1)}, u32[]{:S(2)}, u32[]{:S(2)}) collective-permute-start(bf16[512,128]{1,0:T(8,128)(2,1)S(1)} %collective-permute-done.17.refs_11_), channel_id=1, source_target_pairs={{0,2},{2,0},{4,6},{6,4},{8,10},{10,8},{12,14},{14,12},{1,3},{3,1},... | collective-permute-start | bytes 393224 | tf_op jit(solution)/shard_map/ppermute | solution.py:295
  101.9 4.4 %collective-permute-start.15 = (f32[72,128]{1,0:T(8,128)S(1)}, f32[72,128]{1,0:T(8,128)S(1)}, u32[]{:S(2)}, u32[]{:S(2)}) collective-permute-start(f32[72,128]{1,0:T(8,128)S(1)} %convert_reduce_fusion.mine_ref), channel_id=1, source_target_pairs={{0,1},{1,0},{2,3},{3,2},{4,5},{5,4},{6,7},{7,6},{8,9},{9,8},{10,11... | collective-permute-start | bytes 110600 | tf_op jit(solution)/shard_map/ppermute | solution.py:282
  (25 other events, 139.4 us)

commit v2 on v1

v2 whole, which is shorter than its diff:
```python
from functools import partial

import jax
import jax.numpy as jnp
from jax import lax
from jax.experimental import pallas as pl
from jax.experimental.pallas import tpu as pltpu
from jax.sharding import PartitionSpec as P


epsilon = 1e-06
F32 = jnp.float32
BF16 = jnp.bfloat16
PAD = 8
NEAR = 2


def turned(rows):
    half = rows.shape[1] // 2
    return jnp.concatenate([rows[:, half:], -rows[:, :half]], 1)


def unturned(rows):
    half = rows.shape[1] // 2
    return jnp.concatenate([-rows[:, half:], rows[:, :half]], 1)


def both_halves(norm):
    half = norm.shape[1] // 2
    once = norm[:, :half] + norm[:, half:]
    return jnp.concatenate([once, once], 1)


def pair_of(left_low):
    return jnp.concatenate([left_low, turned(left_low)], 0)


def model_of(pair, right_low):
    return lax.dot_general(pair, right_low, (((1,), (1,)), ((), ())), preferred_element_type=F32)


def residual_of(piece_real, piece_imag, model, level):
    rows = model.shape[0] // 2
    real = piece_real.astype(F32) - model[:rows]
    imag = piece_imag.astype(F32) - model[rows:]
    kept = level * lax.rsqrt(jnp.maximum(real * real + imag * imag, level * level))
    return real, imag, kept


def live_mask(begin, end, first_col, count):
    column = lax.broadcasted_iota(jnp.int32, (begin.shape[0], count), 1)
    return (column >= begin - first_col) & (column < end - first_col)


def masked_error(real, imag, kept, inside):
    share = jnp.where(inside, kept, 0.0)
    return jnp.concatenate([(real * share).astype(BF16), (imag * share).astype(BF16)], 0)


BASE = 128


def row_numbers(dest_ref, first_ref, valid_ref, rows_ref):
    first = first_ref[...]
    end = first + valid_ref[...]
    both = jnp.concatenate(
        [jnp.concatenate([dest_ref[...], first], 1), jnp.concatenate([end, jnp.zeros_like(end)], 1)], 0
    )
    high = both >> (BASE.bit_length() - 1)
    table = rows_ref[...]
    norm = [way.astype(F32) for way in three_ways(jnp.sum(table * table, 0, keepdims=True))]
    low = (both & (BASE - 1)).astype(F32)
    return jnp.concatenate([high.astype(F32), low, *norm, jnp.zeros((PAD - 7, table.shape[1]), F32)], 0).astype(BF16)


def read_numbers(numbers):
    value = numbers.astype(F32)
    return value[0:2] * BASE + value[2:4]


def standing_numbers(numbers, rows):
    value = read_numbers(numbers)
    value = jnp.concatenate([value, jnp.zeros((6, value.shape[1]), F32)], 0)
    columns = value.T.astype(jnp.int32)
    return columns[:rows, 0:1], columns[rows : 2 * rows, 0:1], columns[:rows, 1:2]


def three_ways(table):
    high = table.astype(BF16)
    rest = table - high.astype(F32)
    middle = rest.astype(BF16)
    return [high, middle, (rest - middle.astype(F32)).astype(BF16)]


def picked(dest, table):
    row = lax.broadcasted_iota(jnp.int32, (dest.shape[0], table.shape[0]), 1)
    place = jnp.where(row == dest, 1.0, 0.0).astype(BF16)
    return jnp.dot(place, table, preferred_element_type=F32).astype(BF16)


def prep_body(ways, rows_ref, dest_ref, first_ref, valid_ref, *refs):
    piece_ref, header_ref, numbers_ref, *part_refs = refs if ways else (None, *refs)
    count, tall, _ = header_ref.shape
    rows = tall - PAD
    numbers = row_numbers(dest_ref, first_ref, valid_ref, rows_ref)
    numbers_ref[...] = numbers
    low = rows_ref[...].astype(BF16)
    for target in range(count):
        header_ref[target, :rows] = low
        header_ref[target, rows:] = numbers
    for way, part_ref in zip(ways, part_refs):
        cols = part_ref.shape[2]
        part_ref[...] = piece_ref[:, :, pl.ds(pl.multiple_of(device_at(*way) * cols, cols), cols)]


def rows_body(piece_ref, header_ref, numbers_ref, right_ref, level_ref, *refs):
    grad_ref, left_ref, own_ref = refs
    rows, width = left_ref.shape
    cols = right_ref.shape[0]
    part = own_ref.shape[0]
    block = column_block(cols)
    base = lax.axis_index("narrow") * cols
    dest, begin, end = standing_numbers(numbers_ref[...], rows)
    low = picked(dest, header_ref[:, :rows].reshape(-1, width))
    left_ref[...] = low
    own_ref[...] = right_ref[pl.ds(pl.multiple_of(lax.axis_index("wide") * part, part), part), :]
    grad = jnp.zeros((2 * rows, width), F32)
    norm = jnp.zeros((8, width), F32)
    for start in range(0, cols, block):
        at = pl.ds(start, block)
        right = right_ref[at, :]
        right_low = right.astype(BF16)
        model = model_of(pair_of(low), right_low)
        real, imag, kept = residual_of(piece_ref[0, :, at], piece_ref[1, :, at], model, level_ref[:, at])
        error = masked_error(real, imag, kept, live_mask(begin, end, base + start, block))
        grad = grad + jnp.dot(error, right_low, preferred_element_type=F32)
        norm = norm + jnp.sum((right * right).reshape(-1, 8, width), 0)

    grad_ref[:rows] = grad[:rows] + unturned(grad[rows:])
    grad_ref[rows:] = jnp.broadcast_to(jnp.sum(norm, 0, keepdims=True), (PAD, width))


def step_body(mine_ref, *refs):
    *other_refs, move_ref, out_ref = refs
    total = mine_ref[...]
    for other_ref in other_refs:
        total = total + other_ref[...]
    rows = total.shape[0] - PAD
    move = (total[:rows] / (both_halves(total[rows : rows + 1]) + epsilon)).astype(BF16)
    move_ref[...] = move
    for target in range(out_ref.shape[0]):
        out_ref[target] = move


def cols_body(ways, second, header_ref, right_ref, level_ref, *refs):
    many = len(ways) or 1
    piece_refs, refs = refs[:many], refs[many:]
    if second:
        left_ref, move_ref, change_ref, out_ref, pair_ref, model_ref, error_ref, part_ref = refs
    else:
        next_ref, low_ref, left_ref, pair_ref, model_ref, error_ref = refs
    sources, tall, width = header_ref.shape
    rows = tall - PAD
    part = right_ref.shape[0]
    right = right_ref[...]
    right_low = right.astype(BF16)
    me = lax.axis_index("wide")
    base = lax.axis_index("narrow") * (sources * part) + me * part
    if level_ref.shape[1] == part:
        level = level_ref[...]
    else:
        level = level_ref[:, pl.ds(pl.multiple_of(me * part, part), part)]

    if second:
        left = left_ref[...].astype(F32) + move_ref[...].astype(F32)
        norm = jnp.sum(left * left, 0, keepdims=True)
        left_low = left.astype(BF16)
    else:
        norm = jnp.zeros((1, width), F32)
        for source in range(sources):
            norm = norm + jnp.sum(header_ref[source, rows:, :].astype(F32)[4:7], 0, keepdims=True)
        table = header_ref[:, :rows].reshape(-1, width)

    def place_pair(source, low):
        at = pl.ds(pl.multiple_of(source * 2 * rows, 2 * rows), 2 * rows)
        pair_ref[at, :] = pair_of(low)

    def pick(source):
        dest, _, _ = standing_numbers(header_ref[source, rows:, :], rows)
        low = picked(dest, table)
        left_ref[pl.ds(pl.multiple_of(source * rows, rows), rows), :] = low
        place_pair(source, low)

    def shrink(piece_real, piece_imag, source):
        at = pl.ds(pl.multiple_of(source * 2 * rows, 2 * rows), 2 * rows)
        _, begin, end = standing_numbers(header_ref[source, rows:, :], rows)
        real, imag, kept = residual_of(piece_real, piece_imag, model_ref[at, :], level)
        error_ref[at, :] = masked_error(real, imag, kept, live_mask(begin, end, base, part))

    if second:
        for source in range(sources):
            place_pair(source, left_low[source * rows : (source + 1) * rows])
    elif ways:
        for source in range(sources):
            pick(source)
    else:
        pl.loop(0, sources)(pick)

    model_ref[...] = model_of(pair_ref[...], right_low)
    for way, piece_ref in zip(ways, piece_refs):
        shrink(piece_ref[0], piece_ref[1], device_at(-way[0], -way[1]))
    if not ways:

        @pl.loop(0, sources)
        def _(source):
            shrink(piece_refs[0][source, 0], piece_refs[0][source, 1], source)

    grad = lax.dot_general(pair_ref[...], error_ref[...], (((0,), (0,)), ((), ())), preferred_element_type=F32)
    after = right + grad.T / (both_halves(norm) + epsilon)
    if not second:
        next_ref[...] = after
        low_ref[...] = after.astype(BF16)
        return
    change_ref[...] = (after - right_low.astype(F32)).astype(BF16)

    part_ref[...] = jnp.zeros_like(part_ref)

    def place_grads(source):
        at = pl.ds(pl.multiple_of(source * 2 * rows, 2 * rows), 2 * rows)
        grads = jnp.dot(error_ref[at, :], right_low, preferred_element_type=F32)
        grads = (grads[:rows] + unturned(grads[rows:])).astype(BF16)
        named = read_numbers(header_ref[source, rows:, :])[0:1, :rows].astype(jnp.int32)
        row = lax.broadcasted_iota(jnp.int32, (sources * rows, rows), 0)
        place = jnp.where(row == named, 1.0, 0.0).astype(BF16)
        part_ref[...] += jnp.dot(place, grads, preferred_element_type=F32)

    if ways:
        for source in range(sources):
            place_grads(source)
    else:
        pl.loop(0, sources)(place_grads)

    norm = jnp.sum(right * right, 0, keepdims=True)
    high = norm.astype(BF16).astype(F32)
    tail = jnp.concatenate([high, norm - high, jnp.zeros((PAD - 2, width), F32)], 0).astype(BF16)
    for target in range(sources):
        out_ref[target, :rows] = part_ref[target * rows : (target + 1) * rows].astype(BF16)
        out_ref[target, rows:] = tail


def sparse_body(ways, piece_ref, numbers_ref, left_ref, move_ref, level_ref, *refs):
    right_refs, out_ref = refs[:-1], refs[-1]
    low = (left_ref[...].astype(F32) + move_ref[...].astype(F32)).astype(BF16)
    _, begin, end = standing_numbers(numbers_ref[...], low.shape[0])
    base = lax.axis_index("narrow") * piece_ref.shape[2]

    def one(right, source):
        cols = right.shape[0]
        start = source * cols
        at = pl.ds(pl.multiple_of(start, cols), cols)
        model = model_of(pair_of(low), right)
        real, imag, kept = residual_of(piece_ref[0, :, at], piece_ref[1, :, at], model, level_ref[:, at])
        share = jnp.where(live_mask(begin, end, base + start, cols), 1.0 - kept, 0.0)
        out_ref[0, :, at] = (real * share).astype(BF16)
        out_ref[1, :, at] = (imag * share).astype(BF16)

    for way, right_ref in zip(ways, right_refs):
        one(right_ref[...], device_at(-way[0], -way[1]))
    if not ways:
        block = column_block(right_refs[0].shape[0])

        @pl.loop(0, right_refs[0].shape[0] // block)
        def _(step):
            one(right_refs[0][pl.ds(pl.multiple_of(step * block, block), block), :], step)


def join_body(ways, header_ref, move_ref, rows_ref, mine_ref, *refs):
    narrow = lax.axis_size("narrow") - 1
    other_refs, refs = refs[:narrow], refs[narrow:]
    many = len(ways) or 1
    low_refs, change_refs, refs = refs[:many], refs[many : 2 * many], refs[2 * many :]
    out_ref, rows_out_ref, held_ref, sem = refs
    copies = []
    for index, (low_ref, change_ref) in enumerate(zip(low_refs, change_refs)):
        cols = low_ref.shape[0]
        source = device_at(-ways[index][0], -ways[index][1]) if ways else 0
        held_ref[index] = low_ref[...].astype(F32) + change_ref[...].astype(F32)
        at = pl.ds(pl.multiple_of(source * cols, cols), cols)
        copies.append(pltpu.make_async_copy(held_ref.at[index], out_ref.at[at, :], sem.at[index]))
        copies[-1].start()

    total = mine_ref[...]
    for other_ref in other_refs:
        total = total + other_ref[...]
    rows = total.shape[0] - PAD
    norm = both_halves(total[rows : rows + 1] + total[rows + 1 : rows + 2])
    my_row = lax.axis_index("wide") * rows + lax.broadcasted_iota(jnp.int32, (rows, rows), 0)
    first = jnp.zeros(rows_ref.shape, F32)
    for source in range(header_ref.shape[0]):
        named = read_numbers(header_ref[source, rows:, :])[0:1, :rows].astype(jnp.int32)
        place = jnp.where(my_row == named, 1.0, 0.0).astype(BF16)
        first = first + jnp.dot(place, move_ref[source], preferred_element_type=F32)
    rows_out_ref[...] = rows_ref[...] + first + total[:rows] / (norm + epsilon)
    for copy in copies:
        copy.wait()


VMEM = pl.BlockSpec(memory_space=pltpu.VMEM)


ANY = pl.BlockSpec(memory_space=pl.ANY)


def call(body, shapes, arrays, scratch=(), out_specs=None):
    return pl.pallas_call(
        body,
        in_specs=[VMEM] * len(arrays),
        out_specs=out_specs or jax.tree.map(lambda _: VMEM, shapes),
        out_shape=shapes,
        scratch_shapes=list(scratch),
    )(*arrays)


def column_block(count):
    block = min(512, count)
    while count % block:
        block //= 2
    return block


def exchange(blocks):
    return lax.all_to_all(blocks, "wide", split_axis=0, concat_axis=0, tiled=True)


def other_narrow(value):
    count = lax.axis_size("narrow")
    return [lax.ppermute(value, "narrow", [(i, (i + k) % count) for i in range(count)]) for k in range(1, count)]


def small_wide():
    count = lax.axis_size("wide")
    return count % NEAR == 0 and count <= 4 * NEAR


def shift(value, far, near):
    outer = lax.axis_size("wide") // NEAR
    pairs = [
        (z * NEAR + x, (z + far) % outer * NEAR + (x + near) % NEAR) for z in range(outer) for x in range(NEAR)
    ]
    return lax.ppermute(value, "wide", pairs)


def device_at(far, near):
    outer = lax.axis_size("wide") // NEAR
    me = lax.axis_index("wide")
    return (me // NEAR + far) % outer * NEAR + (me % NEAR + near) % NEAR


def part_ways():
    if not small_wide():
        return ()
    outer = lax.axis_size("wide") // NEAR
    far_first = sorted(range(1, outer), key=lambda far: -min(far, outer - far))
    ways = [(far, near) for far in far_first for near in range(NEAR)]
    return (*ways, *((0, near) for near in range(1, NEAR)), (0, 0))


def gather_ways():
    if not small_wide():
        return ()
    return tuple((far, near) for far in range(lax.axis_size("wide") // NEAR) for near in range(NEAR))


def gather_parts(block, passed_on):
    count = lax.axis_size("wide")
    ways = gather_ways()
    if not ways:
        return [exchange(jnp.broadcast_to(block[None], (count,) + block.shape)).reshape(-1, block.shape[1])]
    outer = count // NEAR
    held = {(0, 0): block}
    for far in sorted(range(1, outer), key=lambda far: -min(far, outer - far)):
        held[far, 0] = shift(block, far, 0)
    for far in range(1, outer):
        if not passed_on(far, outer):
            held |= {(far, near): shift(block, far, near) for near in range(1, NEAR)}
    held |= {(0, near): shift(block, 0, near) for near in range(1, NEAR)}
    return [held[way] if way in held else shift(held[way[0], 0], 0, way[1]) for way in ways]


def program(pieces, destination, first_offset, valid_length, midpoint_factor, offset_factor, threshold):
    count = lax.axis_size("wide")
    _, rows, cols = pieces.shape
    width = offset_factor.shape[1]
    part = cols // count
    total = count * rows
    level = threshold[None, :]
    own_level = level
    if part % 128:
        own_level = lax.dynamic_slice_in_dim(level, lax.axis_index("wide") * part, part, 1)

    ways = part_ways()
    shape = jax.ShapeDtypeStruct
    header, numbers, *parts = call(
        partial(prep_body, ways),
        [shape((count, rows + PAD, width), BF16), shape((PAD, width), BF16)]
        + [shape((2, rows, part), pieces.dtype)] * len(ways),
        [midpoint_factor, destination[None], first_offset[None], valid_length[None]] + [pieces] * bool(ways),
    )
    headers = exchange(header)
    if ways:
        blocks = [block if way == (0, 0) else shift(block, *way) for way, block in zip(ways, parts)]
    else:
        blocks = [exchange(jnp.transpose(pieces.reshape(2, rows, count, part), (2, 0, 1, 3)))]

    row_grad, left_mine, own_right = call(
        rows_body,
        [shape((rows + PAD, width), F32), shape((rows, width), BF16), shape((part, width), F32)],
        [pieces, headers, numbers, offset_factor, level],
    )
    move_mine, moves = call(
        step_body, [shape((rows, width), BF16), shape((count, rows, width), BF16)], [row_grad] + other_narrow(row_grad)
    )
    moves = exchange(moves)

    held = [pltpu.VMEM((2 * total, width), BF16), pltpu.VMEM((2 * total, part), F32), pltpu.VMEM((2 * total, part), BF16)]
    right_one, right_low, left_all = call(
        partial(cols_body, ways, False),
        [shape((part, width), F32), shape((part, width), BF16), shape((total, width), BF16)],
        [headers, own_right, own_level, *blocks],
        held,
    )
    lows = gather_parts(right_low, passed_on=lambda far, outer: True)

    change, outgoing = call(
        partial(cols_body, ways, True),
        [shape((part, width), BF16), shape((count, rows + PAD, width), BF16)],
        [headers, right_one, own_level, *blocks, left_all, moves.reshape(total, width)],
        [*held, pltpu.VMEM((total, width), F32)],
    )
    changes = gather_parts(change, passed_on=lambda far, outer: 2 * far == outer and outer > 2)
    arrived = exchange(outgoing)
    summed = jnp.sum(arrived.astype(F32), 0)

    sparse = call(
        partial(sparse_body, gather_ways()),
        shape(pieces.shape, BF16),
        [pieces, numbers, left_mine, move_mine, level, *lows],
    )
    new_offset, new_midpoint = call(
        partial(join_body, gather_ways()),
        [shape((cols, width), F32), shape((rows, width), F32)],
        [headers, moves, midpoint_factor, summed, *other_narrow(summed), *lows, *changes],
        [pltpu.VMEM((len(lows), cols // len(lows), width), F32), pltpu.SemaphoreType.DMA((len(lows),))],
        [ANY, VMEM],
    )
    return sparse, new_midpoint, new_offset


def solution(mesh):
    placed = (
        P(None, ("groups", "wide"), "narrow"),
        P("wide"),
        P("wide"),
        P("wide"),
        P(("groups", "wide"), None),
        P(("groups", "narrow"), None),
        P(("groups", "narrow")),
    )
    return jax.shard_map(
        program,
        mesh=mesh,
        in_specs=placed,
        out_specs=(
            P(None, ("groups", "wide"), "narrow"),
            P(("groups", "wide"), None),
            P(("groups", "narrow"), None),
        ),
        check_vma=False,
    )
```

time: 112 us -> 108 us (0.964)
  starting transfers between devices: 45.8 us -> 51.6 us
  waiting for transfers between devices: 30 us -> 25 us
  Pallas kernels: 29.8 us -> 25.7 us
    ppermute x21, starting transfers between devices: 30.3 us -> 36.1 us  [shift(): return lax.ppermute(value, 'wide', pairs)]
    pallas_call x7, Pallas kernels: 29.8 us -> 25.7 us  [call(): pl.pallas_call(body, in_specs=[VMEM] * len(arrays), out_specs=out_specs o...]
    all_to_all x3, waiting for transfers between devices: 12.2 us -> 8.86 us  [exchange(): lax.all_to_all(blocks, 'wide', split_axis=0, concat_axis=0, tiled=True)]
    ppermute x21, waiting for transfers between devices: 16.3 us -> 14.7 us  [shift(): return lax.ppermute(value, 'wide', pairs)]
  transfers between devices with their start and end apart: 26 -> 26, of which waited for: 10 -> 9; matrix products, arithmetic and copies ran while one was open for 0% -> 0% of each run, Pallas kernels for 22% -> 18%
where the time goes in v2:
time: 108 us; the launch traced here: 107 us
  starting transfers between devices  51.6 us (48%)
  Pallas kernels  25.7 us (24%)
  waiting for transfers between devices  25 us (23%)
  local copies, waits for them, and re-layouts  3.98 us (4%)
    ppermute x21, starting transfers between devices, shift(): return lax.ppermute(value, 'wide', pairs)  36.1 us
    pallas_call x7, Pallas kernels, call(): pl.pallas_call(body, in_specs=[VMEM] * len(arrays), out_specs=out_specs o...  25.7 us
    all_to_all x3, starting transfers between devices, exchange(): lax.all_to_all(blocks, 'wide', split_axis=0, concat_axis=0, tiled=True)  15.4 us
    ppermute x21, waiting for transfers between devices, shift(): return lax.ppermute(value, 'wide', pairs)  14.7 us
    all_to_all x3, waiting for transfers between devices, exchange(): lax.all_to_all(blocks, 'wide', split_axis=0, concat_axis=0, tiled=True)  8.86 us
    unnamed x62, local copies, waits for them, and re-layouts  3.98 us
  transfers between devices with their start and end apart: 26, of which 9 were waited for; matrix products, arithmetic and copies ran while one was open for 0% of the time, Pallas kernels for 18%

profile of v2, /device:TPU:0, one launch (start us, length us, event | category | flops | bytes accessed | tf_op | source)
XLA Modules:
  0.0 107.2 jit_solution(3565522530582008340)
XLA Ops:
  0.6 2.4 %shard_map.94 = (bf16[8,72,128]{2,1,0:T(8,128)(2,1)}, bf16[8,128]{1,0:T(8,128)(2,1)}, bf16[2,64,512]{2,1,0:T(8,128)(2,1)}, bf16[2,64,512]{2,1,0:T(8,128)(2,1)}, ...) custom-call(f32[64,128]{1,0:T(8,128)} %rows_ref.3, ...), custom_call_target="tpu_custom_call" | custom-call | tf_op jit(solution)/shard_map/pallas_call | solution.py:315
  3.0 7.4 %all-to-all-start = ((bf16[8,72,128]{2,1,0:T(8,128)(2,1)}), bf16[8,72,128]{2,1,0:T(8,128)(2,1)S(1)}, u32[]{:S(2)}, u32[]{:S(2)}) async-start(bf16[8,72,128]{2,1,0:T(8,128)(2,1)} %get-tuple-element.26), calls=%async_computation | async-start | bytes 294912 | tf_op jit(solution)/shard_map/all_to_all | solution.py:332
  10.5 2.9 %collective-permute-start.1 = (bf16[2,64,512]{2,1,0:T(8,128)(2,1)}, bf16[2,64,512]{2,1,0:T(8,128)(2,1)S(1)}, u32[]{:S(2)}, u32[]{:S(2)}) collective-permute-start(bf16[2,64,512]{2,1,0:T(8,128)(2,1)} %get-tuple-element.31), channel_id=1, source_target_pairs={{0,8},{2,10},{4,12},{6,14},{8,0},{10,2},{12,4},{14,6},{1,9},{3,11}... | collective-permute-start | bytes 393224 | tf_op jit(solution)/shard_map/ppermute | solution.py:350
  13.4 1.5 %collective-permute-start.2 = (bf16[2,64,512]{2,1,0:T(8,128)(2,1)}, bf16[2,64,512]{2,1,0:T(8,128)(2,1)S(1)}, u32[]{:S(2)}, u32[]{:S(2)}) collective-permute-start(bf16[2,64,512]{2,1,0:T(8,128)(2,1)} %get-tuple-element.32), channel_id=1, source_target_pairs={{0,10},{2,8},{4,14},{6,12},{8,2},{10,0},{12,6},{14,4},{1,11},{3,9}... | collective-permute-start | bytes 393224 | tf_op jit(solution)/shard_map/ppermute | solution.py:350
  14.8 8.9 %all-to-all-done.header_ref = bf16[8,72,128]{2,1,0:T(8,128)(2,1)S(1)} async-done(((bf16[8,72,128]{2,1,0:T(8,128)(2,1)}), bf16[8,72,128]{2,1,0:T(8,128)(2,1)S(1)}, u32[]{:S(2)}, u32[]{:S(2)}) %all-to-all-start) | async-done | bytes 147488 | tf_op jit(solution)/shard_map/all_to_all | solution.py:332
  24.4 5.0 %shard_map.95 = (f32[72,128]{1,0:T(8,128)}, bf16[64,128]{1,0:T(8,128)(2,1)}, f32[512,128]{1,0:T(8,128)}) custom-call(bf16[2,64,4096]{2,1,0:T(8,128)(2,1)} %piece_ref.3, bf16[8,72,128]{2,1,0:T(8,128)(2,1)} %copy-done, bf16[8,128]{1,0:T(8,128)(2,1)} %get-tuple-element.25.numbers_ref, f32[4096,128]{1,0:T(8,128)} %right_ref.1, f32[1,4096]{1,0:T(1,128)} %bitcast.6), custom_call_target="tpu_custom_call" | custom-call | tf_op jit(solution)/shard_map/pallas_call | solution.py:315
  29.3 1.4 %collective-permute-done.refs_0_ = f32[72,128]{1,0:T(8,128)S(1)} collective-permute-done((f32[72,128]{1,0:T(8,128)}, f32[72,128]{1,0:T(8,128)S(1)}, u32[]{:S(2)}, u32[]{:S(2)}) %collective-permute-start) | collective-permute-done | bytes 36896 | tf_op jit(solution)/shard_map/ppermute | solution.py:337
  31.4 1.6 %shard_map.96 = (bf16[64,128]{1,0:T(8,128)(2,1)}, bf16[8,64,128]{2,1,0:T(8,128)(2,1)}) custom-call(f32[72,128]{1,0:T(8,128)} %get-tuple-element.28.mine_ref, f32[72,128]{1,0:T(8,128)} %copy-done.24), custom_call_target="tpu_custom_call" | custom-call | tf_op jit(solution)/shard_map/pallas_call | solution.py:315
  33.0 3.4 %all-to-all-start.1 = ((bf16[8,64,128]{2,1,0:T(8,128)(2,1)}), bf16[8,64,128]{2,1,0:T(8,128)(2,1)S(1)}, u32[]{:S(2)}, u32[]{:S(2)}) async-start(bf16[8,64,128]{2,1,0:T(8,128)(2,1)} %get-tuple-element.40), calls=%async_computation.1 | async-start | bytes 262144 | tf_op jit(solution)/shard_map/all_to_all | solution.py:332
  36.3 1.9 %collective-permute-start.3 = (bf16[2,64,512]{2,1,0:T(8,128)(2,1)S(1)}, bf16[2,64,512]{2,1,0:T(8,128)(2,1)S(1)}, u32[]{:S(2)}, u32[]{:S(2)}) collective-permute-start(bf16[2,64,512]{2,1,0:T(8,128)(2,1)S(1)} %copy-done.30), channel_id=1, source_target_pairs={{0,4},{2,6},{4,8},{6,10},{8,12},{10,14},{12,0},{14,2},{1,5},{3,7},... | collective-permute-start | bytes 393224 | tf_op jit(solution)/shard_map/ppermute | solution.py:350
  38.3 2.4 %collective-permute-start.4 = (bf16[2,64,512]{2,1,0:T(8,128)(2,1)S(1)}, bf16[2,64,512]{2,1,0:T(8,128)(2,1)S(1)}, u32[]{:S(2)}, u32[]{:S(2)}) collective-permute-start(bf16[2,64,512]{2,1,0:T(8,128)(2,1)S(1)} %copy-done.29), channel_id=1, source_target_pairs={{0,6},{2,4},{4,10},{6,8},{8,14},{10,12},{12,2},{14,0},{1,7},{3,5},... | collective-permute-start | bytes 393224 | tf_op jit(solution)/shard_map/ppermute | solution.py:350
  40.6 2.3 %collective-permute-start.5 = (bf16[2,64,512]{2,1,0:T(8,128)(2,1)S(1)}, bf16[2,64,512]{2,1,0:T(8,128)(2,1)S(1)}, u32[]{:S(2)}, u32[]{:S(2)}) collective-permute-start(bf16[2,64,512]{2,1,0:T(8,128)(2,1)S(1)} %copy-done.28), channel_id=1, source_target_pairs={{0,12},{2,14},{4,0},{6,2},{8,4},{10,6},{12,8},{14,10},{1,13},{3,15... | collective-permute-start | bytes 393224 | tf_op jit(solution)/shard_map/ppermute | solution.py:350
  43.2 1.9 %collective-permute-start.7 = (bf16[2,64,512]{2,1,0:T(8,128)(2,1)S(1)}, bf16[2,64,512]{2,1,0:T(8,128)(2,1)S(1)}, u32[]{:S(2)}, u32[]{:S(2)}) collective-permute-start(bf16[2,64,512]{2,1,0:T(8,128)(2,1)S(1)} %copy-done.26), channel_id=1, source_target_pairs={{0,2},{2,0},{4,6},{6,4},{8,10},{10,8},{12,14},{14,12},{1,3},{3,1},... | collective-permute-start | bytes 393224 | tf_op jit(solution)/shard_map/ppermute | solution.py:350
  45.1 1.6 %collective-permute-done.3.refs_2_ = bf16[2,64,512]{2,1,0:T(8,128)(2,1)S(1)} collective-permute-done((bf16[2,64,512]{2,1,0:T(8,128)(2,1)S(1)}, bf16[2,64,512]{2,1,0:T(8,128)(2,1)S(1)}, u32[]{:S(2)}, u32[]{:S(2)}) %collective-permute-start.3) | collective-permute-done | bytes 131104 | tf_op jit(solution)/shard_map/ppermute | solution.py:350
  46.7 3.7 %collective-permute-done.4.refs_3_ = bf16[2,64,512]{2,1,0:T(8,128)(2,1)S(1)} collective-permute-done((bf16[2,64,512]{2,1,0:T(8,128)(2,1)S(1)}, bf16[2,64,512]{2,1,0:T(8,128)(2,1)S(1)}, u32[]{:S(2)}, u32[]{:S(2)}) %collective-permute-start.4) | collective-permute-done | bytes 131104 | tf_op jit(solution)/shard_map/ppermute | solution.py:350
  51.5 2.9 %collective-permute-done.6.refs_5_ = bf16[2,64,512]{2,1,0:T(8,128)(2,1)S(1)} collective-permute-done((bf16[2,64,512]{2,1,0:T(8,128)(2,1)S(1)}, bf16[2,64,512]{2,1,0:T(8,128)(2,1)S(1)}, u32[]{:S(2)}, u32[]{:S(2)}) %collective-permute-start.6) | collective-permute-done | bytes 131104 | tf_op jit(solution)/shard_map/ppermute | solution.py:350
  55.2 4.7 %shard_map.97 = (f32[512,128]{1,0:T(8,128)}, bf16[512,128]{1,0:T(8,128)(2,1)}, bf16[512,128]{1,0:T(8,128)(2,1)}) custom-call(bf16[8,72,128]{2,1,0:T(8,128)(2,1)} %copy-done, f32[512,128]{1,0:T(8,128)} %get-tuple-element.30.right_ref, f32[1,4096]{1,0:T(1,128)} %bitcast.7, bf16[2,64,512]{2,1,0:T(8,128)(2,1)} %copy-done.9, bf16[2,64,512]{2,1,0:T(8,128)(2,1)} %copy-done.10, ...), custom_call_target="tpu_custom_call" | custom-call | tf_op jit(solution)/shard_map/pallas_call | solution.py:315
  59.9 1.4 %collective-permute-start.13 = (bf16[512,128]{1,0:T(8,128)(2,1)}, bf16[512,128]{1,0:T(8,128)(2,1)S(1)}, u32[]{:S(2)}, u32[]{:S(2)}) collective-permute-start(bf16[512,128]{1,0:T(8,128)(2,1)} %get-tuple-element.39.refs_0_.refs_1_), channel_id=1, source_target_pairs={{0,12},{2,14},{4,0},{6,2},{8,4},{10,6},{12,8},{14,10},{1,13},{3,15... | collective-permute-start | bytes 393224 | tf_op jit(solution)/shard_map/ppermute | solution.py:350
  61.3 1.3 %collective-permute-start.11 = (bf16[512,128]{1,0:T(8,128)(2,1)}, bf16[512,128]{1,0:T(8,128)(2,1)S(1)}, u32[]{:S(2)}, u32[]{:S(2)}) collective-permute-start(bf16[512,128]{1,0:T(8,128)(2,1)} %get-tuple-element.39.refs_0_.refs_1_), channel_id=1, source_target_pairs={{0,8},{2,10},{4,12},{6,14},{8,0},{10,2},{12,4},{14,6},{1,9},{3,11}... | collective-permute-start | bytes 393224 | tf_op jit(solution)/shard_map/ppermute | solution.py:350
  65.2 4.6 %shard_map.99 = (bf16[512,128]{1,0:T(8,128)(2,1)}, bf16[8,72,128]{2,1,0:T(8,128)(2,1)}) custom-call(bf16[8,72,128]{2,1,0:T(8,128)(2,1)} %copy-done, f32[512,128]{1,0:T(8,128)} %get-tuple-element.41.right_ref, f32[1,4096]{1,0:T(1,128)} %bitcast.8, bf16[2,64,512]{2,1,0:T(8,128)(2,1)} %copy-done.9, bf16[2,64,512]{2,1,0:T(8,128)(2,1)} %copy-done.10, ...), custom_call_target="tpu_custom_call" | custom-call | tf_op jit(solution)/shard_map/pallas_call | solution.py:315
  69.9 4.6 %all-to-all-start.2 = ((bf16[8,72,128]{2,1,0:T(8,128)(2,1)}), bf16[8,72,128]{2,1,0:T(8,128)(2,1)S(1)}, u32[]{:S(2)}, u32[]{:S(2)}) async-start(bf16[8,72,128]{2,1,0:T(8,128)(2,1)} %get-tuple-element.43), calls=%async_computation.2 | async-start | bytes 294912 | tf_op jit(solution)/shard_map/all_to_all | solution.py:332
  74.5 2.1 %collective-permute-start.14 = (bf16[512,128]{1,0:T(8,128)(2,1)S(1)}, bf16[512,128]{1,0:T(8,128)(2,1)S(1)}, u32[]{:S(2)}, u32[]{:S(2)}) collective-permute-start(bf16[512,128]{1,0:T(8,128)(2,1)S(1)} %collective-permute-done.13.refs_6_.refs_7_), channel_id=1, source_target_pairs={{0,2},{2,0},{4,6},{6,4},{8,10},{10,8},{12,14},{14,12},{1,3},{3,1},... | collective-permute-start | bytes 393224 | tf_op jit(solution)/shard_map/ppermute | solution.py:350
  76.7 1.9 %collective-permute-start.10 = (bf16[512,128]{1,0:T(8,128)(2,1)S(1)}, bf16[512,128]{1,0:T(8,128)(2,1)S(1)}, u32[]{:S(2)}, u32[]{:S(2)}) collective-permute-start(bf16[512,128]{1,0:T(8,128)(2,1)S(1)} %collective-permute-done.9.refs_2_.refs_3_), channel_id=1, source_target_pairs={{0,2},{2,0},{4,6},{6,4},{8,10},{10,8},{12,14},{14,12},{1,3},{3,1},... | collective-permute-start | bytes 393224 | tf_op jit(solution)/shard_map/ppermute | solution.py:350
  78.6 3.3 %collective-permute-start.22 = (bf16[512,128]{1,0:T(8,128)(2,1)}, bf16[512,128]{1,0:T(8,128)(2,1)S(1)}, u32[]{:S(2)}, u32[]{:S(2)}) collective-permute-start(bf16[512,128]{1,0:T(8,128)(2,1)} %get-tuple-element.44.refs_9_), channel_id=1, source_target_pairs={{0,14},{2,12},{4,2},{6,0},{8,6},{10,4},{12,10},{14,8},{1,15},{3,13... | collective-permute-start | bytes 393224 | tf_op jit(solution)/shard_map/ppermute | solution.py:350
  81.9 2.1 %collective-permute-done.14.refs_7_.refs_8_ = bf16[512,128]{1,0:T(8,128)(2,1)S(1)} collective-permute-done((bf16[512,128]{1,0:T(8,128)(2,1)S(1)}, bf16[512,128]{1,0:T(8,128)(2,1)S(1)}, u32[]{:S(2)}, u32[]{:S(2)}) %collective-permute-start.14) | collective-permute-done | bytes 131104 | tf_op jit(solution)/shard_map/ppermute | solution.py:350
  84.0 2.7 %collective-permute-start.21 = (bf16[512,128]{1,0:T(8,128)(2,1)}, bf16[512,128]{1,0:T(8,128)(2,1)S(1)}, u32[]{:S(2)}, u32[]{:S(2)}) collective-permute-start(bf16[512,128]{1,0:T(8,128)(2,1)} %get-tuple-element.44.refs_9_), channel_id=1, source_target_pairs={{0,12},{2,14},{4,0},{6,2},{8,4},{10,6},{12,8},{14,10},{1,13},{3,15... | collective-permute-start | bytes 393224 | tf_op jit(solution)/shard_map/ppermute | solution.py:350
  87.3 2.7 %collective-permute-start.18 = (bf16[512,128]{1,0:T(8,128)(2,1)}, bf16[512,128]{1,0:T(8,128)(2,1)S(1)}, u32[]{:S(2)}, u32[]{:S(2)}) collective-permute-start(bf16[512,128]{1,0:T(8,128)(2,1)} %get-tuple-element.44.refs_9_), channel_id=1, source_target_pairs={{0,6},{2,4},{4,10},{6,8},{8,14},{10,12},{12,2},{14,0},{1,7},{3,5},... | collective-permute-start | bytes 393224 | tf_op jit(solution)/shard_map/ppermute | solution.py:350
  90.1 1.5 %collective-permute-start.17 = (bf16[512,128]{1,0:T(8,128)(2,1)}, bf16[512,128]{1,0:T(8,128)(2,1)S(1)}, u32[]{:S(2)}, u32[]{:S(2)}) collective-permute-start(bf16[512,128]{1,0:T(8,128)(2,1)} %get-tuple-element.44.refs_9_), channel_id=1, source_target_pairs={{0,4},{2,6},{4,8},{6,10},{8,12},{10,14},{12,0},{14,2},{1,5},{3,7},... | collective-permute-start | bytes 393224 | tf_op jit(solution)/shard_map/ppermute | solution.py:350
  92.7 2.6 %collective-permute-done.19.refs_13_ = bf16[512,128]{1,0:T(8,128)(2,1)S(1)} collective-permute-done((bf16[512,128]{1,0:T(8,128)(2,1)}, bf16[512,128]{1,0:T(8,128)(2,1)S(1)}, u32[]{:S(2)}, u32[]{:S(2)}) %collective-permute-start.19) | collective-permute-done | bytes 131104 | tf_op jit(solution)/shard_map/ppermute | solution.py:350
  95.3 2.9 %collective-permute-start.20 = (bf16[512,128]{1,0:T(8,128)(2,1)S(1)}, bf16[512,128]{1,0:T(8,128)(2,1)S(1)}, u32[]{:S(2)}, u32[]{:S(2)}) collective-permute-start(bf16[512,128]{1,0:T(8,128)(2,1)S(1)} %collective-permute-done.19.refs_13_), channel_id=1, source_target_pairs={{0,2},{2,0},{4,6},{6,4},{8,10},{10,8},{12,14},{14,12},{1,3},{3,1},... | collective-permute-start | bytes 393224 | tf_op jit(solution)/shard_map/ppermute | solution.py:350
  98.4 3.6 %shard_map.98 = bf16[2,64,4096]{2,1,0:T(8,128)(2,1)} custom-call(bf16[2,64,4096]{2,1,0:T(8,128)(2,1)} %piece_ref.3, bf16[8,128]{1,0:T(8,128)(2,1)} %get-tuple-element.25.numbers_ref, bf16[64,128]{1,0:T(8,128)(2,1)} %get-tuple-element.27.left_ref, bf16[64,128]{1,0:T(8,128)(2,1)} %get-tuple-element.29.move_ref, f32[1,4096]{1,0:T(1,128)} %bitcast.9, ...), custom_call_target="tpu_custom_call" | custom-call | tf_op jit(solution)/shard_map/pallas_call | solution.py:315
  103.4 3.8 %shard_map.100 = (f32[4096,128]{1,0:T(8,128)}, f32[64,128]{1,0:T(8,128)}) custom-call(bf16[8,72,128]{2,1,0:T(8,128)(2,1)} %copy-done, bf16[8,64,128]{2,1,0:T(8,128)(2,1)} %copy-done.1, f32[64,128]{1,0:T(8,128)} %rows_ref.3, f32[72,128]{1,0:T(8,128)} %copy-done.16, f32[72,128]{1,0:T(8,128)} %copy-done.25, bf16[512,128]{1,0:T(8,128)(2,1)} %get-tuple-element.39.refs_0_.refs_1_, ...), custom_call_target="tpu_custom_call" | custom-call | tf_op jit(solution)/shard_map/pallas_call | solution.py:315
  (90 shorter events, 9.1 us)
Async XLA Ops:
  3.0 33.3 %copy-start.30 = (bf16[2,64,512]{2,1,0:T(8,128)(2,1)S(1)}, bf16[2,64,512]{2,1,0:T(8,128)(2,1)}, u32[]{:S(2)}) copy-start(bf16[2,64,512]{2,1,0:T(8,128)(2,1)} %get-tuple-element.33) | copy-start | bytes 393220
  3.0 35.3 %copy-start.29 = (bf16[2,64,512]{2,1,0:T(8,128)(2,1)S(1)}, bf16[2,64,512]{2,1,0:T(8,128)(2,1)}, u32[]{:S(2)}) copy-start(bf16[2,64,512]{2,1,0:T(8,128)(2,1)} %get-tuple-element.34) | copy-start | bytes 393220
  3.0 37.6 %copy-start.28 = (bf16[2,64,512]{2,1,0:T(8,128)(2,1)S(1)}, bf16[2,64,512]{2,1,0:T(8,128)(2,1)}, u32[]{:S(2)}) copy-start(bf16[2,64,512]{2,1,0:T(8,128)(2,1)} %get-tuple-element.35) | copy-start | bytes 393220
  3.0 40.0 %copy-start.27 = (bf16[2,64,512]{2,1,0:T(8,128)(2,1)S(1)}, bf16[2,64,512]{2,1,0:T(8,128)(2,1)}, u32[]{:S(2)}) copy-start(bf16[2,64,512]{2,1,0:T(8,128)(2,1)} %get-tuple-element.36) | copy-start | bytes 393220
  3.0 40.2 %copy-start.26 = (bf16[2,64,512]{2,1,0:T(8,128)(2,1)S(1)}, bf16[2,64,512]{2,1,0:T(8,128)(2,1)}, u32[]{:S(2)}) copy-start(bf16[2,64,512]{2,1,0:T(8,128)(2,1)} %get-tuple-element.37) | copy-start | bytes 393220
  3.0 20.7 %all-to-all-start = ((bf16[8,72,128]{2,1,0:T(8,128)(2,1)}), bf16[8,72,128]{2,1,0:T(8,128)(2,1)S(1)}, u32[]{:S(2)}, u32[]{:S(2)}) async-start(bf16[8,72,128]{2,1,0:T(8,128)(2,1)} %get-tuple-element.26), calls=%async_computation | async-start | bytes 294912 | tf_op jit(solution)/shard_map/all_to_all | solution.py:332
  10.5 32.5 %collective-permute-start.1 = (bf16[2,64,512]{2,1,0:T(8,128)(2,1)}, bf16[2,64,512]{2,1,0:T(8,128)(2,1)S(1)}, u32[]{:S(2)}, u32[]{:S(2)}) collective-permute-start(bf16[2,64,512]{2,1,0:T(8,128)(2,1)} %get-tuple-element.31), channel_id=1, source_target_pairs={{0,8},{2,10},{4,12},{6,14},{8,0},{10,2},{12,4},{14,6},{1,9},{3,11}... | collective-permute-start | bytes 393224 | tf_op jit(solution)/shard_map/ppermute | solution.py:350
  13.4 29.8 %collective-permute-start.2 = (bf16[2,64,512]{2,1,0:T(8,128)(2,1)}, bf16[2,64,512]{2,1,0:T(8,128)(2,1)S(1)}, u32[]{:S(2)}, u32[]{:S(2)}) collective-permute-start(bf16[2,64,512]{2,1,0:T(8,128)(2,1)} %get-tuple-element.32), channel_id=1, source_target_pairs={{0,10},{2,8},{4,14},{6,12},{8,2},{10,0},{12,6},{14,4},{1,11},{3,9}... | collective-permute-start | bytes 393224 | tf_op jit(solution)/shard_map/ppermute | solution.py:350
  29.3 1.4 %collective-permute-start = (f32[72,128]{1,0:T(8,128)}, f32[72,128]{1,0:T(8,128)S(1)}, u32[]{:S(2)}, u32[]{:S(2)}) collective-permute-start(f32[72,128]{1,0:T(8,128)} %get-tuple-element.28.mine_ref), channel_id=1, source_target_pairs={{0,1},{1,0},{2,3},{3,2},{4,5},{5,4},{6,7},{7,6},{8,9},{9,8},{10,11... | collective-permute-start | bytes 110600 | tf_op jit(solution)/shard_map/ppermute | solution.py:337
  33.0 31.6 %all-to-all-start.1 = ((bf16[8,64,128]{2,1,0:T(8,128)(2,1)}), bf16[8,64,128]{2,1,0:T(8,128)(2,1)S(1)}, u32[]{:S(2)}, u32[]{:S(2)}) async-start(bf16[8,64,128]{2,1,0:T(8,128)(2,1)} %get-tuple-element.40), calls=%async_computation.1 | async-start | bytes 262144 | tf_op jit(solution)/shard_map/all_to_all | solution.py:332
  36.3 10.4 %collective-permute-start.3 = (bf16[2,64,512]{2,1,0:T(8,128)(2,1)S(1)}, bf16[2,64,512]{2,1,0:T(8,128)(2,1)S(1)}, u32[]{:S(2)}, u32[]{:S(2)}) collective-permute-start(bf16[2,64,512]{2,1,0:T(8,128)(2,1)S(1)} %copy-done.30), channel_id=1, source_target_pairs={{0,4},{2,6},{4,8},{6,10},{8,12},{10,14},{12,0},{14,2},{1,5},{3,7},... | collective-permute-start | bytes 393224 | tf_op jit(solution)/shard_map/ppermute | solution.py:350
  38.3 12.2 %collective-permute-start.4 = (bf16[2,64,512]{2,1,0:T(8,128)(2,1)S(1)}, bf16[2,64,512]{2,1,0:T(8,128)(2,1)S(1)}, u32[]{:S(2)}, u32[]{:S(2)}) collective-permute-start(bf16[2,64,512]{2,1,0:T(8,128)(2,1)S(1)} %copy-done.29), channel_id=1, source_target_pairs={{0,6},{2,4},{4,10},{6,8},{8,14},{10,12},{12,2},{14,0},{1,7},{3,5},... | collective-permute-start | bytes 393224 | tf_op jit(solution)/shard_map/ppermute | solution.py:350
  40.6 10.9 %collective-permute-start.5 = (bf16[2,64,512]{2,1,0:T(8,128)(2,1)S(1)}, bf16[2,64,512]{2,1,0:T(8,128)(2,1)S(1)}, u32[]{:S(2)}, u32[]{:S(2)}) collective-permute-start(bf16[2,64,512]{2,1,0:T(8,128)(2,1)S(1)} %copy-done.28), channel_id=1, source_target_pairs={{0,12},{2,14},{4,0},{6,2},{8,4},{10,6},{12,8},{14,10},{1,13},{3,15... | collective-permute-start | bytes 393224 | tf_op jit(solution)/shard_map/ppermute | solution.py:350
  43.0 11.5 %collective-permute-start.6 = (bf16[2,64,512]{2,1,0:T(8,128)(2,1)S(1)}, bf16[2,64,512]{2,1,0:T(8,128)(2,1)S(1)}, u32[]{:S(2)}, u32[]{:S(2)}) collective-permute-start(bf16[2,64,512]{2,1,0:T(8,128)(2,1)S(1)} %copy-done.27), channel_id=1, source_target_pairs={{0,14},{2,12},{4,2},{6,0},{8,6},{10,4},{12,10},{14,8},{1,15},{3,13... | collective-permute-start | bytes 393224 | tf_op jit(solution)/shard_map/ppermute | solution.py:350
  43.2 11.3 %collective-permute-start.7 = (bf16[2,64,512]{2,1,0:T(8,128)(2,1)S(1)}, bf16[2,64,512]{2,1,0:T(8,128)(2,1)S(1)}, u32[]{:S(2)}, u32[]{:S(2)}) collective-permute-start(bf16[2,64,512]{2,1,0:T(8,128)(2,1)S(1)} %copy-done.26), channel_id=1, source_target_pairs={{0,2},{2,0},{4,6},{6,4},{8,10},{10,8},{12,14},{14,12},{1,3},{3,1},... | collective-permute-start | bytes 393224 | tf_op jit(solution)/shard_map/ppermute | solution.py:350
  59.9 14.5 %collective-permute-start.13 = (bf16[512,128]{1,0:T(8,128)(2,1)}, bf16[512,128]{1,0:T(8,128)(2,1)S(1)}, u32[]{:S(2)}, u32[]{:S(2)}) collective-permute-start(bf16[512,128]{1,0:T(8,128)(2,1)} %get-tuple-element.39.refs_0_.refs_1_), channel_id=1, source_target_pairs={{0,12},{2,14},{4,0},{6,2},{8,4},{10,6},{12,8},{14,10},{1,13},{3,15... | collective-permute-start | bytes 393224 | tf_op jit(solution)/shard_map/ppermute | solution.py:350
  61.3 15.2 %collective-permute-start.11 = (bf16[512,128]{1,0:T(8,128)(2,1)}, bf16[512,128]{1,0:T(8,128)(2,1)S(1)}, u32[]{:S(2)}, u32[]{:S(2)}) collective-permute-start(bf16[512,128]{1,0:T(8,128)(2,1)} %get-tuple-element.39.refs_0_.refs_1_), channel_id=1, source_target_pairs={{0,8},{2,10},{4,12},{6,14},{8,0},{10,2},{12,4},{14,6},{1,9},{3,11}... | collective-permute-start | bytes 393224 | tf_op jit(solution)/shard_map/ppermute | solution.py:350
  62.6 14.0 %collective-permute-start.9 = (bf16[512,128]{1,0:T(8,128)(2,1)}, bf16[512,128]{1,0:T(8,128)(2,1)S(1)}, u32[]{:S(2)}, u32[]{:S(2)}) collective-permute-start(bf16[512,128]{1,0:T(8,128)(2,1)} %get-tuple-element.39.refs_0_.refs_1_), channel_id=1, source_target_pairs={{0,4},{2,6},{4,8},{6,10},{8,12},{10,14},{12,0},{14,2},{1,5},{3,7},... | collective-permute-start | bytes 393224 | tf_op jit(solution)/shard_map/ppermute | solution.py:350
  63.9 18.0 %collective-permute-start.8 = (bf16[512,128]{1,0:T(8,128)(2,1)}, bf16[512,128]{1,0:T(8,128)(2,1)S(1)}, u32[]{:S(2)}, u32[]{:S(2)}) collective-permute-start(bf16[512,128]{1,0:T(8,128)(2,1)} %get-tuple-element.39.refs_0_.refs_1_), channel_id=1, source_target_pairs={{0,2},{2,0},{4,6},{6,4},{8,10},{10,8},{12,14},{14,12},{1,3},{3,1},... | collective-permute-start | bytes 393224 | tf_op jit(solution)/shard_map/ppermute | solution.py:350
  69.9 28.3 %all-to-all-start.2 = ((bf16[8,72,128]{2,1,0:T(8,128)(2,1)}), bf16[8,72,128]{2,1,0:T(8,128)(2,1)S(1)}, u32[]{:S(2)}, u32[]{:S(2)}) async-start(bf16[8,72,128]{2,1,0:T(8,128)(2,1)} %get-tuple-element.43), calls=%async_computation.2 | async-start | bytes 294912 | tf_op jit(solution)/shard_map/all_to_all | solution.py:332
  74.5 23.8 %copy-start.2 = (bf16[512,128]{1,0:T(8,128)(2,1)}, bf16[512,128]{1,0:T(8,128)(2,1)S(1)}, u32[]{:S(2)}) copy-start(bf16[512,128]{1,0:T(8,128)(2,1)S(1)} %collective-permute-done.13.refs_6_.refs_7_) | copy-start | bytes 393220
  74.5 9.5 %collective-permute-start.14 = (bf16[512,128]{1,0:T(8,128)(2,1)S(1)}, bf16[512,128]{1,0:T(8,128)(2,1)S(1)}, u32[]{:S(2)}, u32[]{:S(2)}) collective-permute-start(bf16[512,128]{1,0:T(8,128)(2,1)S(1)} %collective-permute-done.13.refs_6_.refs_7_), channel_id=1, source_target_pairs={{0,2},{2,0},{4,6},{6,4},{8,10},{10,8},{12,14},{14,12},{1,3},{3,1},... | collective-permute-start | bytes 393224 | tf_op jit(solution)/shard_map/ppermute | solution.py:350
  76.6 10.7 %collective-permute-start.12 = (bf16[512,128]{1,0:T(8,128)(2,1)S(1)}, bf16[512,128]{1,0:T(8,128)(2,1)S(1)}, u32[]{:S(2)}, u32[]{:S(2)}) collective-permute-start(bf16[512,128]{1,0:T(8,128)(2,1)S(1)} %collective-permute-done.11.refs_4_.refs_5_), channel_id=1, source_target_pairs={{0,2},{2,0},{4,6},{6,4},{8,10},{10,8},{12,14},{14,12},{1,3},{3,1},... | collective-permute-start | bytes 393224 | tf_op jit(solution)/shard_map/ppermute | solution.py:350
  76.7 13.4 %collective-permute-start.10 = (bf16[512,128]{1,0:T(8,128)(2,1)S(1)}, bf16[512,128]{1,0:T(8,128)(2,1)S(1)}, u32[]{:S(2)}, u32[]{:S(2)}) collective-permute-start(bf16[512,128]{1,0:T(8,128)(2,1)S(1)} %collective-permute-done.9.refs_2_.refs_3_), channel_id=1, source_target_pairs={{0,2},{2,0},{4,6},{6,4},{8,10},{10,8},{12,14},{14,12},{1,3},{3,1},... | collective-permute-start | bytes 393224 | tf_op jit(solution)/shard_map/ppermute | solution.py:350
  78.6 13.0 %collective-permute-start.22 = (bf16[512,128]{1,0:T(8,128)(2,1)}, bf16[512,128]{1,0:T(8,128)(2,1)S(1)}, u32[]{:S(2)}, u32[]{:S(2)}) collective-permute-start(bf16[512,128]{1,0:T(8,128)(2,1)} %get-tuple-element.44.refs_9_), channel_id=1, source_target_pairs={{0,14},{2,12},{4,2},{6,0},{8,6},{10,4},{12,10},{14,8},{1,15},{3,13... | collective-permute-start | bytes 393224 | tf_op jit(solution)/shard_map/ppermute | solution.py:350
  81.9 13.4 %collective-permute-start.19 = (bf16[512,128]{1,0:T(8,128)(2,1)}, bf16[512,128]{1,0:T(8,128)(2,1)S(1)}, u32[]{:S(2)}, u32[]{:S(2)}) collective-permute-start(bf16[512,128]{1,0:T(8,128)(2,1)} %get-tuple-element.44.refs_9_), channel_id=1, source_target_pairs={{0,8},{2,10},{4,12},{6,14},{8,0},{10,2},{12,4},{14,6},{1,9},{3,11}... | collective-permute-start | bytes 393224 | tf_op jit(solution)/shard_map/ppermute | solution.py:350
  84.0 14.2 %collective-permute-start.21 = (bf16[512,128]{1,0:T(8,128)(2,1)}, bf16[512,128]{1,0:T(8,128)(2,1)S(1)}, u32[]{:S(2)}, u32[]{:S(2)}) collective-permute-start(bf16[512,128]{1,0:T(8,128)(2,1)} %get-tuple-element.44.refs_9_), channel_id=1, source_target_pairs={{0,12},{2,14},{4,0},{6,2},{8,4},{10,6},{12,8},{14,10},{1,13},{3,15... | collective-permute-start | bytes 393224 | tf_op jit(solution)/shard_map/ppermute | solution.py:350
  87.3 14.7 %collective-permute-start.18 = (bf16[512,128]{1,0:T(8,128)(2,1)}, bf16[512,128]{1,0:T(8,128)(2,1)S(1)}, u32[]{:S(2)}, u32[]{:S(2)}) collective-permute-start(bf16[512,128]{1,0:T(8,128)(2,1)} %get-tuple-element.44.refs_9_), channel_id=1, source_target_pairs={{0,6},{2,4},{4,10},{6,8},{8,14},{10,12},{12,2},{14,0},{1,7},{3,5},... | collective-permute-start | bytes 393224 | tf_op jit(solution)/shard_map/ppermute | solution.py:350
  90.1 11.9 %collective-permute-start.17 = (bf16[512,128]{1,0:T(8,128)(2,1)}, bf16[512,128]{1,0:T(8,128)(2,1)S(1)}, u32[]{:S(2)}, u32[]{:S(2)}) collective-permute-start(bf16[512,128]{1,0:T(8,128)(2,1)} %get-tuple-element.44.refs_9_), channel_id=1, source_target_pairs={{0,4},{2,6},{4,8},{6,10},{8,12},{10,14},{12,0},{14,2},{1,5},{3,7},... | collective-permute-start | bytes 393224 | tf_op jit(solution)/shard_map/ppermute | solution.py:350
  91.6 10.4 %collective-permute-start.16 = (bf16[512,128]{1,0:T(8,128)(2,1)}, bf16[512,128]{1,0:T(8,128)(2,1)S(1)}, u32[]{:S(2)}, u32[]{:S(2)}) collective-permute-start(bf16[512,128]{1,0:T(8,128)(2,1)} %get-tuple-element.44.refs_9_), channel_id=1, source_target_pairs={{0,2},{2,0},{4,6},{6,4},{8,10},{10,8},{12,14},{14,12},{1,3},{3,1},... | collective-permute-start | bytes 393224 | tf_op jit(solution)/shard_map/ppermute | solution.py:350
  95.3 6.7 %collective-permute-start.20 = (bf16[512,128]{1,0:T(8,128)(2,1)S(1)}, bf16[512,128]{1,0:T(8,128)(2,1)S(1)}, u32[]{:S(2)}, u32[]{:S(2)}) collective-permute-start(bf16[512,128]{1,0:T(8,128)(2,1)S(1)} %collective-permute-done.19.refs_13_), channel_id=1, source_target_pairs={{0,2},{2,0},{4,6},{6,4},{8,10},{10,8},{12,14},{14,12},{1,3},{3,1},... | collective-permute-start | bytes 393224 | tf_op jit(solution)/shard_map/ppermute | solution.py:350
  98.2 3.8 %collective-permute-start.15 = (f32[72,128]{1,0:T(8,128)S(1)}, f32[72,128]{1,0:T(8,128)S(1)}, u32[]{:S(2)}, u32[]{:S(2)}) collective-permute-start(f32[72,128]{1,0:T(8,128)S(1)} %convert_reduce_fusion.mine_ref), channel_id=1, source_target_pairs={{0,1},{1,0},{2,3},{3,2},{4,5},{5,4},{6,7},{7,6},{8,9},{9,8},{10,11... | collective-permute-start | bytes 110600 | tf_op jit(solution)/shard_map/ppermute | solution.py:337
  (25 other events, 162.9 us)

commit v3 on v2

--- a/solution.py
+++ b/solution.py
@@ -1,3 +1,4 @@
+import math
 from functools import partial
 
 import jax
@@ -208,7 +209,7 @@
 
     model_ref[...] = model_of(pair_ref[...], right_low)
     for way, piece_ref in zip(ways, piece_refs):
-        shrink(piece_ref[0], piece_ref[1], device_at(-way[0], -way[1]))
+        shrink(piece_ref[0], piece_ref[1], device_at(*way))
     if not ways:
 
         @pl.loop(0, sources)
@@ -265,7 +266,7 @@
         out_ref[1, :, at] = (imag * share).astype(BF16)
 
     for way, right_ref in zip(ways, right_refs):
-        one(right_ref[...], device_at(-way[0], -way[1]))
+        one(right_ref[...], device_at(*way))
     if not ways:
         block = column_block(right_refs[0].shape[0])
 
@@ -283,7 +284,7 @@
     copies = []
     for index, (low_ref, change_ref) in enumerate(zip(low_refs, change_refs)):
         cols = low_ref.shape[0]
-        source = device_at(-ways[index][0], -ways[index][1]) if ways else 0
+        source = device_at(*ways[index]) if ways else 0
         held_ref[index] = low_ref[...].astype(F32) + change_ref[...].astype(F32)
         at = pl.ds(pl.multiple_of(source * cols, cols), cols)
         copies.append(pltpu.make_async_copy(held_ref.at[index], out_ref.at[at, :], sem.at[index]))
@@ -308,10 +309,21 @@
 VMEM = pl.BlockSpec(memory_space=pltpu.VMEM)
 
 
+SMALL = 400000
+
+
+def small(value):
+    return math.prod(value.shape) * jnp.dtype(value.dtype).itemsize < SMALL
+
+
 ANY = pl.BlockSpec(memory_space=pl.ANY)
 
 
-def call(body, shapes, arrays, scratch=(), out_specs=None):
+def call(body, name, shapes, arrays, scratch=(), out_specs=None, keep=True):
+    if keep:
+        shapes = jax.tree.map(lambda v: pltpu.VMEM(v.shape, v.dtype) if small(v) else v, shapes)
+    if name != "prep":
+        arrays = [pltpu.with_memory_space_constraint(v, pltpu.VMEM) if small(v) else v for v in arrays]
     return pl.pallas_call(
         body,
         in_specs=[VMEM] * len(arrays),
@@ -345,15 +357,14 @@
 def shift(value, far, near):
     outer = lax.axis_size("wide") // NEAR
     pairs = [
-        (z * NEAR + x, (z + far) % outer * NEAR + (x + near) % NEAR) for z in range(outer) for x in range(NEAR)
+        (z * NEAR + x, (z ^ far) * NEAR + (x ^ near)) for z in range(outer) for x in range(NEAR)
     ]
     return lax.ppermute(value, "wide", pairs)
 
 
 def device_at(far, near):
-    outer = lax.axis_size("wide") // NEAR
     me = lax.axis_index("wide")
-    return (me // NEAR + far) % outer * NEAR + (me % NEAR + near) % NEAR
+    return ((me // NEAR) ^ far) * NEAR + ((me % NEAR) ^ near)
 
 
 def part_ways():
@@ -362,7 +373,7 @@
     outer = lax.axis_size("wide") // NEAR
     far_first = sorted(range(1, outer), key=lambda far: -min(far, outer - far))
     ways = [(far, near) for far in far_first for near in range(NEAR)]
-    return (*ways, *((0, near) for near in range(1, NEAR)), (0, 0))
+    return (*((0, near) for near in range(1, NEAR)), *reversed(ways), (0, 0))
 
 
 def gather_ways():
@@ -402,9 +413,11 @@
     shape = jax.ShapeDtypeStruct
     header, numbers, *parts = call(
         partial(prep_body, ways),
+        "prep",
         [shape((count, rows + PAD, width), BF16), shape((PAD, width), BF16)]
         + [shape((2, rows, part), pieces.dtype)] * len(ways),
         [midpoint_factor, destination[None], first_offset[None], valid_length[None]] + [pieces] * bool(ways),
+        keep=False,
     )
     headers = exchange(header)
     if ways:
@@ -414,17 +427,22 @@
 
     row_grad, left_mine, own_right = call(
         rows_body,
+        "row_pass",
         [shape((rows + PAD, width), F32), shape((rows, width), BF16), shape((part, width), F32)],
         [pieces, headers, numbers, offset_factor, level],
     )
     move_mine, moves = call(
-        step_body, [shape((rows, width), BF16), shape((count, rows, width), BF16)], [row_grad] + other_narrow(row_grad)
+        step_body,
+        "step",
+        [shape((rows, width), BF16), shape((count, rows, width), BF16)],
+        [row_grad] + other_narrow(row_grad),
     )
     moves = exchange(moves)
 
     held = [pltpu.VMEM((2 * total, width), BF16), pltpu.VMEM((2 * total, part), F32), pltpu.VMEM((2 * total, part), BF16)]
     right_one, right_low, left_all = call(
         partial(cols_body, ways, False),
+        "col_pass_1",
         [shape((part, width), F32), shape((part, width), BF16), shape((total, width), BF16)],
         [headers, own_right, own_level, *blocks],
         held,
@@ -433,25 +451,30 @@
 
     change, outgoing = call(
         partial(cols_body, ways, True),
+        "col_pass_2",
         [shape((part, width), BF16), shape((count, rows + PAD, width), BF16)],
         [headers, right_one, own_level, *blocks, left_all, moves.reshape(total, width)],
         [*held, pltpu.VMEM((total, width), F32)],
     )
-    changes = gather_parts(change, passed_on=lambda far, outer: 2 * far == outer and outer > 2)
+    changes = gather_parts(change, passed_on=lambda far, outer: True)
     arrived = exchange(outgoing)
     summed = jnp.sum(arrived.astype(F32), 0)
 
     sparse = call(
         partial(sparse_body, gather_ways()),
+        "sparse_pass",
         shape(pieces.shape, BF16),
         [pieces, numbers, left_mine, move_mine, level, *lows],
+        keep=False,
     )
     new_offset, new_midpoint = call(
         partial(join_body, gather_ways()),
+        "join",
         [shape((cols, width), F32), shape((rows, width), F32)],
         [headers, moves, midpoint_factor, summed, *other_narrow(summed), *lows, *changes],
         [pltpu.VMEM((len(lows), cols // len(lows), width), F32), pltpu.SemaphoreType.DMA((len(lows),))],
         [ANY, VMEM],
+        keep=False,
     )
     return sparse, new_midpoint, new_offset
 

time: 108 us -> 96.7 us (0.90)
  Pallas kernels: 25.7 us -> 18.5 us
  starting transfers between devices: 51.6 us -> 49 us
  local copies, waits for them, and re-layouts: 3.98 us -> 1.43 us
  waiting for transfers between devices: 25 us -> 26.4 us
    pallas_call x7, Pallas kernels: 25.7 us -> 18.5 us  [call(): pl.pallas_call(body, in_specs=[VMEM] * len(arrays), out_specs=out_specs o...]
    ppermute x21, waiting for transfers between devices: 14.7 us -> 20.1 us  [shift(): return lax.ppermute(value, 'wide', pairs)]
    all_to_all x3, waiting for transfers between devices: 8.86 us -> 5.1 us  [exchange(): lax.all_to_all(blocks, 'wide', split_axis=0, concat_axis=0, tiled=True)]
    unnamed x62 -> x18, local copies, waits for them, and re-layouts: 3.98 us -> 1.43 us
    ppermute x21, starting transfers between devices: 36.1 us -> 34.5 us  [shift(): return lax.ppermute(value, 'wide', pairs)]
    all_to_all x3, starting transfers between devices: 15.4 us -> 14.3 us  [exchange(): lax.all_to_all(blocks, 'wide', split_axis=0, concat_axis=0, tiled=True)]
  transfers between devices with their start and end apart: 26 -> 26, of which waited for: 9 -> 10; matrix products, arithmetic and copies ran while one was open for 0% -> 0% of each run, Pallas kernels for 18% -> 15%
where the time goes in v3:
time: 96.7 us; the launch traced here: 96.1 us
  starting transfers between devices  49 us (51%)
  waiting for transfers between devices  26.4 us (27%)
  Pallas kernels  18.5 us (19%)
  local copies, waits for them, and re-layouts  1.43 us (1%)
    ppermute x21, starting transfers between devices, shift(): return lax.ppermute(value, 'wide', pairs)  34.5 us
    ppermute x21, waiting for transfers between devices, shift(): return lax.ppermute(value, 'wide', pairs)  20.1 us
    pallas_call x7, Pallas kernels, call(): pl.pallas_call(body, in_specs=[VMEM] * len(arrays), out_specs=out_specs o...  18.5 us
    all_to_all x3, starting transfers between devices, exchange(): lax.all_to_all(blocks, 'wide', split_axis=0, concat_axis=0, tiled=True)  14.3 us
    all_to_all x3, waiting for transfers between devices, exchange(): lax.all_to_all(blocks, 'wide', split_axis=0, concat_axis=0, tiled=True)  5.1 us
  transfers between devices with their start and end apart: 26, of which 10 were waited for; matrix products, arithmetic and copies ran while one was open for 0% of the time, Pallas kernels for 15%

profile of v3, /device:TPU:0, one launch (start us, length us, event | category | flops | bytes accessed | tf_op | source)
XLA Modules:
  0.0 96.1 jit_solution(5009407451431702843)
XLA Ops:
  0.6 2.3 %shard_map.94 = (bf16[8,72,128]{2,1,0:T(8,128)(2,1)}, bf16[8,128]{1,0:T(8,128)(2,1)}, bf16[2,64,512]{2,1,0:T(8,128)(2,1)}, bf16[2,64,512]{2,1,0:T(8,128)(2,1)}, ...) custom-call(f32[64,128]{1,0:T(8,128)} %rows_ref.3, ...), custom_call_target="tpu_custom_call" | custom-call | tf_op jit(solution)/shard_map/pallas_call | solution.py:327
  3.0 7.4 %all-to-all-start = ((bf16[8,72,128]{2,1,0:T(8,128)(2,1)}), bf16[8,72,128]{2,1,0:T(8,128)(2,1)S(1)}, u32[]{:S(2)}, u32[]{:S(2)}) async-start(bf16[8,72,128]{2,1,0:T(8,128)(2,1)} %get-tuple-element.26), calls=%async_computation | async-start | bytes 294912 | tf_op jit(solution)/shard_map/all_to_all | solution.py:344
  10.4 2.0 %collective-permute-start.1 = (bf16[2,64,512]{2,1,0:T(8,128)(2,1)}, bf16[2,64,512]{2,1,0:T(8,128)(2,1)S(1)}, u32[]{:S(2)}, u32[]{:S(2)}) collective-permute-start(bf16[2,64,512]{2,1,0:T(8,128)(2,1)} %get-tuple-element.31), channel_id=1, source_target_pairs={{0,2},{2,0},{4,6},{6,4},{8,10},{10,8},{12,14},{14,12},{1,3},{3,1},... | collective-permute-start | bytes 393224 | tf_op jit(solution)/shard_map/ppermute | solution.py:362
  12.4 3.3 %collective-permute-start.2 = (bf16[2,64,512]{2,1,0:T(8,128)(2,1)}, bf16[2,64,512]{2,1,0:T(8,128)(2,1)S(1)}, u32[]{:S(2)}, u32[]{:S(2)}) collective-permute-start(bf16[2,64,512]{2,1,0:T(8,128)(2,1)} %get-tuple-element.32), channel_id=1, source_target_pairs={{0,14},{2,12},{4,10},{6,8},{8,6},{10,4},{12,2},{14,0},{1,15},{3,13... | collective-permute-start | bytes 393224 | tf_op jit(solution)/shard_map/ppermute | solution.py:362
  15.7 5.1 %all-to-all-done.header_ref = bf16[8,72,128]{2,1,0:T(8,128)(2,1)S(1)} async-done(((bf16[8,72,128]{2,1,0:T(8,128)(2,1)}), bf16[8,72,128]{2,1,0:T(8,128)(2,1)S(1)}, u32[]{:S(2)}, u32[]{:S(2)}) %all-to-all-start) | async-done | bytes 147488 | tf_op jit(solution)/shard_map/all_to_all | solution.py:344
  22.2 4.3 %shard_map.95 = (f32[72,128]{1,0:T(8,128)S(1)}, bf16[64,128]{1,0:T(8,128)(2,1)S(1)}, f32[512,128]{1,0:T(8,128)S(1)}) custom-call(bf16[2,64,4096]{2,1,0:T(8,128)(2,1)} %piece_ref.3, bf16[8,72,128]{2,1,0:T(8,128)(2,1)S(1)} %all-to-all-done.header_ref, bf16[8,128]{1,0:T(8,128)(2,1)S(1)} %copy-done.3, f32[4096,128]{1,0:T(8,128)} %right_ref.1, f32[1,4096]{1,0:T(1,128)S(1)} %bitcast.6), custom_call_target="tpu_custom_call" | custom-call | tf_op jit(solution)/shard_map/pallas_call | solution.py:327
  26.6 1.2 %collective-permute-done.refs_0_ = f32[72,128]{1,0:T(8,128)S(1)} collective-permute-done((f32[72,128]{1,0:T(8,128)S(1)}, f32[72,128]{1,0:T(8,128)S(1)}, u32[]{:S(2)}, u32[]{:S(2)}) %collective-permute-start) | collective-permute-done | bytes 36896 | tf_op jit(solution)/shard_map/ppermute | solution.py:349
  27.8 0.8 shard_map.96
  28.6 3.4 %all-to-all-start.1 = ((bf16[8,64,128]{2,1,0:T(8,128)(2,1)}), bf16[8,64,128]{2,1,0:T(8,128)(2,1)S(1)}, u32[]{:S(2)}, u32[]{:S(2)}) async-start(bf16[8,64,128]{2,1,0:T(8,128)(2,1)} %get-tuple-element.40), calls=%async_computation.1 | async-start | bytes 262144 | tf_op jit(solution)/shard_map/all_to_all | solution.py:344
  32.0 3.7 %collective-permute-start.3 = (bf16[2,64,512]{2,1,0:T(8,128)(2,1)S(1)}, bf16[2,64,512]{2,1,0:T(8,128)(2,1)S(1)}, u32[]{:S(2)}, u32[]{:S(2)}) collective-permute-start(bf16[2,64,512]{2,1,0:T(8,128)(2,1)S(1)} %copy-done.8), channel_id=1, source_target_pairs={{0,12},{2,14},{4,8},{6,10},{8,4},{10,6},{12,0},{14,2},{1,13},{3,15... | collective-permute-start | bytes 393224 | tf_op jit(solution)/shard_map/ppermute | solution.py:362
  36.3 2.4 %collective-permute-start.5 = (bf16[2,64,512]{2,1,0:T(8,128)(2,1)S(1)}, bf16[2,64,512]{2,1,0:T(8,128)(2,1)S(1)}, u32[]{:S(2)}, u32[]{:S(2)}) collective-permute-start(bf16[2,64,512]{2,1,0:T(8,128)(2,1)S(1)} %copy-done.6), channel_id=1, source_target_pairs={{0,4},{2,6},{4,0},{6,2},{8,12},{10,14},{12,8},{14,10},{1,5},{3,7},... | collective-permute-start | bytes 393224 | tf_op jit(solution)/shard_map/ppermute | solution.py:362
  38.7 2.9 %collective-permute-start.7 = (bf16[2,64,512]{2,1,0:T(8,128)(2,1)S(1)}, bf16[2,64,512]{2,1,0:T(8,128)(2,1)S(1)}, u32[]{:S(2)}, u32[]{:S(2)}) collective-permute-start(bf16[2,64,512]{2,1,0:T(8,128)(2,1)S(1)} %copy-done.4), channel_id=1, source_target_pairs={{0,8},{2,10},{4,12},{6,14},{8,0},{10,2},{12,4},{14,6},{1,9},{3,11}... | collective-permute-start | bytes 393224 | tf_op jit(solution)/shard_map/ppermute | solution.py:362
  42.4 5.3 %collective-permute-done.4.refs_3_ = bf16[2,64,512]{2,1,0:T(8,128)(2,1)S(1)} collective-permute-done((bf16[2,64,512]{2,1,0:T(8,128)(2,1)S(1)}, bf16[2,64,512]{2,1,0:T(8,128)(2,1)S(1)}, u32[]{:S(2)}, u32[]{:S(2)}) %collective-permute-start.4) | collective-permute-done | bytes 131104 | tf_op jit(solution)/shard_map/ppermute | solution.py:362
  47.7 2.5 %collective-permute-done.5.refs_4_ = bf16[2,64,512]{2,1,0:T(8,128)(2,1)S(1)} collective-permute-done((bf16[2,64,512]{2,1,0:T(8,128)(2,1)S(1)}, bf16[2,64,512]{2,1,0:T(8,128)(2,1)S(1)}, u32[]{:S(2)}, u32[]{:S(2)}) %collective-permute-start.5) | collective-permute-done | bytes 131104 | tf_op jit(solution)/shard_map/ppermute | solution.py:362
  50.3 4.1 %collective-permute-done.6.refs_5_ = bf16[2,64,512]{2,1,0:T(8,128)(2,1)S(1)} collective-permute-done((bf16[2,64,512]{2,1,0:T(8,128)(2,1)S(1)}, bf16[2,64,512]{2,1,0:T(8,128)(2,1)S(1)}, u32[]{:S(2)}, u32[]{:S(2)}) %collective-permute-start.6) | collective-permute-done | bytes 131104 | tf_op jit(solution)/shard_map/ppermute | solution.py:362
  54.4 1.1 %collective-permute-done.7.refs_6_ = bf16[2,64,512]{2,1,0:T(8,128)(2,1)S(1)} collective-permute-done((bf16[2,64,512]{2,1,0:T(8,128)(2,1)S(1)}, bf16[2,64,512]{2,1,0:T(8,128)(2,1)S(1)}, u32[]{:S(2)}, u32[]{:S(2)}) %collective-permute-start.7) | collective-permute-done | bytes 131104 | tf_op jit(solution)/shard_map/ppermute | solution.py:362
  55.5 2.6 %shard_map.97 = (f32[512,128]{1,0:T(8,128)S(1)}, bf16[512,128]{1,0:T(8,128)(2,1)S(1)}, bf16[512,128]{1,0:T(8,128)(2,1)S(1)}) custom-call(bf16[8,72,128]{2,1,0:T(8,128)(2,1)S(1)} %all-to-all-done.header_ref, f32[512,128]{1,0:T(8,128)S(1)} %get-tuple-element.30.right_ref, f32[1,4096]{1,0:T(1,128)S(1)} %bitcast.7, ...), custom_call_target="tpu_custom_call" | custom-call | tf_op jit(solution)/shard_map/pallas_call | solution.py:327
  58.1 1.3 %collective-permute-start.13 = (bf16[512,128]{1,0:T(8,128)(2,1)S(1)}, bf16[512,128]{1,0:T(8,128)(2,1)S(1)}, u32[]{:S(2)}, u32[]{:S(2)}) collective-permute-start(bf16[512,128]{1,0:T(8,128)(2,1)S(1)} %get-tuple-element.39.refs_0_.refs_1_), channel_id=1, source_target_pairs={{0,12},{2,14},{4,8},{6,10},{8,4},{10,6},{12,0},{14,2},{1,13},{3,15... | collective-permute-start | bytes 393224 | tf_op jit(solution)/shard_map/ppermute | solution.py:362
  59.5 3.1 %collective-permute-start.9 = (bf16[512,128]{1,0:T(8,128)(2,1)S(1)}, bf16[512,128]{1,0:T(8,128)(2,1)S(1)}, u32[]{:S(2)}, u32[]{:S(2)}) collective-permute-start(bf16[512,128]{1,0:T(8,128)(2,1)S(1)} %get-tuple-element.39.refs_0_.refs_1_), channel_id=1, source_target_pairs={{0,4},{2,6},{4,0},{6,2},{8,12},{10,14},{12,8},{14,10},{1,5},{3,7},... | collective-permute-start | bytes 393224 | tf_op jit(solution)/shard_map/ppermute | solution.py:362
  62.6 1.5 %collective-permute-start.8 = (bf16[512,128]{1,0:T(8,128)(2,1)S(1)}, bf16[512,128]{1,0:T(8,128)(2,1)S(1)}, u32[]{:S(2)}, u32[]{:S(2)}) collective-permute-start(bf16[512,128]{1,0:T(8,128)(2,1)S(1)} %get-tuple-element.39.refs_0_.refs_1_), channel_id=1, source_target_pairs={{0,2},{2,0},{4,6},{6,4},{8,10},{10,8},{12,14},{14,12},{1,3},{3,1},... | collective-permute-start | bytes 393224 | tf_op jit(solution)/shard_map/ppermute | solution.py:362
  64.0 3.1 %shard_map.99 = (bf16[512,128]{1,0:T(8,128)(2,1)S(1)}, bf16[8,72,128]{2,1,0:T(8,128)(2,1)}) custom-call(bf16[8,72,128]{2,1,0:T(8,128)(2,1)S(1)} %all-to-all-done.header_ref, f32[512,128]{1,0:T(8,128)S(1)} %get-tuple-element.41.right_ref, f32[1,4096]{1,0:T(1,128)S(1)} %bitcast.8, bf16[2,64,512]{2,1,0:T(8,128)(2,1)S(1)} %collective-permute-done.1.refs_0_, ...), custom_call_target="tpu_custom_call" | custom-call | tf_op jit(solution)/shard_map/pallas_call | solution.py:327
  67.2 3.5 %all-to-all-start.2 = ((bf16[8,72,128]{2,1,0:T(8,128)(2,1)}), bf16[8,72,128]{2,1,0:T(8,128)(2,1)S(1)}, u32[]{:S(2)}, u32[]{:S(2)}) async-start(bf16[8,72,128]{2,1,0:T(8,128)(2,1)} %get-tuple-element.43), calls=%async_computation.2 | async-start | bytes 294912 | tf_op jit(solution)/shard_map/all_to_all | solution.py:344
  70.7 1.9 %collective-permute-start.14 = (bf16[512,128]{1,0:T(8,128)(2,1)S(1)}, bf16[512,128]{1,0:T(8,128)(2,1)S(1)}, u32[]{:S(2)}, u32[]{:S(2)}) collective-permute-start(bf16[512,128]{1,0:T(8,128)(2,1)S(1)} %collective-permute-done.13.refs_6_.refs_7_), channel_id=1, source_target_pairs={{0,2},{2,0},{4,6},{6,4},{8,10},{10,8},{12,14},{14,12},{1,3},{3,1},... | collective-permute-start | bytes 393224 | tf_op jit(solution)/shard_map/ppermute | solution.py:362
  72.8 3.7 %collective-permute-start.21 = (bf16[512,128]{1,0:T(8,128)(2,1)S(1)}, bf16[512,128]{1,0:T(8,128)(2,1)S(1)}, u32[]{:S(2)}, u32[]{:S(2)}) collective-permute-start(bf16[512,128]{1,0:T(8,128)(2,1)S(1)} %get-tuple-element.44.refs_9_), channel_id=1, source_target_pairs={{0,12},{2,14},{4,8},{6,10},{8,4},{10,6},{12,0},{14,2},{1,13},{3,15... | collective-permute-start | bytes 393224 | tf_op jit(solution)/shard_map/ppermute | solution.py:362
  77.2 1.8 %collective-permute-start.10 = (bf16[512,128]{1,0:T(8,128)(2,1)S(1)}, bf16[512,128]{1,0:T(8,128)(2,1)S(1)}, u32[]{:S(2)}, u32[]{:S(2)}) collective-permute-start(bf16[512,128]{1,0:T(8,128)(2,1)S(1)} %collective-permute-done.9.refs_2_.refs_3_), channel_id=1, source_target_pairs={{0,2},{2,0},{4,6},{6,4},{8,10},{10,8},{12,14},{14,12},{1,3},{3,1},... | collective-permute-start | bytes 393224 | tf_op jit(solution)/shard_map/ppermute | solution.py:362
  79.5 2.0 %collective-permute-start.16 = (bf16[512,128]{1,0:T(8,128)(2,1)S(1)}, bf16[512,128]{1,0:T(8,128)(2,1)S(1)}, u32[]{:S(2)}, u32[]{:S(2)}) collective-permute-start(bf16[512,128]{1,0:T(8,128)(2,1)S(1)} %get-tuple-element.44.refs_9_), channel_id=1, source_target_pairs={{0,2},{2,0},{4,6},{6,4},{8,10},{10,8},{12,14},{14,12},{1,3},{3,1},... | collective-permute-start | bytes 393224 | tf_op jit(solution)/shard_map/ppermute | solution.py:362
  81.5 1.4 %collective-permute-start.22 = (bf16[512,128]{1,0:T(8,128)(2,1)S(1)}, bf16[512,128]{1,0:T(8,128)(2,1)S(1)}, u32[]{:S(2)}, u32[]{:S(2)}) collective-permute-start(bf16[512,128]{1,0:T(8,128)(2,1)S(1)} %collective-permute-done.21.refs_15_), channel_id=1, source_target_pairs={{0,2},{2,0},{4,6},{6,4},{8,10},{10,8},{12,14},{14,12},{1,3},{3,1},... | collective-permute-start | bytes 393224 | tf_op jit(solution)/shard_map/ppermute | solution.py:362
  82.8 4.6 %collective-permute-done.19.refs_13_ = bf16[512,128]{1,0:T(8,128)(2,1)S(1)} collective-permute-done((bf16[512,128]{1,0:T(8,128)(2,1)S(1)}, bf16[512,128]{1,0:T(8,128)(2,1)S(1)}, u32[]{:S(2)}, u32[]{:S(2)}) %collective-permute-start.19) | collective-permute-done | bytes 131104 | tf_op jit(solution)/shard_map/ppermute | solution.py:362
  87.4 1.3 %collective-permute-start.20 = (bf16[512,128]{1,0:T(8,128)(2,1)S(1)}, bf16[512,128]{1,0:T(8,128)(2,1)S(1)}, u32[]{:S(2)}, u32[]{:S(2)}) collective-permute-start(bf16[512,128]{1,0:T(8,128)(2,1)S(1)} %collective-permute-done.19.refs_13_), channel_id=1, source_target_pairs={{0,2},{2,0},{4,6},{6,4},{8,10},{10,8},{12,14},{14,12},{1,3},{3,1},... | collective-permute-start | bytes 393224 | tf_op jit(solution)/shard_map/ppermute | solution.py:362
  89.5 3.2 %shard_map.98 = bf16[2,64,4096]{2,1,0:T(8,128)(2,1)} custom-call(bf16[2,64,4096]{2,1,0:T(8,128)(2,1)} %piece_ref.3, bf16[8,128]{1,0:T(8,128)(2,1)S(1)} %copy-done.3, bf16[64,128]{1,0:T(8,128)(2,1)S(1)} %get-tuple-element.27.left_ref, bf16[64,128]{1,0:T(8,128)(2,1)S(1)} %get-tuple-element.29.move_ref, f32[1,4096]{1,0:T(1,128)S(1)} %bitcast.9, ...), custom_call_target="tpu_custom_call" | custom-call | tf_op jit(solution)/shard_map/pallas_call | solution.py:327
  92.7 1.2 %collective-permute-done.18.refs_12_ = bf16[512,128]{1,0:T(8,128)(2,1)S(1)} collective-permute-done((bf16[512,128]{1,0:T(8,128)(2,1)S(1)}, bf16[512,128]{1,0:T(8,128)(2,1)S(1)}, u32[]{:S(2)}, u32[]{:S(2)}) %collective-permute-start.18) | collective-permute-done | bytes 131104 | tf_op jit(solution)/shard_map/ppermute | solution.py:362
  94.0 2.1 %shard_map.100 = (f32[4096,128]{1,0:T(8,128)}, f32[64,128]{1,0:T(8,128)}) custom-call(bf16[8,72,128]{2,1,0:T(8,128)(2,1)S(1)} %all-to-all-done.header_ref, bf16[8,64,128]{2,1,0:T(8,128)(2,1)S(1)} %all-to-all-done.1.move_ref, f32[64,128]{1,0:T(8,128)S(1)} %copy-done.2, f32[72,128]{1,0:T(8,128)S(1)} %convert_reduce_fusion.mine_ref, ...), custom_call_target="tpu_custom_call" | custom-call | tf_op jit(solution)/shard_map/pallas_call | solution.py:327
  (46 shorter events, 5.0 us)
Async XLA Ops:
  3.0 35.8 %copy-start.4 = (bf16[2,64,512]{2,1,0:T(8,128)(2,1)S(1)}, bf16[2,64,512]{2,1,0:T(8,128)(2,1)}, u32[]{:S(2)}) copy-start(bf16[2,64,512]{2,1,0:T(8,128)(2,1)} %get-tuple-element.37) | copy-start | bytes 393220
  3.0 52.5 %copy-start = (bf16[2,64,512]{2,1,0:T(8,128)(2,1)S(1)}, bf16[2,64,512]{2,1,0:T(8,128)(2,1)}, u32[]{:S(2)}) copy-start(bf16[2,64,512]{2,1,0:T(8,128)(2,1)} %get-tuple-element.38.refs_7_) | copy-start | bytes 393220
  3.0 17.8 %all-to-all-start = ((bf16[8,72,128]{2,1,0:T(8,128)(2,1)}), bf16[8,72,128]{2,1,0:T(8,128)(2,1)S(1)}, u32[]{:S(2)}, u32[]{:S(2)}) async-start(bf16[8,72,128]{2,1,0:T(8,128)(2,1)} %get-tuple-element.26), calls=%async_computation | async-start | bytes 294912 | tf_op jit(solution)/shard_map/all_to_all | solution.py:344
  10.4 28.3 %collective-permute-start.1 = (bf16[2,64,512]{2,1,0:T(8,128)(2,1)}, bf16[2,64,512]{2,1,0:T(8,128)(2,1)S(1)}, u32[]{:S(2)}, u32[]{:S(2)}) collective-permute-start(bf16[2,64,512]{2,1,0:T(8,128)(2,1)} %get-tuple-element.31), channel_id=1, source_target_pairs={{0,2},{2,0},{4,6},{6,4},{8,10},{10,8},{12,14},{14,12},{1,3},{3,1},... | collective-permute-start | bytes 393224 | tf_op jit(solution)/shard_map/ppermute | solution.py:362
  12.4 26.3 %collective-permute-start.2 = (bf16[2,64,512]{2,1,0:T(8,128)(2,1)}, bf16[2,64,512]{2,1,0:T(8,128)(2,1)S(1)}, u32[]{:S(2)}, u32[]{:S(2)}) collective-permute-start(bf16[2,64,512]{2,1,0:T(8,128)(2,1)} %get-tuple-element.32), channel_id=1, source_target_pairs={{0,14},{2,12},{4,10},{6,8},{8,6},{10,4},{12,2},{14,0},{1,15},{3,13... | collective-permute-start | bytes 393224 | tf_op jit(solution)/shard_map/ppermute | solution.py:362
  22.2 13.6 %copy-start.7 = (bf16[2,64,512]{2,1,0:T(8,128)(2,1)S(1)}, bf16[2,64,512]{2,1,0:T(8,128)(2,1)}, u32[]{:S(2)}) copy-start(bf16[2,64,512]{2,1,0:T(8,128)(2,1)} %get-tuple-element.34) | copy-start | bytes 393220
  22.2 14.1 %copy-start.6 = (bf16[2,64,512]{2,1,0:T(8,128)(2,1)S(1)}, bf16[2,64,512]{2,1,0:T(8,128)(2,1)}, u32[]{:S(2)}) copy-start(bf16[2,64,512]{2,1,0:T(8,128)(2,1)} %get-tuple-element.35) | copy-start | bytes 393220
  22.2 16.5 %copy-start.5 = (bf16[2,64,512]{2,1,0:T(8,128)(2,1)S(1)}, bf16[2,64,512]{2,1,0:T(8,128)(2,1)}, u32[]{:S(2)}) copy-start(bf16[2,64,512]{2,1,0:T(8,128)(2,1)} %get-tuple-element.36) | copy-start | bytes 393220
  26.5 1.3 %collective-permute-start = (f32[72,128]{1,0:T(8,128)S(1)}, f32[72,128]{1,0:T(8,128)S(1)}, u32[]{:S(2)}, u32[]{:S(2)}) collective-permute-start(f32[72,128]{1,0:T(8,128)S(1)} %get-tuple-element.28.mine_ref), channel_id=1, source_target_pairs={{0,1},{1,0},{2,3},{3,2},{4,5},{5,4},{6,7},{7,6},{8,9},{9,8},{10,11... | collective-permute-start | bytes 110600 | tf_op jit(solution)/shard_map/ppermute | solution.py:349
  28.6 35.4 %all-to-all-start.1 = ((bf16[8,64,128]{2,1,0:T(8,128)(2,1)}), bf16[8,64,128]{2,1,0:T(8,128)(2,1)S(1)}, u32[]{:S(2)}, u32[]{:S(2)}) async-start(bf16[8,64,128]{2,1,0:T(8,128)(2,1)} %get-tuple-element.40), calls=%async_computation.1 | async-start | bytes 262144 | tf_op jit(solution)/shard_map/all_to_all | solution.py:344
  32.0 10.4 %collective-permute-start.3 = (bf16[2,64,512]{2,1,0:T(8,128)(2,1)S(1)}, bf16[2,64,512]{2,1,0:T(8,128)(2,1)S(1)}, u32[]{:S(2)}, u32[]{:S(2)}) collective-permute-start(bf16[2,64,512]{2,1,0:T(8,128)(2,1)S(1)} %copy-done.8), channel_id=1, source_target_pairs={{0,12},{2,14},{4,8},{6,10},{8,4},{10,6},{12,0},{14,2},{1,13},{3,15... | collective-permute-start | bytes 393224 | tf_op jit(solution)/shard_map/ppermute | solution.py:362
  35.8 11.9 %collective-permute-start.4 = (bf16[2,64,512]{2,1,0:T(8,128)(2,1)S(1)}, bf16[2,64,512]{2,1,0:T(8,128)(2,1)S(1)}, u32[]{:S(2)}, u32[]{:S(2)}) collective-permute-start(bf16[2,64,512]{2,1,0:T(8,128)(2,1)S(1)} %copy-done.7), channel_id=1, source_target_pairs={{0,6},{2,4},{4,2},{6,0},{8,14},{10,12},{12,10},{14,8},{1,7},{3,5},... | collective-permute-start | bytes 393224 | tf_op jit(solution)/shard_map/ppermute | solution.py:362
  36.3 13.9 %collective-permute-start.5 = (bf16[2,64,512]{2,1,0:T(8,128)(2,1)S(1)}, bf16[2,64,512]{2,1,0:T(8,128)(2,1)S(1)}, u32[]{:S(2)}, u32[]{:S(2)}) collective-permute-start(bf16[2,64,512]{2,1,0:T(8,128)(2,1)S(1)} %copy-done.6), channel_id=1, source_target_pairs={{0,4},{2,6},{4,0},{6,2},{8,12},{10,14},{12,8},{14,10},{1,5},{3,7},... | collective-permute-start | bytes 393224 | tf_op jit(solution)/shard_map/ppermute | solution.py:362
  38.7 15.7 %collective-permute-start.6 = (bf16[2,64,512]{2,1,0:T(8,128)(2,1)S(1)}, bf16[2,64,512]{2,1,0:T(8,128)(2,1)S(1)}, u32[]{:S(2)}, u32[]{:S(2)}) collective-permute-start(bf16[2,64,512]{2,1,0:T(8,128)(2,1)S(1)} %copy-done.5), channel_id=1, source_target_pairs={{0,10},{2,8},{4,14},{6,12},{8,2},{10,0},{12,6},{14,4},{1,11},{3,9}... | collective-permute-start | bytes 393224 | tf_op jit(solution)/shard_map/ppermute | solution.py:362
  38.7 16.8 %collective-permute-start.7 = (bf16[2,64,512]{2,1,0:T(8,128)(2,1)S(1)}, bf16[2,64,512]{2,1,0:T(8,128)(2,1)S(1)}, u32[]{:S(2)}, u32[]{:S(2)}) collective-permute-start(bf16[2,64,512]{2,1,0:T(8,128)(2,1)S(1)} %copy-done.4), channel_id=1, source_target_pairs={{0,8},{2,10},{4,12},{6,14},{8,0},{10,2},{12,4},{14,6},{1,9},{3,11}... | collective-permute-start | bytes 393224 | tf_op jit(solution)/shard_map/ppermute | solution.py:362
  58.1 12.6 %collective-permute-start.13 = (bf16[512,128]{1,0:T(8,128)(2,1)S(1)}, bf16[512,128]{1,0:T(8,128)(2,1)S(1)}, u32[]{:S(2)}, u32[]{:S(2)}) collective-permute-start(bf16[512,128]{1,0:T(8,128)(2,1)S(1)} %get-tuple-element.39.refs_0_.refs_1_), channel_id=1, source_target_pairs={{0,12},{2,14},{4,8},{6,10},{8,4},{10,6},{12,0},{14,2},{1,13},{3,15... | collective-permute-start | bytes 393224 | tf_op jit(solution)/shard_map/ppermute | solution.py:362
  59.5 13.2 %collective-permute-start.11 = (bf16[512,128]{1,0:T(8,128)(2,1)S(1)}, bf16[512,128]{1,0:T(8,128)(2,1)S(1)}, u32[]{:S(2)}, u32[]{:S(2)}) collective-permute-start(bf16[512,128]{1,0:T(8,128)(2,1)S(1)} %get-tuple-element.39.refs_0_.refs_1_), channel_id=1, source_target_pairs={{0,8},{2,10},{4,12},{6,14},{8,0},{10,2},{12,4},{14,6},{1,9},{3,11}... | collective-permute-start | bytes 393224 | tf_op jit(solution)/shard_map/ppermute | solution.py:362
  59.5 17.0 %collective-permute-start.9 = (bf16[512,128]{1,0:T(8,128)(2,1)S(1)}, bf16[512,128]{1,0:T(8,128)(2,1)S(1)}, u32[]{:S(2)}, u32[]{:S(2)}) collective-permute-start(bf16[512,128]{1,0:T(8,128)(2,1)S(1)} %get-tuple-element.39.refs_0_.refs_1_), channel_id=1, source_target_pairs={{0,4},{2,6},{4,0},{6,2},{8,12},{10,14},{12,8},{14,10},{1,5},{3,7},... | collective-permute-start | bytes 393224 | tf_op jit(solution)/shard_map/ppermute | solution.py:362
  62.6 13.9 %collective-permute-start.8 = (bf16[512,128]{1,0:T(8,128)(2,1)S(1)}, bf16[512,128]{1,0:T(8,128)(2,1)S(1)}, u32[]{:S(2)}, u32[]{:S(2)}) collective-permute-start(bf16[512,128]{1,0:T(8,128)(2,1)S(1)} %get-tuple-element.39.refs_0_.refs_1_), channel_id=1, source_target_pairs={{0,2},{2,0},{4,6},{6,4},{8,10},{10,8},{12,14},{14,12},{1,3},{3,1},... | collective-permute-start | bytes 393224 | tf_op jit(solution)/shard_map/ppermute | solution.py:362
  67.2 26.8 %copy-start.2 = (f32[64,128]{1,0:T(8,128)S(1)}, f32[64,128]{1,0:T(8,128)}, u32[]{:S(2)}) copy-start(f32[64,128]{1,0:T(8,128)} %rows_ref.3) | copy-start | bytes 98308
  67.2 22.3 %all-to-all-start.2 = ((bf16[8,72,128]{2,1,0:T(8,128)(2,1)}), bf16[8,72,128]{2,1,0:T(8,128)(2,1)S(1)}, u32[]{:S(2)}, u32[]{:S(2)}) async-start(bf16[8,72,128]{2,1,0:T(8,128)(2,1)} %get-tuple-element.43), calls=%async_computation.2 | async-start | bytes 294912 | tf_op jit(solution)/shard_map/all_to_all | solution.py:344
  70.7 6.5 %collective-permute-start.14 = (bf16[512,128]{1,0:T(8,128)(2,1)S(1)}, bf16[512,128]{1,0:T(8,128)(2,1)S(1)}, u32[]{:S(2)}, u32[]{:S(2)}) collective-permute-start(bf16[512,128]{1,0:T(8,128)(2,1)S(1)} %collective-permute-done.13.refs_6_.refs_7_), channel_id=1, source_target_pairs={{0,2},{2,0},{4,6},{6,4},{8,10},{10,8},{12,14},{14,12},{1,3},{3,1},... | collective-permute-start | bytes 393224 | tf_op jit(solution)/shard_map/ppermute | solution.py:362
  72.6 6.9 %collective-permute-start.12 = (bf16[512,128]{1,0:T(8,128)(2,1)S(1)}, bf16[512,128]{1,0:T(8,128)(2,1)S(1)}, u32[]{:S(2)}, u32[]{:S(2)}) collective-permute-start(bf16[512,128]{1,0:T(8,128)(2,1)S(1)} %collective-permute-done.11.refs_4_.refs_5_), channel_id=1, source_target_pairs={{0,2},{2,0},{4,6},{6,4},{8,10},{10,8},{12,14},{14,12},{1,3},{3,1},... | collective-permute-start | bytes 393224 | tf_op jit(solution)/shard_map/ppermute | solution.py:362
  72.8 8.7 %collective-permute-start.21 = (bf16[512,128]{1,0:T(8,128)(2,1)S(1)}, bf16[512,128]{1,0:T(8,128)(2,1)S(1)}, u32[]{:S(2)}, u32[]{:S(2)}) collective-permute-start(bf16[512,128]{1,0:T(8,128)(2,1)S(1)} %get-tuple-element.44.refs_9_), channel_id=1, source_target_pairs={{0,12},{2,14},{4,8},{6,10},{8,4},{10,6},{12,0},{14,2},{1,13},{3,15... | collective-permute-start | bytes 393224 | tf_op jit(solution)/shard_map/ppermute | solution.py:362
  76.5 10.9 %collective-permute-start.19 = (bf16[512,128]{1,0:T(8,128)(2,1)S(1)}, bf16[512,128]{1,0:T(8,128)(2,1)S(1)}, u32[]{:S(2)}, u32[]{:S(2)}) collective-permute-start(bf16[512,128]{1,0:T(8,128)(2,1)S(1)} %get-tuple-element.44.refs_9_), channel_id=1, source_target_pairs={{0,8},{2,10},{4,12},{6,14},{8,0},{10,2},{12,4},{14,6},{1,9},{3,11}... | collective-permute-start | bytes 393224 | tf_op jit(solution)/shard_map/ppermute | solution.py:362
  76.5 12.2 %collective-permute-start.17 = (bf16[512,128]{1,0:T(8,128)(2,1)S(1)}, bf16[512,128]{1,0:T(8,128)(2,1)S(1)}, u32[]{:S(2)}, u32[]{:S(2)}) collective-permute-start(bf16[512,128]{1,0:T(8,128)(2,1)S(1)} %get-tuple-element.44.refs_9_), channel_id=1, source_target_pairs={{0,4},{2,6},{4,0},{6,2},{8,12},{10,14},{12,8},{14,10},{1,5},{3,7},... | collective-permute-start | bytes 393224 | tf_op jit(solution)/shard_map/ppermute | solution.py:362
  77.2 12.3 %collective-permute-start.10 = (bf16[512,128]{1,0:T(8,128)(2,1)S(1)}, bf16[512,128]{1,0:T(8,128)(2,1)S(1)}, u32[]{:S(2)}, u32[]{:S(2)}) collective-permute-start(bf16[512,128]{1,0:T(8,128)(2,1)S(1)} %collective-permute-done.9.refs_2_.refs_3_), channel_id=1, source_target_pairs={{0,2},{2,0},{4,6},{6,4},{8,10},{10,8},{12,14},{14,12},{1,3},{3,1},... | collective-permute-start | bytes 393224 | tf_op jit(solution)/shard_map/ppermute | solution.py:362
  79.5 13.3 %collective-permute-start.16 = (bf16[512,128]{1,0:T(8,128)(2,1)S(1)}, bf16[512,128]{1,0:T(8,128)(2,1)S(1)}, u32[]{:S(2)}, u32[]{:S(2)}) collective-permute-start(bf16[512,128]{1,0:T(8,128)(2,1)S(1)} %get-tuple-element.44.refs_9_), channel_id=1, source_target_pairs={{0,2},{2,0},{4,6},{6,4},{8,10},{10,8},{12,14},{14,12},{1,3},{3,1},... | collective-permute-start | bytes 393224 | tf_op jit(solution)/shard_map/ppermute | solution.py:362
  81.5 11.3 %collective-permute-start.22 = (bf16[512,128]{1,0:T(8,128)(2,1)S(1)}, bf16[512,128]{1,0:T(8,128)(2,1)S(1)}, u32[]{:S(2)}, u32[]{:S(2)}) collective-permute-start(bf16[512,128]{1,0:T(8,128)(2,1)S(1)} %collective-permute-done.21.refs_15_), channel_id=1, source_target_pairs={{0,2},{2,0},{4,6},{6,4},{8,10},{10,8},{12,14},{14,12},{1,3},{3,1},... | collective-permute-start | bytes 393224 | tf_op jit(solution)/shard_map/ppermute | solution.py:362
  87.4 5.3 %collective-permute-start.20 = (bf16[512,128]{1,0:T(8,128)(2,1)S(1)}, bf16[512,128]{1,0:T(8,128)(2,1)S(1)}, u32[]{:S(2)}, u32[]{:S(2)}) collective-permute-start(bf16[512,128]{1,0:T(8,128)(2,1)S(1)} %collective-permute-done.19.refs_13_), channel_id=1, source_target_pairs={{0,2},{2,0},{4,6},{6,4},{8,10},{10,8},{12,14},{14,12},{1,3},{3,1},... | collective-permute-start | bytes 393224 | tf_op jit(solution)/shard_map/ppermute | solution.py:362
  88.7 5.3 %collective-permute-start.18 = (bf16[512,128]{1,0:T(8,128)(2,1)S(1)}, bf16[512,128]{1,0:T(8,128)(2,1)S(1)}, u32[]{:S(2)}, u32[]{:S(2)}) collective-permute-start(bf16[512,128]{1,0:T(8,128)(2,1)S(1)} %collective-permute-done.17.refs_11_), channel_id=1, source_target_pairs={{0,2},{2,0},{4,6},{6,4},{8,10},{10,8},{12,14},{14,12},{1,3},{3,1},... | collective-permute-start | bytes 393224 | tf_op jit(solution)/shard_map/ppermute | solution.py:362
  89.5 4.5 %collective-permute-start.15 = (f32[72,128]{1,0:T(8,128)S(1)}, f32[72,128]{1,0:T(8,128)S(1)}, u32[]{:S(2)}, u32[]{:S(2)}) collective-permute-start(f32[72,128]{1,0:T(8,128)S(1)} %convert_reduce_fusion.mine_ref), channel_id=1, source_target_pairs={{0,1},{1,0},{2,3},{3,2},{4,5},{5,4},{6,7},{7,6},{8,9},{9,8},{10,11... | collective-permute-start | bytes 110600 | tf_op jit(solution)/shard_map/ppermute | solution.py:349
  (3 other events, 11.2 us)

commit v4 on v3

--- a/solution.py
+++ b/solution.py
@@ -350,8 +350,7 @@
 
 
 def small_wide():
-    count = lax.axis_size("wide")
-    return count % NEAR == 0 and count <= 4 * NEAR
+    return lax.axis_size("wide") in (NEAR, 2 * NEAR, 4 * NEAR)
 
 
 def shift(value, far, near):
@@ -382,20 +381,27 @@
     return tuple((far, near) for far in range(lax.axis_size("wide") // NEAR) for near in range(NEAR))
 
 
-def gather_parts(block, passed_on):
+def gather_parts(block):
     count = lax.axis_size("wide")
     ways = gather_ways()
     if not ways:
         return [exchange(jnp.broadcast_to(block[None], (count,) + block.shape)).reshape(-1, block.shape[1])]
     outer = count // NEAR
     held = {(0, 0): block}
-    for far in sorted(range(1, outer), key=lambda far: -min(far, outer - far)):
+    far = 1
+    while far < outer:
         held[far, 0] = shift(block, far, 0)
-    for far in range(1, outer):
-        if not passed_on(far, outer):
-            held |= {(far, near): shift(block, far, near) for near in range(1, NEAR)}
-    held |= {(0, near): shift(block, 0, near) for near in range(1, NEAR)}
-    return [held[way] if way in held else shift(held[way[0], 0], 0, way[1]) for way in ways]
+        far *= 2
+    held[0, 1] = shift(block, 0, 1)
+    if outer == 4:
+        held[3, 0] = shift(held[2, 0], 1, 0)
+    for way in ways:
+        if way not in held and way[0] < 3:
+            held[way] = shift(held[way[0], 0], 0, way[1])
+    for way in ways:
+        if way not in held:
+            held[way] = shift(held[2, 1], 1, 0)
+    return [held[way] for way in ways]
 
 
 def program(pieces, destination, first_offset, valid_length, midpoint_factor, offset_factor, threshold):
@@ -421,7 +427,9 @@
     )
     headers = exchange(header)
     if ways:
-        blocks = [block if way == (0, 0) else shift(block, *way) for way, block in zip(ways, parts)]
+        blocks = []
+        for way, block in zip(ways, parts):
+            blocks.append(block if way == (0, 0) else shift(block, *way))
     else:
         blocks = [exchange(jnp.transpose(pieces.reshape(2, rows, count, part), (2, 0, 1, 3)))]
 
@@ -447,7 +455,7 @@
         [headers, own_right, own_level, *blocks],
         held,
     )
-    lows = gather_parts(right_low, passed_on=lambda far, outer: True)
+    lows = gather_parts(right_low)
 
     change, outgoing = call(
         partial(cols_body, ways, True),
@@ -456,7 +464,7 @@
         [headers, right_one, own_level, *blocks, left_all, moves.reshape(total, width)],
         [*held, pltpu.VMEM((total, width), F32)],
     )
-    changes = gather_parts(change, passed_on=lambda far, outer: True)
+    changes = gather_parts(change)
     arrived = exchange(outgoing)
     summed = jnp.sum(arrived.astype(F32), 0)
 

time: 96.7 us -> 91.7 us (0.948)
  starting transfers between devices: 49 us -> 45.4 us
  waiting for transfers between devices: 26.4 us -> 25 us
    ppermute x21, starting transfers between devices: 34.5 us -> 31.1 us  [shift(): return lax.ppermute(value, 'wide', pairs)]
    ppermute x21, waiting for transfers between devices: 20.1 us -> 18.7 us  [shift(): return lax.ppermute(value, 'wide', pairs)]
  transfers between devices with their start and end apart: 26 -> 26, of which waited for: 10 -> 14; matrix products, arithmetic and copies ran while one was open for 0% -> 0% of each run, Pallas kernels for 15% -> 15%
where the time goes in v4:
time: 91.7 us; the launch traced here: 91.1 us
  starting transfers between devices  45.4 us (50%)
  waiting for transfers between devices  25 us (27%)
  Pallas kernels  18.5 us (20%)
  local copies, waits for them, and re-layouts  1.43 us (2%)
    ppermute x21, starting transfers between devices, shift(): return lax.ppermute(value, 'wide', pairs)  31.1 us
    ppermute x21, waiting for transfers between devices, shift(): return lax.ppermute(value, 'wide', pairs)  18.7 us
    pallas_call x7, Pallas kernels, call(): pl.pallas_call(body, in_specs=[VMEM] * len(arrays), out_specs=out_specs o...  18.5 us
    all_to_all x3, starting transfers between devices, exchange(): lax.all_to_all(blocks, 'wide', split_axis=0, concat_axis=0, tiled=True)  14.2 us
    all_to_all x3, waiting for transfers between devices, exchange(): lax.all_to_all(blocks, 'wide', split_axis=0, concat_axis=0, tiled=True)  5.1 us
  transfers between devices with their start and end apart: 26, of which 14 were waited for; matrix products, arithmetic and copies ran while one was open for 0% of the time, Pallas kernels for 15%

profile of v4, /device:TPU:0, one launch (start us, length us, event | category | flops | bytes accessed | tf_op | source)
XLA Modules:
  0.0 91.1 jit_solution(5146497146630132121)
XLA Ops:
  0.6 2.3 %shard_map.94 = (bf16[8,72,128]{2,1,0:T(8,128)(2,1)}, bf16[8,128]{1,0:T(8,128)(2,1)}, bf16[2,64,512]{2,1,0:T(8,128)(2,1)}, bf16[2,64,512]{2,1,0:T(8,128)(2,1)}, ...) custom-call(f32[64,128]{1,0:T(8,128)} %rows_ref.3, ...), custom_call_target="tpu_custom_call" | custom-call | tf_op jit(solution)/shard_map/pallas_call | solution.py:327
  3.0 7.4 %all-to-all-start = ((bf16[8,72,128]{2,1,0:T(8,128)(2,1)}), bf16[8,72,128]{2,1,0:T(8,128)(2,1)S(1)}, u32[]{:S(2)}, u32[]{:S(2)}) async-start(bf16[8,72,128]{2,1,0:T(8,128)(2,1)} %get-tuple-element.26), calls=%async_computation | async-start | bytes 294912 | tf_op jit(solution)/shard_map/all_to_all | solution.py:344
  10.4 2.0 %collective-permute-start.1 = (bf16[2,64,512]{2,1,0:T(8,128)(2,1)}, bf16[2,64,512]{2,1,0:T(8,128)(2,1)S(1)}, u32[]{:S(2)}, u32[]{:S(2)}) collective-permute-start(bf16[2,64,512]{2,1,0:T(8,128)(2,1)} %get-tuple-element.31), channel_id=1, source_target_pairs={{0,2},{2,0},{4,6},{6,4},{8,10},{10,8},{12,14},{14,12},{1,3},{3,1},... | collective-permute-start | bytes 393224 | tf_op jit(solution)/shard_map/ppermute | solution.py:361
  12.4 3.3 %collective-permute-start.2 = (bf16[2,64,512]{2,1,0:T(8,128)(2,1)}, bf16[2,64,512]{2,1,0:T(8,128)(2,1)S(1)}, u32[]{:S(2)}, u32[]{:S(2)}) collective-permute-start(bf16[2,64,512]{2,1,0:T(8,128)(2,1)} %get-tuple-element.32), channel_id=1, source_target_pairs={{0,14},{2,12},{4,10},{6,8},{8,6},{10,4},{12,2},{14,0},{1,15},{3,13... | collective-permute-start | bytes 393224 | tf_op jit(solution)/shard_map/ppermute | solution.py:361
  15.7 5.1 %all-to-all-done.header_ref = bf16[8,72,128]{2,1,0:T(8,128)(2,1)S(1)} async-done(((bf16[8,72,128]{2,1,0:T(8,128)(2,1)}), bf16[8,72,128]{2,1,0:T(8,128)(2,1)S(1)}, u32[]{:S(2)}, u32[]{:S(2)}) %all-to-all-start) | async-done | bytes 147488 | tf_op jit(solution)/shard_map/all_to_all | solution.py:344
  22.2 4.3 %shard_map.95 = (f32[72,128]{1,0:T(8,128)S(1)}, bf16[64,128]{1,0:T(8,128)(2,1)S(1)}, f32[512,128]{1,0:T(8,128)S(1)}) custom-call(bf16[2,64,4096]{2,1,0:T(8,128)(2,1)} %piece_ref.3, bf16[8,72,128]{2,1,0:T(8,128)(2,1)S(1)} %all-to-all-done.header_ref, bf16[8,128]{1,0:T(8,128)(2,1)S(1)} %copy-done.3, f32[4096,128]{1,0:T(8,128)} %right_ref.1, f32[1,4096]{1,0:T(1,128)S(1)} %bitcast.6), custom_call_target="tpu_custom_call" | custom-call | tf_op jit(solution)/shard_map/pallas_call | solution.py:327
  26.6 1.2 %collective-permute-done.refs_0_ = f32[72,128]{1,0:T(8,128)S(1)} collective-permute-done((f32[72,128]{1,0:T(8,128)S(1)}, f32[72,128]{1,0:T(8,128)S(1)}, u32[]{:S(2)}, u32[]{:S(2)}) %collective-permute-start) | collective-permute-done | bytes 36896 | tf_op jit(solution)/shard_map/ppermute | solution.py:349
  28.6 3.4 %all-to-all-start.1 = ((bf16[8,64,128]{2,1,0:T(8,128)(2,1)}), bf16[8,64,128]{2,1,0:T(8,128)(2,1)S(1)}, u32[]{:S(2)}, u32[]{:S(2)}) async-start(bf16[8,64,128]{2,1,0:T(8,128)(2,1)} %get-tuple-element.40), calls=%async_computation.1 | async-start | bytes 262144 | tf_op jit(solution)/shard_map/all_to_all | solution.py:344
  32.0 3.7 %collective-permute-start.3 = (bf16[2,64,512]{2,1,0:T(8,128)(2,1)S(1)}, bf16[2,64,512]{2,1,0:T(8,128)(2,1)S(1)}, u32[]{:S(2)}, u32[]{:S(2)}) collective-permute-start(bf16[2,64,512]{2,1,0:T(8,128)(2,1)S(1)} %copy-done.8), channel_id=1, source_target_pairs={{0,12},{2,14},{4,8},{6,10},{8,4},{10,6},{12,0},{14,2},{1,13},{3,15... | collective-permute-start | bytes 393224 | tf_op jit(solution)/shard_map/ppermute | solution.py:361
  36.3 2.4 %collective-permute-start.5 = (bf16[2,64,512]{2,1,0:T(8,128)(2,1)S(1)}, bf16[2,64,512]{2,1,0:T(8,128)(2,1)S(1)}, u32[]{:S(2)}, u32[]{:S(2)}) collective-permute-start(bf16[2,64,512]{2,1,0:T(8,128)(2,1)S(1)} %copy-done.6), channel_id=1, source_target_pairs={{0,4},{2,6},{4,0},{6,2},{8,12},{10,14},{12,8},{14,10},{1,5},{3,7},... | collective-permute-start | bytes 393224 | tf_op jit(solution)/shard_map/ppermute | solution.py:361
  38.7 2.9 %collective-permute-start.7 = (bf16[2,64,512]{2,1,0:T(8,128)(2,1)S(1)}, bf16[2,64,512]{2,1,0:T(8,128)(2,1)S(1)}, u32[]{:S(2)}, u32[]{:S(2)}) collective-permute-start(bf16[2,64,512]{2,1,0:T(8,128)(2,1)S(1)} %copy-done.4), channel_id=1, source_target_pairs={{0,8},{2,10},{4,12},{6,14},{8,0},{10,2},{12,4},{14,6},{1,9},{3,11}... | collective-permute-start | bytes 393224 | tf_op jit(solution)/shard_map/ppermute | solution.py:361
  42.4 5.3 %collective-permute-done.4.refs_3_ = bf16[2,64,512]{2,1,0:T(8,128)(2,1)S(1)} collective-permute-done((bf16[2,64,512]{2,1,0:T(8,128)(2,1)S(1)}, bf16[2,64,512]{2,1,0:T(8,128)(2,1)S(1)}, u32[]{:S(2)}, u32[]{:S(2)}) %collective-permute-start.4) | collective-permute-done | bytes 131104 | tf_op jit(solution)/shard_map/ppermute | solution.py:361
  47.7 2.5 %collective-permute-done.5.refs_4_ = bf16[2,64,512]{2,1,0:T(8,128)(2,1)S(1)} collective-permute-done((bf16[2,64,512]{2,1,0:T(8,128)(2,1)S(1)}, bf16[2,64,512]{2,1,0:T(8,128)(2,1)S(1)}, u32[]{:S(2)}, u32[]{:S(2)}) %collective-permute-start.5) | collective-permute-done | bytes 131104 | tf_op jit(solution)/shard_map/ppermute | solution.py:361
  50.3 4.1 %collective-permute-done.6.refs_5_ = bf16[2,64,512]{2,1,0:T(8,128)(2,1)S(1)} collective-permute-done((bf16[2,64,512]{2,1,0:T(8,128)(2,1)S(1)}, bf16[2,64,512]{2,1,0:T(8,128)(2,1)S(1)}, u32[]{:S(2)}, u32[]{:S(2)}) %collective-permute-start.6) | collective-permute-done | bytes 131104 | tf_op jit(solution)/shard_map/ppermute | solution.py:361
  54.4 1.1 %collective-permute-done.7.refs_6_ = bf16[2,64,512]{2,1,0:T(8,128)(2,1)S(1)} collective-permute-done((bf16[2,64,512]{2,1,0:T(8,128)(2,1)S(1)}, bf16[2,64,512]{2,1,0:T(8,128)(2,1)S(1)}, u32[]{:S(2)}, u32[]{:S(2)}) %collective-permute-start.7) | collective-permute-done | bytes 131104 | tf_op jit(solution)/shard_map/ppermute | solution.py:361
  55.5 2.6 %shard_map.97 = (f32[512,128]{1,0:T(8,128)S(1)}, bf16[512,128]{1,0:T(8,128)(2,1)S(1)}, bf16[512,128]{1,0:T(8,128)(2,1)S(1)}) custom-call(bf16[8,72,128]{2,1,0:T(8,128)(2,1)S(1)} %all-to-all-done.header_ref, f32[512,128]{1,0:T(8,128)S(1)} %get-tuple-element.30.right_ref, f32[1,4096]{1,0:T(1,128)S(1)} %bitcast.7, ...), custom_call_target="tpu_custom_call" | custom-call | tf_op jit(solution)/shard_map/pallas_call | solution.py:327
  58.2 1.8 %collective-permute-start.9 = (bf16[512,128]{1,0:T(8,128)(2,1)S(1)}, bf16[512,128]{1,0:T(8,128)(2,1)S(1)}, u32[]{:S(2)}, u32[]{:S(2)}) collective-permute-start(bf16[512,128]{1,0:T(8,128)(2,1)S(1)} %get-tuple-element.39.refs_0_.refs_1_), channel_id=1, source_target_pairs={{0,4},{2,6},{4,0},{6,2},{8,12},{10,14},{12,8},{14,10},{1,5},{3,7},... | collective-permute-start | bytes 393224 | tf_op jit(solution)/shard_map/ppermute | solution.py:361
  60.0 1.6 %collective-permute-start.8 = (bf16[512,128]{1,0:T(8,128)(2,1)S(1)}, bf16[512,128]{1,0:T(8,128)(2,1)S(1)}, u32[]{:S(2)}, u32[]{:S(2)}) collective-permute-start(bf16[512,128]{1,0:T(8,128)(2,1)S(1)} %get-tuple-element.39.refs_0_.refs_1_), channel_id=1, source_target_pairs={{0,2},{2,0},{4,6},{6,4},{8,10},{10,8},{12,14},{14,12},{1,3},{3,1},... | collective-permute-start | bytes 393224 | tf_op jit(solution)/shard_map/ppermute | solution.py:361
  61.7 3.1 %shard_map.99 = (bf16[512,128]{1,0:T(8,128)(2,1)S(1)}, bf16[8,72,128]{2,1,0:T(8,128)(2,1)}) custom-call(bf16[8,72,128]{2,1,0:T(8,128)(2,1)S(1)} %all-to-all-done.header_ref, f32[512,128]{1,0:T(8,128)S(1)} %get-tuple-element.41.right_ref, f32[1,4096]{1,0:T(1,128)S(1)} %bitcast.8, bf16[2,64,512]{2,1,0:T(8,128)(2,1)S(1)} %collective-permute-done.1.refs_0_, ...), custom_call_target="tpu_custom_call" | custom-call | tf_op jit(solution)/shard_map/pallas_call | solution.py:327
  65.7 3.4 %all-to-all-start.2 = ((bf16[8,72,128]{2,1,0:T(8,128)(2,1)}), bf16[8,72,128]{2,1,0:T(8,128)(2,1)S(1)}, u32[]{:S(2)}, u32[]{:S(2)}) async-start(bf16[8,72,128]{2,1,0:T(8,128)(2,1)} %get-tuple-element.43), calls=%async_computation.2 | async-start | bytes 294912 | tf_op jit(solution)/shard_map/all_to_all | solution.py:344
  69.1 1.9 %collective-permute-start.12 = (bf16[512,128]{1,0:T(8,128)(2,1)S(1)}, bf16[512,128]{1,0:T(8,128)(2,1)S(1)}, u32[]{:S(2)}, u32[]{:S(2)}) collective-permute-start(bf16[512,128]{1,0:T(8,128)(2,1)S(1)} %collective-permute-done.11.refs_4_.refs_5_), channel_id=1, source_target_pairs={{0,2},{2,0},{4,6},{6,4},{8,10},{10,8},{12,14},{14,12},{1,3},{3,1},... | collective-permute-start | bytes 393224 | tf_op jit(solution)/shard_map/ppermute | solution.py:361
  71.0 1.5 %collective-permute-start.13 = (bf16[512,128]{1,0:T(8,128)(2,1)S(1)}, bf16[512,128]{1,0:T(8,128)(2,1)S(1)}, u32[]{:S(2)}, u32[]{:S(2)}) collective-permute-start(bf16[512,128]{1,0:T(8,128)(2,1)S(1)} %collective-permute-done.11.refs_4_.refs_5_), channel_id=1, source_target_pairs={{0,4},{2,6},{4,0},{6,2},{8,12},{10,14},{12,8},{14,10},{1,5},{3,7},... | collective-permute-start | bytes 393224 | tf_op jit(solution)/shard_map/ppermute | solution.py:361
  73.8 1.3 %collective-permute-start.20 = (bf16[512,128]{1,0:T(8,128)(2,1)S(1)}, bf16[512,128]{1,0:T(8,128)(2,1)S(1)}, u32[]{:S(2)}, u32[]{:S(2)}) collective-permute-start(bf16[512,128]{1,0:T(8,128)(2,1)S(1)} %collective-permute-done.19.refs_13_), channel_id=1, source_target_pairs={{0,2},{2,0},{4,6},{6,4},{8,10},{10,8},{12,14},{14,12},{1,3},{3,1},... | collective-permute-start | bytes 393224 | tf_op jit(solution)/shard_map/ppermute | solution.py:361
  75.1 1.7 %collective-permute-done.12.refs_5_.refs_6_ = bf16[512,128]{1,0:T(8,128)(2,1)S(1)} collective-permute-done((bf16[512,128]{1,0:T(8,128)(2,1)S(1)}, bf16[512,128]{1,0:T(8,128)(2,1)S(1)}, u32[]{:S(2)}, u32[]{:S(2)}) %collective-permute-start.12) | collective-permute-done | bytes 131104 | tf_op jit(solution)/shard_map/ppermute | solution.py:361
  76.8 1.3 %collective-permute-start.14 = (bf16[512,128]{1,0:T(8,128)(2,1)S(1)}, bf16[512,128]{1,0:T(8,128)(2,1)S(1)}, u32[]{:S(2)}, u32[]{:S(2)}) collective-permute-start(bf16[512,128]{1,0:T(8,128)(2,1)S(1)} %collective-permute-done.12.refs_5_.refs_6_), channel_id=1, source_target_pairs={{0,4},{2,6},{4,0},{6,2},{8,12},{10,14},{12,8},{14,10},{1,5},{3,7},... | collective-permute-start | bytes 393224 | tf_op jit(solution)/shard_map/ppermute | solution.py:361
  78.2 1.0 %collective-permute-start.16 = (bf16[512,128]{1,0:T(8,128)(2,1)S(1)}, bf16[512,128]{1,0:T(8,128)(2,1)S(1)}, u32[]{:S(2)}, u32[]{:S(2)}) collective-permute-start(bf16[512,128]{1,0:T(8,128)(2,1)S(1)} %get-tuple-element.44.refs_9_), channel_id=1, source_target_pairs={{0,2},{2,0},{4,6},{6,4},{8,10},{10,8},{12,14},{14,12},{1,3},{3,1},... | collective-permute-start | bytes 393224 | tf_op jit(solution)/shard_map/ppermute | solution.py:361
  79.5 1.4 %collective-permute-start.21 = (bf16[512,128]{1,0:T(8,128)(2,1)S(1)}, bf16[512,128]{1,0:T(8,128)(2,1)S(1)}, u32[]{:S(2)}, u32[]{:S(2)}) collective-permute-start(bf16[512,128]{1,0:T(8,128)(2,1)S(1)} %collective-permute-done.19.refs_13_), channel_id=1, source_target_pairs={{0,4},{2,6},{4,0},{6,2},{8,12},{10,14},{12,8},{14,10},{1,5},{3,7},... | collective-permute-start | bytes 393224 | tf_op jit(solution)/shard_map/ppermute | solution.py:361
  81.0 1.0 %collective-permute-start.18 = (bf16[512,128]{1,0:T(8,128)(2,1)S(1)}, bf16[512,128]{1,0:T(8,128)(2,1)S(1)}, u32[]{:S(2)}, u32[]{:S(2)}) collective-permute-start(bf16[512,128]{1,0:T(8,128)(2,1)S(1)} %collective-permute-done.17.refs_11_), channel_id=1, source_target_pairs={{0,2},{2,0},{4,6},{6,4},{8,10},{10,8},{12,14},{14,12},{1,3},{3,1},... | collective-permute-start | bytes 393224 | tf_op jit(solution)/shard_map/ppermute | solution.py:361
  82.0 1.7 %collective-permute-start.22 = (bf16[512,128]{1,0:T(8,128)(2,1)S(1)}, bf16[512,128]{1,0:T(8,128)(2,1)S(1)}, u32[]{:S(2)}, u32[]{:S(2)}) collective-permute-start(bf16[512,128]{1,0:T(8,128)(2,1)S(1)} %collective-permute-done.20.refs_14_), channel_id=1, source_target_pairs={{0,4},{2,6},{4,0},{6,2},{8,12},{10,14},{12,8},{14,10},{1,5},{3,7},... | collective-permute-start | bytes 393224 | tf_op jit(solution)/shard_map/ppermute | solution.py:361
  83.8 3.2 %shard_map.98 = bf16[2,64,4096]{2,1,0:T(8,128)(2,1)} custom-call(bf16[2,64,4096]{2,1,0:T(8,128)(2,1)} %piece_ref.3, bf16[8,128]{1,0:T(8,128)(2,1)S(1)} %copy-done.3, bf16[64,128]{1,0:T(8,128)(2,1)S(1)} %get-tuple-element.27.left_ref, bf16[64,128]{1,0:T(8,128)(2,1)S(1)} %get-tuple-element.29.move_ref, f32[1,4096]{1,0:T(1,128)S(1)} %bitcast.9, ...), custom_call_target="tpu_custom_call" | custom-call | tf_op jit(solution)/shard_map/pallas_call | solution.py:327
  87.1 1.9 %collective-permute-done.22.refs_16_ = bf16[512,128]{1,0:T(8,128)(2,1)S(1)} collective-permute-done((bf16[512,128]{1,0:T(8,128)(2,1)S(1)}, bf16[512,128]{1,0:T(8,128)(2,1)S(1)}, u32[]{:S(2)}, u32[]{:S(2)}) %collective-permute-start.22) | collective-permute-done | bytes 131104 | tf_op jit(solution)/shard_map/ppermute | solution.py:361
  89.0 2.1 %shard_map.100 = (f32[4096,128]{1,0:T(8,128)}, f32[64,128]{1,0:T(8,128)}) custom-call(bf16[8,72,128]{2,1,0:T(8,128)(2,1)S(1)} %all-to-all-done.header_ref, bf16[8,64,128]{2,1,0:T(8,128)(2,1)S(1)} %all-to-all-done.1.move_ref, f32[64,128]{1,0:T(8,128)S(1)} %copy-done.2, f32[72,128]{1,0:T(8,128)S(1)} %convert_reduce_fusion.mine_ref, ...), custom_call_target="tpu_custom_call" | custom-call | tf_op jit(solution)/shard_map/pallas_call | solution.py:327
  (46 shorter events, 6.6 us)
Async XLA Ops:
  3.0 35.8 %copy-start.4 = (bf16[2,64,512]{2,1,0:T(8,128)(2,1)S(1)}, bf16[2,64,512]{2,1,0:T(8,128)(2,1)}, u32[]{:S(2)}) copy-start(bf16[2,64,512]{2,1,0:T(8,128)(2,1)} %get-tuple-element.37) | copy-start | bytes 393220
  3.0 52.5 %copy-start = (bf16[2,64,512]{2,1,0:T(8,128)(2,1)S(1)}, bf16[2,64,512]{2,1,0:T(8,128)(2,1)}, u32[]{:S(2)}) copy-start(bf16[2,64,512]{2,1,0:T(8,128)(2,1)} %get-tuple-element.38.refs_7_) | copy-start | bytes 393220
  3.0 17.8 %all-to-all-start = ((bf16[8,72,128]{2,1,0:T(8,128)(2,1)}), bf16[8,72,128]{2,1,0:T(8,128)(2,1)S(1)}, u32[]{:S(2)}, u32[]{:S(2)}) async-start(bf16[8,72,128]{2,1,0:T(8,128)(2,1)} %get-tuple-element.26), calls=%async_computation | async-start | bytes 294912 | tf_op jit(solution)/shard_map/all_to_all | solution.py:344
  10.4 28.3 %collective-permute-start.1 = (bf16[2,64,512]{2,1,0:T(8,128)(2,1)}, bf16[2,64,512]{2,1,0:T(8,128)(2,1)S(1)}, u32[]{:S(2)}, u32[]{:S(2)}) collective-permute-start(bf16[2,64,512]{2,1,0:T(8,128)(2,1)} %get-tuple-element.31), channel_id=1, source_target_pairs={{0,2},{2,0},{4,6},{6,4},{8,10},{10,8},{12,14},{14,12},{1,3},{3,1},... | collective-permute-start | bytes 393224 | tf_op jit(solution)/shard_map/ppermute | solution.py:361
  12.4 26.3 %collective-permute-start.2 = (bf16[2,64,512]{2,1,0:T(8,128)(2,1)}, bf16[2,64,512]{2,1,0:T(8,128)(2,1)S(1)}, u32[]{:S(2)}, u32[]{:S(2)}) collective-permute-start(bf16[2,64,512]{2,1,0:T(8,128)(2,1)} %get-tuple-element.32), channel_id=1, source_target_pairs={{0,14},{2,12},{4,10},{6,8},{8,6},{10,4},{12,2},{14,0},{1,15},{3,13... | collective-permute-start | bytes 393224 | tf_op jit(solution)/shard_map/ppermute | solution.py:361
  22.2 13.6 %copy-start.7 = (bf16[2,64,512]{2,1,0:T(8,128)(2,1)S(1)}, bf16[2,64,512]{2,1,0:T(8,128)(2,1)}, u32[]{:S(2)}) copy-start(bf16[2,64,512]{2,1,0:T(8,128)(2,1)} %get-tuple-element.34) | copy-start | bytes 393220
  22.2 14.1 %copy-start.6 = (bf16[2,64,512]{2,1,0:T(8,128)(2,1)S(1)}, bf16[2,64,512]{2,1,0:T(8,128)(2,1)}, u32[]{:S(2)}) copy-start(bf16[2,64,512]{2,1,0:T(8,128)(2,1)} %get-tuple-element.35) | copy-start | bytes 393220
  22.2 16.5 %copy-start.5 = (bf16[2,64,512]{2,1,0:T(8,128)(2,1)S(1)}, bf16[2,64,512]{2,1,0:T(8,128)(2,1)}, u32[]{:S(2)}) copy-start(bf16[2,64,512]{2,1,0:T(8,128)(2,1)} %get-tuple-element.36) | copy-start | bytes 393220
  26.5 1.3 %collective-permute-start = (f32[72,128]{1,0:T(8,128)S(1)}, f32[72,128]{1,0:T(8,128)S(1)}, u32[]{:S(2)}, u32[]{:S(2)}) collective-permute-start(f32[72,128]{1,0:T(8,128)S(1)} %get-tuple-element.28.mine_ref), channel_id=1, source_target_pairs={{0,1},{1,0},{2,3},{3,2},{4,5},{5,4},{6,7},{7,6},{8,9},{9,8},{10,11... | collective-permute-start | bytes 110600 | tf_op jit(solution)/shard_map/ppermute | solution.py:349
  28.6 33.0 %all-to-all-start.1 = ((bf16[8,64,128]{2,1,0:T(8,128)(2,1)}), bf16[8,64,128]{2,1,0:T(8,128)(2,1)S(1)}, u32[]{:S(2)}, u32[]{:S(2)}) async-start(bf16[8,64,128]{2,1,0:T(8,128)(2,1)} %get-tuple-element.40), calls=%async_computation.1 | async-start | bytes 262144 | tf_op jit(solution)/shard_map/all_to_all | solution.py:344
  32.0 10.4 %collective-permute-start.3 = (bf16[2,64,512]{2,1,0:T(8,128)(2,1)S(1)}, bf16[2,64,512]{2,1,0:T(8,128)(2,1)S(1)}, u32[]{:S(2)}, u32[]{:S(2)}) collective-permute-start(bf16[2,64,512]{2,1,0:T(8,128)(2,1)S(1)} %copy-done.8), channel_id=1, source_target_pairs={{0,12},{2,14},{4,8},{6,10},{8,4},{10,6},{12,0},{14,2},{1,13},{3,15... | collective-permute-start | bytes 393224 | tf_op jit(solution)/shard_map/ppermute | solution.py:361
  35.8 11.9 %collective-permute-start.4 = (bf16[2,64,512]{2,1,0:T(8,128)(2,1)S(1)}, bf16[2,64,512]{2,1,0:T(8,128)(2,1)S(1)}, u32[]{:S(2)}, u32[]{:S(2)}) collective-permute-start(bf16[2,64,512]{2,1,0:T(8,128)(2,1)S(1)} %copy-done.7), channel_id=1, source_target_pairs={{0,6},{2,4},{4,2},{6,0},{8,14},{10,12},{12,10},{14,8},{1,7},{3,5},... | collective-permute-start | bytes 393224 | tf_op jit(solution)/shard_map/ppermute | solution.py:361
  36.3 13.9 %collective-permute-start.5 = (bf16[2,64,512]{2,1,0:T(8,128)(2,1)S(1)}, bf16[2,64,512]{2,1,0:T(8,128)(2,1)S(1)}, u32[]{:S(2)}, u32[]{:S(2)}) collective-permute-start(bf16[2,64,512]{2,1,0:T(8,128)(2,1)S(1)} %copy-done.6), channel_id=1, source_target_pairs={{0,4},{2,6},{4,0},{6,2},{8,12},{10,14},{12,8},{14,10},{1,5},{3,7},... | collective-permute-start | bytes 393224 | tf_op jit(solution)/shard_map/ppermute | solution.py:361
  38.7 15.7 %collective-permute-start.6 = (bf16[2,64,512]{2,1,0:T(8,128)(2,1)S(1)}, bf16[2,64,512]{2,1,0:T(8,128)(2,1)S(1)}, u32[]{:S(2)}, u32[]{:S(2)}) collective-permute-start(bf16[2,64,512]{2,1,0:T(8,128)(2,1)S(1)} %copy-done.5), channel_id=1, source_target_pairs={{0,10},{2,8},{4,14},{6,12},{8,2},{10,0},{12,6},{14,4},{1,11},{3,9}... | collective-permute-start | bytes 393224 | tf_op jit(solution)/shard_map/ppermute | solution.py:361
  38.7 16.8 %collective-permute-start.7 = (bf16[2,64,512]{2,1,0:T(8,128)(2,1)S(1)}, bf16[2,64,512]{2,1,0:T(8,128)(2,1)S(1)}, u32[]{:S(2)}, u32[]{:S(2)}) collective-permute-start(bf16[2,64,512]{2,1,0:T(8,128)(2,1)S(1)} %copy-done.4), channel_id=1, source_target_pairs={{0,8},{2,10},{4,12},{6,14},{8,0},{10,2},{12,4},{14,6},{1,9},{3,11}... | collective-permute-start | bytes 393224 | tf_op jit(solution)/shard_map/ppermute | solution.py:361
  58.1 11.0 %collective-permute-start.11 = (bf16[512,128]{1,0:T(8,128)(2,1)S(1)}, bf16[512,128]{1,0:T(8,128)(2,1)S(1)}, u32[]{:S(2)}, u32[]{:S(2)}) collective-permute-start(bf16[512,128]{1,0:T(8,128)(2,1)S(1)} %get-tuple-element.39.refs_0_.refs_1_), channel_id=1, source_target_pairs={{0,8},{2,10},{4,12},{6,14},{8,0},{10,2},{12,4},{14,6},{1,9},{3,11}... | collective-permute-start | bytes 393224 | tf_op jit(solution)/shard_map/ppermute | solution.py:361
  58.2 14.3 %collective-permute-start.9 = (bf16[512,128]{1,0:T(8,128)(2,1)S(1)}, bf16[512,128]{1,0:T(8,128)(2,1)S(1)}, u32[]{:S(2)}, u32[]{:S(2)}) collective-permute-start(bf16[512,128]{1,0:T(8,128)(2,1)S(1)} %get-tuple-element.39.refs_0_.refs_1_), channel_id=1, source_target_pairs={{0,4},{2,6},{4,0},{6,2},{8,12},{10,14},{12,8},{14,10},{1,5},{3,7},... | collective-permute-start | bytes 393224 | tf_op jit(solution)/shard_map/ppermute | solution.py:361
  60.0 13.2 %collective-permute-start.8 = (bf16[512,128]{1,0:T(8,128)(2,1)S(1)}, bf16[512,128]{1,0:T(8,128)(2,1)S(1)}, u32[]{:S(2)}, u32[]{:S(2)}) collective-permute-start(bf16[512,128]{1,0:T(8,128)(2,1)S(1)} %get-tuple-element.39.refs_0_.refs_1_), channel_id=1, source_target_pairs={{0,2},{2,0},{4,6},{6,4},{8,10},{10,8},{12,14},{14,12},{1,3},{3,1},... | collective-permute-start | bytes 393224 | tf_op jit(solution)/shard_map/ppermute | solution.py:361
  64.8 24.2 %copy-start.2 = (f32[64,128]{1,0:T(8,128)S(1)}, f32[64,128]{1,0:T(8,128)}, u32[]{:S(2)}) copy-start(f32[64,128]{1,0:T(8,128)} %rows_ref.3) | copy-start | bytes 98308
  64.8 9.0 %collective-permute-start.19 = (bf16[512,128]{1,0:T(8,128)(2,1)S(1)}, bf16[512,128]{1,0:T(8,128)(2,1)S(1)}, u32[]{:S(2)}, u32[]{:S(2)}) collective-permute-start(bf16[512,128]{1,0:T(8,128)(2,1)S(1)} %get-tuple-element.44.refs_9_), channel_id=1, source_target_pairs={{0,8},{2,10},{4,12},{6,14},{8,0},{10,2},{12,4},{14,6},{1,9},{3,11}... | collective-permute-start | bytes 393224 | tf_op jit(solution)/shard_map/ppermute | solution.py:361
  65.7 18.0 %all-to-all-start.2 = ((bf16[8,72,128]{2,1,0:T(8,128)(2,1)}), bf16[8,72,128]{2,1,0:T(8,128)(2,1)S(1)}, u32[]{:S(2)}, u32[]{:S(2)}) async-start(bf16[8,72,128]{2,1,0:T(8,128)(2,1)} %get-tuple-element.43), calls=%async_computation.2 | async-start | bytes 294912 | tf_op jit(solution)/shard_map/all_to_all | solution.py:344
  69.1 7.7 %collective-permute-start.12 = (bf16[512,128]{1,0:T(8,128)(2,1)S(1)}, bf16[512,128]{1,0:T(8,128)(2,1)S(1)}, u32[]{:S(2)}, u32[]{:S(2)}) collective-permute-start(bf16[512,128]{1,0:T(8,128)(2,1)S(1)} %collective-permute-done.11.refs_4_.refs_5_), channel_id=1, source_target_pairs={{0,2},{2,0},{4,6},{6,4},{8,10},{10,8},{12,14},{14,12},{1,3},{3,1},... | collective-permute-start | bytes 393224 | tf_op jit(solution)/shard_map/ppermute | solution.py:361
  71.0 7.2 %collective-permute-start.13 = (bf16[512,128]{1,0:T(8,128)(2,1)S(1)}, bf16[512,128]{1,0:T(8,128)(2,1)S(1)}, u32[]{:S(2)}, u32[]{:S(2)}) collective-permute-start(bf16[512,128]{1,0:T(8,128)(2,1)S(1)} %collective-permute-done.11.refs_4_.refs_5_), channel_id=1, source_target_pairs={{0,4},{2,6},{4,0},{6,2},{8,12},{10,14},{12,8},{14,10},{1,5},{3,7},... | collective-permute-start | bytes 393224 | tf_op jit(solution)/shard_map/ppermute | solution.py:361
  72.5 7.0 %collective-permute-start.10 = (bf16[512,128]{1,0:T(8,128)(2,1)S(1)}, bf16[512,128]{1,0:T(8,128)(2,1)S(1)}, u32[]{:S(2)}, u32[]{:S(2)}) collective-permute-start(bf16[512,128]{1,0:T(8,128)(2,1)S(1)} %collective-permute-done.9.refs_2_.refs_3_), channel_id=1, source_target_pairs={{0,2},{2,0},{4,6},{6,4},{8,10},{10,8},{12,14},{14,12},{1,3},{3,1},... | collective-permute-start | bytes 393224 | tf_op jit(solution)/shard_map/ppermute | solution.py:361
  73.2 7.8 %collective-permute-start.17 = (bf16[512,128]{1,0:T(8,128)(2,1)S(1)}, bf16[512,128]{1,0:T(8,128)(2,1)S(1)}, u32[]{:S(2)}, u32[]{:S(2)}) collective-permute-start(bf16[512,128]{1,0:T(8,128)(2,1)S(1)} %get-tuple-element.44.refs_9_), channel_id=1, source_target_pairs={{0,4},{2,6},{4,0},{6,2},{8,12},{10,14},{12,8},{14,10},{1,5},{3,7},... | collective-permute-start | bytes 393224 | tf_op jit(solution)/shard_map/ppermute | solution.py:361
  73.8 8.1 %collective-permute-start.20 = (bf16[512,128]{1,0:T(8,128)(2,1)S(1)}, bf16[512,128]{1,0:T(8,128)(2,1)S(1)}, u32[]{:S(2)}, u32[]{:S(2)}) collective-permute-start(bf16[512,128]{1,0:T(8,128)(2,1)S(1)} %collective-permute-done.19.refs_13_), channel_id=1, source_target_pairs={{0,2},{2,0},{4,6},{6,4},{8,10},{10,8},{12,14},{14,12},{1,3},{3,1},... | collective-permute-start | bytes 393224 | tf_op jit(solution)/shard_map/ppermute | solution.py:361
  76.8 7.0 %collective-permute-start.14 = (bf16[512,128]{1,0:T(8,128)(2,1)S(1)}, bf16[512,128]{1,0:T(8,128)(2,1)S(1)}, u32[]{:S(2)}, u32[]{:S(2)}) collective-permute-start(bf16[512,128]{1,0:T(8,128)(2,1)S(1)} %collective-permute-done.12.refs_5_.refs_6_), channel_id=1, source_target_pairs={{0,4},{2,6},{4,0},{6,2},{8,12},{10,14},{12,8},{14,10},{1,5},{3,7},... | collective-permute-start | bytes 393224 | tf_op jit(solution)/shard_map/ppermute | solution.py:361
  78.2 8.8 %collective-permute-start.16 = (bf16[512,128]{1,0:T(8,128)(2,1)S(1)}, bf16[512,128]{1,0:T(8,128)(2,1)S(1)}, u32[]{:S(2)}, u32[]{:S(2)}) collective-permute-start(bf16[512,128]{1,0:T(8,128)(2,1)S(1)} %get-tuple-element.44.refs_9_), channel_id=1, source_target_pairs={{0,2},{2,0},{4,6},{6,4},{8,10},{10,8},{12,14},{14,12},{1,3},{3,1},... | collective-permute-start | bytes 393224 | tf_op jit(solution)/shard_map/ppermute | solution.py:361
  79.5 7.5 %collective-permute-start.21 = (bf16[512,128]{1,0:T(8,128)(2,1)S(1)}, bf16[512,128]{1,0:T(8,128)(2,1)S(1)}, u32[]{:S(2)}, u32[]{:S(2)}) collective-permute-start(bf16[512,128]{1,0:T(8,128)(2,1)S(1)} %collective-permute-done.19.refs_13_), channel_id=1, source_target_pairs={{0,4},{2,6},{4,0},{6,2},{8,12},{10,14},{12,8},{14,10},{1,5},{3,7},... | collective-permute-start | bytes 393224 | tf_op jit(solution)/shard_map/ppermute | solution.py:361
  81.0 6.0 %collective-permute-start.18 = (bf16[512,128]{1,0:T(8,128)(2,1)S(1)}, bf16[512,128]{1,0:T(8,128)(2,1)S(1)}, u32[]{:S(2)}, u32[]{:S(2)}) collective-permute-start(bf16[512,128]{1,0:T(8,128)(2,1)S(1)} %collective-permute-done.17.refs_11_), channel_id=1, source_target_pairs={{0,2},{2,0},{4,6},{6,4},{8,10},{10,8},{12,14},{14,12},{1,3},{3,1},... | collective-permute-start | bytes 393224 | tf_op jit(solution)/shard_map/ppermute | solution.py:361
  82.0 7.0 %collective-permute-start.22 = (bf16[512,128]{1,0:T(8,128)(2,1)S(1)}, bf16[512,128]{1,0:T(8,128)(2,1)S(1)}, u32[]{:S(2)}, u32[]{:S(2)}) collective-permute-start(bf16[512,128]{1,0:T(8,128)(2,1)S(1)} %collective-permute-done.20.refs_14_), channel_id=1, source_target_pairs={{0,4},{2,6},{4,0},{6,2},{8,12},{10,14},{12,8},{14,10},{1,5},{3,7},... | collective-permute-start | bytes 393224 | tf_op jit(solution)/shard_map/ppermute | solution.py:361
  83.8 3.2 %collective-permute-start.15 = (f32[72,128]{1,0:T(8,128)S(1)}, f32[72,128]{1,0:T(8,128)S(1)}, u32[]{:S(2)}, u32[]{:S(2)}) collective-permute-start(f32[72,128]{1,0:T(8,128)S(1)} %convert_reduce_fusion.mine_ref), channel_id=1, source_target_pairs={{0,1},{1,0},{2,3},{3,2},{4,5},{5,4},{6,7},{7,6},{8,9},{9,8},{10,11... | collective-permute-start | bytes 110600 | tf_op jit(solution)/shard_map/ppermute | solution.py:349
  (3 other events, 11.2 us)

commit v5 on v4

--- a/solution.py
+++ b/solution.py
@@ -100,7 +100,9 @@
 
 
 def prep_body(ways, rows_ref, dest_ref, first_ref, valid_ref, *refs):
-    piece_ref, header_ref, numbers_ref, *part_refs = refs if ways else (None, *refs)
+    level_in_ref, *refs = refs
+    piece_ref, header_ref, numbers_ref, level_ref, *part_refs = refs if ways else (None, *refs)
+    level_ref[...] = level_in_ref[...]
     count, tall, _ = header_ref.shape
     rows = tall - PAD
     numbers = row_numbers(dest_ref, first_ref, valid_ref, rows_ref)
@@ -366,13 +368,13 @@
     return ((me // NEAR) ^ far) * NEAR + ((me % NEAR) ^ near)
 
 
+PART_ORDER = ((3, 0), (3, 1), (0, 1), (1, 1), (1, 0), (2, 1), (2, 0), (0, 0))
+
+
 def part_ways():
     if not small_wide():
         return ()
-    outer = lax.axis_size("wide") // NEAR
-    far_first = sorted(range(1, outer), key=lambda far: -min(far, outer - far))
-    ways = [(far, near) for far in far_first for near in range(NEAR)]
-    return (*((0, near) for near in range(1, NEAR)), *reversed(ways), (0, 0))
+    return tuple(way for way in PART_ORDER if way[0] < lax.axis_size("wide") // NEAR)
 
 
 def gather_ways():
@@ -393,11 +395,11 @@
         held[far, 0] = shift(block, far, 0)
         far *= 2
     held[0, 1] = shift(block, 0, 1)
-    if outer == 4:
+    for way in reversed(ways):
+        if way not in held and way[0] < 3 and way[1]:
+            held[way] = shift(held[way[0], 0], 0, way[1])
+    if outer == 4 and (3, 0) not in held:
         held[3, 0] = shift(held[2, 0], 1, 0)
-    for way in ways:
-        if way not in held and way[0] < 3:
-            held[way] = shift(held[way[0], 0], 0, way[1])
     for way in ways:
         if way not in held:
             held[way] = shift(held[2, 1], 1, 0)
@@ -411,20 +413,20 @@
     part = cols // count
     total = count * rows
     level = threshold[None, :]
+
+    ways = part_ways()
+    shape = jax.ShapeDtypeStruct
+    header, numbers, level, *parts = call(
+        partial(prep_body, ways),
+        "prep",
+        [shape((count, rows + PAD, width), BF16), pltpu.VMEM((PAD, width), BF16), pltpu.VMEM(level.shape, F32)]
+        + [shape((2, rows, part), pieces.dtype)] * len(ways),
+        [midpoint_factor, destination[None], first_offset[None], valid_length[None], level] + [pieces] * bool(ways),
+        keep=False,
+    )
     own_level = level
     if part % 128:
         own_level = lax.dynamic_slice_in_dim(level, lax.axis_index("wide") * part, part, 1)
-
-    ways = part_ways()
-    shape = jax.ShapeDtypeStruct
-    header, numbers, *parts = call(
-        partial(prep_body, ways),
-        "prep",
-        [shape((count, rows + PAD, width), BF16), shape((PAD, width), BF16)]
-        + [shape((2, rows, part), pieces.dtype)] * len(ways),
-        [midpoint_factor, destination[None], first_offset[None], valid_length[None]] + [pieces] * bool(ways),
-        keep=False,
-    )
     headers = exchange(header)
     if ways:
         blocks = []

time: 91.7 us -> 88.4 us (0.964)
  waiting for transfers between devices: 25 us -> 23.3 us
  local copies, waits for them, and re-layouts: 1.43 us -> 0.03 us
    ppermute x21, waiting for transfers between devices: 18.7 us -> 14.2 us  [shift(): return lax.ppermute(value, 'wide', pairs)]
    all_to_all x3, waiting for transfers between devices: 5.1 us -> 7.96 us  [exchange(): lax.all_to_all(blocks, 'wide', split_axis=0, concat_axis=0, tiled=True)]
    ppermute x21, starting transfers between devices: 31.1 us -> 29.2 us  [shift(): return lax.ppermute(value, 'wide', pairs)]
    all_to_all x3, starting transfers between devices: 14.2 us -> 15.8 us  [exchange(): lax.all_to_all(blocks, 'wide', split_axis=0, concat_axis=0, tiled=True)]
    unnamed x18 -> x14, local copies, waits for them, and re-layouts: 1.43 us -> 0.03 us
  transfers between devices with their start and end apart: 26 -> 26, of which waited for: 14 -> 10; matrix products, arithmetic and copies ran while one was open for 0% -> 0% of each run, Pallas kernels for 15% -> 16%
where the time goes in v5:
time: 88.4 us; the launch traced here: 87.8 us
  starting transfers between devices  45.2 us (51%)
  waiting for transfers between devices  23.3 us (26%)
  Pallas kernels  18.5 us (21%)
    ppermute x21, starting transfers between devices, shift(): return lax.ppermute(value, 'wide', pairs)  29.2 us
    pallas_call x7, Pallas kernels, call(): pl.pallas_call(body, in_specs=[VMEM] * len(arrays), out_specs=out_specs o...  18.5 us
    all_to_all x3, starting transfers between devices, exchange(): lax.all_to_all(blocks, 'wide', split_axis=0, concat_axis=0, tiled=True)  15.8 us
    ppermute x21, waiting for transfers between devices, shift(): return lax.ppermute(value, 'wide', pairs)  14.2 us
    all_to_all x3, waiting for transfers between devices, exchange(): lax.all_to_all(blocks, 'wide', split_axis=0, concat_axis=0, tiled=True)  7.96 us
  transfers between devices with their start and end apart: 26, of which 10 were waited for; matrix products, arithmetic and copies ran while one was open for 0% of the time, Pallas kernels for 16%

profile of v5, /device:TPU:0, one launch (start us, length us, event | category | flops | bytes accessed | tf_op | source)
XLA Modules:
  0.0 87.8 jit_solution(15538383607224496381)
XLA Ops:
  0.6 2.4 %shard_map.94 = (bf16[8,72,128]{2,1,0:T(8,128)(2,1)}, bf16[8,128]{1,0:T(8,128)(2,1)S(1)}, f32[1,4096]{1,0:T(1,128)S(1)}, bf16[2,64,512]{2,1,0:T(8,128)(2,1)}, bf...) custom-call(f32[64,128]{1,0:T(8,128)} %rows_ref.3, ...), custom_call_target="tpu_custom_call" | custom-call | tf_op jit(solution)/shard_map/pallas_call | solution.py:329
  3.0 7.4 %all-to-all-start = ((bf16[8,72,128]{2,1,0:T(8,128)(2,1)}), bf16[8,72,128]{2,1,0:T(8,128)(2,1)S(1)}, u32[]{:S(2)}, u32[]{:S(2)}) async-start(bf16[8,72,128]{2,1,0:T(8,128)(2,1)} %get-tuple-element.27), calls=%async_computation | async-start | bytes 294912 | tf_op jit(solution)/shard_map/all_to_all | solution.py:346
  10.5 3.8 %collective-permute-start.1 = (bf16[2,64,512]{2,1,0:T(8,128)(2,1)}, bf16[2,64,512]{2,1,0:T(8,128)(2,1)S(1)}, u32[]{:S(2)}, u32[]{:S(2)}) collective-permute-start(bf16[2,64,512]{2,1,0:T(8,128)(2,1)} %get-tuple-element.33), channel_id=1, source_target_pairs={{0,12},{2,14},{4,8},{6,10},{8,4},{10,6},{12,0},{14,2},{1,13},{3,15... | collective-permute-start | bytes 393224 | tf_op jit(solution)/shard_map/ppermute | solution.py:363
  14.3 1.5 %collective-permute-start.2 = (bf16[2,64,512]{2,1,0:T(8,128)(2,1)}, bf16[2,64,512]{2,1,0:T(8,128)(2,1)S(1)}, u32[]{:S(2)}, u32[]{:S(2)}) collective-permute-start(bf16[2,64,512]{2,1,0:T(8,128)(2,1)} %get-tuple-element.34), channel_id=1, source_target_pairs={{0,14},{2,12},{4,10},{6,8},{8,6},{10,4},{12,2},{14,0},{1,15},{3,13... | collective-permute-start | bytes 393224 | tf_op jit(solution)/shard_map/ppermute | solution.py:363
  15.8 8.0 %all-to-all-done.header_ref = bf16[8,72,128]{2,1,0:T(8,128)(2,1)S(1)} async-done(((bf16[8,72,128]{2,1,0:T(8,128)(2,1)}), bf16[8,72,128]{2,1,0:T(8,128)(2,1)S(1)}, u32[]{:S(2)}, u32[]{:S(2)}) %all-to-all-start) | async-done | bytes 147488 | tf_op jit(solution)/shard_map/all_to_all | solution.py:346
  23.7 4.3 %shard_map.95 = (f32[72,128]{1,0:T(8,128)S(1)}, bf16[64,128]{1,0:T(8,128)(2,1)S(1)}, f32[512,128]{1,0:T(8,128)S(1)}) custom-call(bf16[2,64,4096]{2,1,0:T(8,128)(2,1)} %piece_ref.3, bf16[8,72,128]{2,1,0:T(8,128)(2,1)S(1)} %all-to-all-done.header_ref, bf16[8,128]{1,0:T(8,128)(2,1)S(1)} %get-tuple-element.26.numbers_ref, f32[4096,128]{1,0:T(8,128)} %right_ref.1, ...), custom_call_target="tpu_custom_call" | custom-call | tf_op jit(solution)/shard_map/pallas_call | solution.py:329
  28.1 1.2 %collective-permute-done.refs_0_ = f32[72,128]{1,0:T(8,128)S(1)} collective-permute-done((f32[72,128]{1,0:T(8,128)S(1)}, f32[72,128]{1,0:T(8,128)S(1)}, u32[]{:S(2)}, u32[]{:S(2)}) %collective-permute-start) | collective-permute-done | bytes 36896 | tf_op jit(solution)/shard_map/ppermute | solution.py:351
  29.3 0.8 shard_map.96
  30.1 3.4 %all-to-all-start.1 = ((bf16[8,64,128]{2,1,0:T(8,128)(2,1)}), bf16[8,64,128]{2,1,0:T(8,128)(2,1)S(1)}, u32[]{:S(2)}, u32[]{:S(2)}) async-start(bf16[8,64,128]{2,1,0:T(8,128)(2,1)} %get-tuple-element.42), calls=%async_computation.1 | async-start | bytes 262144 | tf_op jit(solution)/shard_map/all_to_all | solution.py:346
  33.5 1.9 %collective-permute-start.3 = (bf16[2,64,512]{2,1,0:T(8,128)(2,1)S(1)}, bf16[2,64,512]{2,1,0:T(8,128)(2,1)S(1)}, u32[]{:S(2)}, u32[]{:S(2)}) collective-permute-start(bf16[2,64,512]{2,1,0:T(8,128)(2,1)S(1)} %copy-done.6), channel_id=1, source_target_pairs={{0,2},{2,0},{4,6},{6,4},{8,10},{10,8},{12,14},{14,12},{1,3},{3,1},... | collective-permute-start | bytes 393224 | tf_op jit(solution)/shard_map/ppermute | solution.py:363
  35.4 1.5 %collective-permute-start.4 = (bf16[2,64,512]{2,1,0:T(8,128)(2,1)S(1)}, bf16[2,64,512]{2,1,0:T(8,128)(2,1)S(1)}, u32[]{:S(2)}, u32[]{:S(2)}) collective-permute-start(bf16[2,64,512]{2,1,0:T(8,128)(2,1)S(1)} %copy-done.5), channel_id=1, source_target_pairs={{0,6},{2,4},{4,2},{6,0},{8,14},{10,12},{12,10},{14,8},{1,7},{3,5},... | collective-permute-start | bytes 393224 | tf_op jit(solution)/shard_map/ppermute | solution.py:363
  37.0 3.7 %collective-permute-start.6 = (bf16[2,64,512]{2,1,0:T(8,128)(2,1)S(1)}, bf16[2,64,512]{2,1,0:T(8,128)(2,1)S(1)}, u32[]{:S(2)}, u32[]{:S(2)}) collective-permute-start(bf16[2,64,512]{2,1,0:T(8,128)(2,1)S(1)} %copy-done.3), channel_id=1, source_target_pairs={{0,10},{2,8},{4,14},{6,12},{8,2},{10,0},{12,6},{14,4},{1,11},{3,9}... | collective-permute-start | bytes 393224 | tf_op jit(solution)/shard_map/ppermute | solution.py:363
  41.3 3.2 %collective-permute-done.3.refs_2_ = bf16[2,64,512]{2,1,0:T(8,128)(2,1)S(1)} collective-permute-done((bf16[2,64,512]{2,1,0:T(8,128)(2,1)S(1)}, bf16[2,64,512]{2,1,0:T(8,128)(2,1)S(1)}, u32[]{:S(2)}, u32[]{:S(2)}) %collective-permute-start.3) | collective-permute-done | bytes 131104 | tf_op jit(solution)/shard_map/ppermute | solution.py:363
  44.4 4.4 %collective-permute-done.4.refs_3_ = bf16[2,64,512]{2,1,0:T(8,128)(2,1)S(1)} collective-permute-done((bf16[2,64,512]{2,1,0:T(8,128)(2,1)S(1)}, bf16[2,64,512]{2,1,0:T(8,128)(2,1)S(1)}, u32[]{:S(2)}, u32[]{:S(2)}) %collective-permute-start.4) | collective-permute-done | bytes 131104 | tf_op jit(solution)/shard_map/ppermute | solution.py:363
  49.1 3.5 %collective-permute-done.7.refs_6_ = bf16[2,64,512]{2,1,0:T(8,128)(2,1)S(1)} collective-permute-done((bf16[2,64,512]{2,1,0:T(8,128)(2,1)S(1)}, bf16[2,64,512]{2,1,0:T(8,128)(2,1)S(1)}, u32[]{:S(2)}, u32[]{:S(2)}) %collective-permute-start.7) | collective-permute-done | bytes 131104 | tf_op jit(solution)/shard_map/ppermute | solution.py:363
  52.6 2.6 %shard_map.97 = (f32[512,128]{1,0:T(8,128)S(1)}, bf16[512,128]{1,0:T(8,128)(2,1)S(1)}, bf16[512,128]{1,0:T(8,128)(2,1)S(1)}) custom-call(bf16[8,72,128]{2,1,0:T(8,128)(2,1)S(1)} %all-to-all-done.header_ref, f32[512,128]{1,0:T(8,128)S(1)} %get-tuple-element.32.right_ref, f32[1,4096]{1,0:T(1,128)S(1)} %get-tuple-element.28.level_ref, ...), custom_call_target="tpu_custom_call" | custom-call | tf_op jit(solution)/shard_map/pallas_call | solution.py:329
  55.3 3.4 %collective-permute-start.9 = (bf16[512,128]{1,0:T(8,128)(2,1)S(1)}, bf16[512,128]{1,0:T(8,128)(2,1)S(1)}, u32[]{:S(2)}, u32[]{:S(2)}) collective-permute-start(bf16[512,128]{1,0:T(8,128)(2,1)S(1)} %get-tuple-element.41.refs_0_.refs_1_), channel_id=1, source_target_pairs={{0,4},{2,6},{4,0},{6,2},{8,12},{10,14},{12,8},{14,10},{1,5},{3,7},... | collective-permute-start | bytes 393224 | tf_op jit(solution)/shard_map/ppermute | solution.py:363
  58.7 0.6 collective-permute-start.8
  59.3 3.1 %shard_map.99 = (bf16[512,128]{1,0:T(8,128)(2,1)S(1)}, bf16[8,72,128]{2,1,0:T(8,128)(2,1)}) custom-call(bf16[8,72,128]{2,1,0:T(8,128)(2,1)S(1)} %all-to-all-done.header_ref, f32[512,128]{1,0:T(8,128)S(1)} %get-tuple-element.43.right_ref, f32[1,4096]{1,0:T(1,128)S(1)} %get-tuple-element.28.level_ref, bf16[2,64,512]{2,1,0:T(8,128)(2,1)S(1)} %collective-permute-done.1.refs_0_, ...), custom_call_target="tpu_custom_call" | custom-call | tf_op jit(solution)/shard_map/pallas_call | solution.py:329
  62.5 5.0 %all-to-all-start.2 = ((bf16[8,72,128]{2,1,0:T(8,128)(2,1)}), bf16[8,72,128]{2,1,0:T(8,128)(2,1)S(1)}, u32[]{:S(2)}, u32[]{:S(2)}) async-start(bf16[8,72,128]{2,1,0:T(8,128)(2,1)} %get-tuple-element.45), calls=%async_computation.2 | async-start | bytes 294912 | tf_op jit(solution)/shard_map/all_to_all | solution.py:346
  67.5 2.0 %collective-permute-start.12 = (bf16[512,128]{1,0:T(8,128)(2,1)S(1)}, bf16[512,128]{1,0:T(8,128)(2,1)S(1)}, u32[]{:S(2)}, u32[]{:S(2)}) collective-permute-start(bf16[512,128]{1,0:T(8,128)(2,1)S(1)} %collective-permute-done.11.refs_4_.refs_5_), channel_id=1, source_target_pairs={{0,2},{2,0},{4,6},{6,4},{8,10},{10,8},{12,14},{14,12},{1,3},{3,1},... | collective-permute-start | bytes 393224 | tf_op jit(solution)/shard_map/ppermute | solution.py:363
  69.5 1.5 %collective-permute-start.13 = (bf16[512,128]{1,0:T(8,128)(2,1)S(1)}, bf16[512,128]{1,0:T(8,128)(2,1)S(1)}, u32[]{:S(2)}, u32[]{:S(2)}) collective-permute-start(bf16[512,128]{1,0:T(8,128)(2,1)S(1)} %collective-permute-done.11.refs_4_.refs_5_), channel_id=1, source_target_pairs={{0,4},{2,6},{4,0},{6,2},{8,12},{10,14},{12,8},{14,10},{1,5},{3,7},... | collective-permute-start | bytes 393224 | tf_op jit(solution)/shard_map/ppermute | solution.py:363
  71.0 0.6 collective-permute-start.10
  71.6 2.0 %collective-permute-start.20 = (bf16[512,128]{1,0:T(8,128)(2,1)S(1)}, bf16[512,128]{1,0:T(8,128)(2,1)S(1)}, u32[]{:S(2)}, u32[]{:S(2)}) collective-permute-start(bf16[512,128]{1,0:T(8,128)(2,1)S(1)} %collective-permute-done.19.refs_13_), channel_id=1, source_target_pairs={{0,2},{2,0},{4,6},{6,4},{8,10},{10,8},{12,14},{14,12},{1,3},{3,1},... | collective-permute-start | bytes 393224 | tf_op jit(solution)/shard_map/ppermute | solution.py:363
  73.6 1.4 %collective-permute-done.12.refs_5_.refs_6_ = bf16[512,128]{1,0:T(8,128)(2,1)S(1)} collective-permute-done((bf16[512,128]{1,0:T(8,128)(2,1)S(1)}, bf16[512,128]{1,0:T(8,128)(2,1)S(1)}, u32[]{:S(2)}, u32[]{:S(2)}) %collective-permute-start.12) | collective-permute-done | bytes 131104 | tf_op jit(solution)/shard_map/ppermute | solution.py:363
  75.0 1.5 %collective-permute-start.14 = (bf16[512,128]{1,0:T(8,128)(2,1)S(1)}, bf16[512,128]{1,0:T(8,128)(2,1)S(1)}, u32[]{:S(2)}, u32[]{:S(2)}) collective-permute-start(bf16[512,128]{1,0:T(8,128)(2,1)S(1)} %collective-permute-done.12.refs_5_.refs_6_), channel_id=1, source_target_pairs={{0,4},{2,6},{4,0},{6,2},{8,12},{10,14},{12,8},{14,10},{1,5},{3,7},... | collective-permute-start | bytes 393224 | tf_op jit(solution)/shard_map/ppermute | solution.py:363
  76.5 1.0 %collective-permute-start.16 = (bf16[512,128]{1,0:T(8,128)(2,1)S(1)}, bf16[512,128]{1,0:T(8,128)(2,1)S(1)}, u32[]{:S(2)}, u32[]{:S(2)}) collective-permute-start(bf16[512,128]{1,0:T(8,128)(2,1)S(1)} %get-tuple-element.46.refs_9_), channel_id=1, source_target_pairs={{0,2},{2,0},{4,6},{6,4},{8,10},{10,8},{12,14},{14,12},{1,3},{3,1},... | collective-permute-start | bytes 393224 | tf_op jit(solution)/shard_map/ppermute | solution.py:363
  78.0 1.3 %collective-permute-start.21 = (bf16[512,128]{1,0:T(8,128)(2,1)S(1)}, bf16[512,128]{1,0:T(8,128)(2,1)S(1)}, u32[]{:S(2)}, u32[]{:S(2)}) collective-permute-start(bf16[512,128]{1,0:T(8,128)(2,1)S(1)} %collective-permute-done.19.refs_13_), channel_id=1, source_target_pairs={{0,4},{2,6},{4,0},{6,2},{8,12},{10,14},{12,8},{14,10},{1,5},{3,7},... | collective-permute-start | bytes 393224 | tf_op jit(solution)/shard_map/ppermute | solution.py:363
  79.3 1.0 %collective-permute-start.18 = (bf16[512,128]{1,0:T(8,128)(2,1)S(1)}, bf16[512,128]{1,0:T(8,128)(2,1)S(1)}, u32[]{:S(2)}, u32[]{:S(2)}) collective-permute-start(bf16[512,128]{1,0:T(8,128)(2,1)S(1)} %collective-permute-done.17.refs_11_), channel_id=1, source_target_pairs={{0,2},{2,0},{4,6},{6,4},{8,10},{10,8},{12,14},{14,12},{1,3},{3,1},... | collective-permute-start | bytes 393224 | tf_op jit(solution)/shard_map/ppermute | solution.py:363
  80.8 1.1 %collective-permute-start.22 = (bf16[512,128]{1,0:T(8,128)(2,1)S(1)}, bf16[512,128]{1,0:T(8,128)(2,1)S(1)}, u32[]{:S(2)}, u32[]{:S(2)}) collective-permute-start(bf16[512,128]{1,0:T(8,128)(2,1)S(1)} %collective-permute-done.20.refs_14_), channel_id=1, source_target_pairs={{0,4},{2,6},{4,0},{6,2},{8,12},{10,14},{12,8},{14,10},{1,5},{3,7},... | collective-permute-start | bytes 393224 | tf_op jit(solution)/shard_map/ppermute | solution.py:363
  82.0 3.2 %shard_map.98 = bf16[2,64,4096]{2,1,0:T(8,128)(2,1)} custom-call(bf16[2,64,4096]{2,1,0:T(8,128)(2,1)} %piece_ref.3, bf16[8,128]{1,0:T(8,128)(2,1)S(1)} %get-tuple-element.26.numbers_ref, bf16[64,128]{1,0:T(8,128)(2,1)S(1)} %get-tuple-element.29.left_ref, bf16[64,128]{1,0:T(8,128)(2,1)S(1)} %get-tuple-element.31.move_ref, ...), custom_call_target="tpu_custom_call" | custom-call | tf_op jit(solution)/shard_map/pallas_call | solution.py:329
  85.7 2.1 %shard_map.100 = (f32[4096,128]{1,0:T(8,128)}, f32[64,128]{1,0:T(8,128)}) custom-call(bf16[8,72,128]{2,1,0:T(8,128)(2,1)S(1)} %all-to-all-done.header_ref, bf16[8,64,128]{2,1,0:T(8,128)(2,1)S(1)} %all-to-all-done.1.move_ref, f32[64,128]{1,0:T(8,128)S(1)} %copy-done.1, f32[72,128]{1,0:T(8,128)S(1)} %convert_reduce_fusion.mine_ref, ...), custom_call_target="tpu_custom_call" | custom-call | tf_op jit(solution)/shard_map/pallas_call | solution.py:329
  (42 shorter events, 2.8 us)
Async XLA Ops:
  3.0 30.5 %copy-start.6 = (bf16[2,64,512]{2,1,0:T(8,128)(2,1)S(1)}, bf16[2,64,512]{2,1,0:T(8,128)(2,1)}, u32[]{:S(2)}) copy-start(bf16[2,64,512]{2,1,0:T(8,128)(2,1)} %get-tuple-element.35) | copy-start | bytes 393220
  3.0 32.4 %copy-start.5 = (bf16[2,64,512]{2,1,0:T(8,128)(2,1)S(1)}, bf16[2,64,512]{2,1,0:T(8,128)(2,1)}, u32[]{:S(2)}) copy-start(bf16[2,64,512]{2,1,0:T(8,128)(2,1)} %get-tuple-element.36) | copy-start | bytes 393220
  3.0 33.9 %copy-start.4 = (bf16[2,64,512]{2,1,0:T(8,128)(2,1)S(1)}, bf16[2,64,512]{2,1,0:T(8,128)(2,1)}, u32[]{:S(2)}) copy-start(bf16[2,64,512]{2,1,0:T(8,128)(2,1)} %get-tuple-element.37) | copy-start | bytes 393220
  3.0 34.0 %copy-start.3 = (bf16[2,64,512]{2,1,0:T(8,128)(2,1)S(1)}, bf16[2,64,512]{2,1,0:T(8,128)(2,1)}, u32[]{:S(2)}) copy-start(bf16[2,64,512]{2,1,0:T(8,128)(2,1)} %get-tuple-element.38) | copy-start | bytes 393220
  3.0 37.7 %copy-start.2 = (bf16[2,64,512]{2,1,0:T(8,128)(2,1)S(1)}, bf16[2,64,512]{2,1,0:T(8,128)(2,1)}, u32[]{:S(2)}) copy-start(bf16[2,64,512]{2,1,0:T(8,128)(2,1)} %get-tuple-element.39) | copy-start | bytes 393220
  3.0 49.6 %copy-start = (bf16[2,64,512]{2,1,0:T(8,128)(2,1)S(1)}, bf16[2,64,512]{2,1,0:T(8,128)(2,1)}, u32[]{:S(2)}) copy-start(bf16[2,64,512]{2,1,0:T(8,128)(2,1)} %get-tuple-element.40.refs_7_) | copy-start | bytes 393220
  3.0 20.7 %all-to-all-start = ((bf16[8,72,128]{2,1,0:T(8,128)(2,1)}), bf16[8,72,128]{2,1,0:T(8,128)(2,1)S(1)}, u32[]{:S(2)}, u32[]{:S(2)}) async-start(bf16[8,72,128]{2,1,0:T(8,128)(2,1)} %get-tuple-element.27), calls=%async_computation | async-start | bytes 294912 | tf_op jit(solution)/shard_map/all_to_all | solution.py:346
  10.5 26.6 %collective-permute-start.1 = (bf16[2,64,512]{2,1,0:T(8,128)(2,1)}, bf16[2,64,512]{2,1,0:T(8,128)(2,1)S(1)}, u32[]{:S(2)}, u32[]{:S(2)}) collective-permute-start(bf16[2,64,512]{2,1,0:T(8,128)(2,1)} %get-tuple-element.33), channel_id=1, source_target_pairs={{0,12},{2,14},{4,8},{6,10},{8,4},{10,6},{12,0},{14,2},{1,13},{3,15... | collective-permute-start | bytes 393224 | tf_op jit(solution)/shard_map/ppermute | solution.py:363
  14.3 26.4 %collective-permute-start.2 = (bf16[2,64,512]{2,1,0:T(8,128)(2,1)}, bf16[2,64,512]{2,1,0:T(8,128)(2,1)S(1)}, u32[]{:S(2)}, u32[]{:S(2)}) collective-permute-start(bf16[2,64,512]{2,1,0:T(8,128)(2,1)} %get-tuple-element.34), channel_id=1, source_target_pairs={{0,14},{2,12},{4,10},{6,8},{8,6},{10,4},{12,2},{14,0},{1,15},{3,13... | collective-permute-start | bytes 393224 | tf_op jit(solution)/shard_map/ppermute | solution.py:363
  28.0 1.3 %collective-permute-start = (f32[72,128]{1,0:T(8,128)S(1)}, f32[72,128]{1,0:T(8,128)S(1)}, u32[]{:S(2)}, u32[]{:S(2)}) collective-permute-start(f32[72,128]{1,0:T(8,128)S(1)} %get-tuple-element.30.mine_ref), channel_id=1, source_target_pairs={{0,1},{1,0},{2,3},{3,2},{4,5},{5,4},{6,7},{7,6},{8,9},{9,8},{10,11... | collective-permute-start | bytes 110600 | tf_op jit(solution)/shard_map/ppermute | solution.py:351
  30.1 29.2 %all-to-all-start.1 = ((bf16[8,64,128]{2,1,0:T(8,128)(2,1)}), bf16[8,64,128]{2,1,0:T(8,128)(2,1)S(1)}, u32[]{:S(2)}, u32[]{:S(2)}) async-start(bf16[8,64,128]{2,1,0:T(8,128)(2,1)} %get-tuple-element.42), calls=%async_computation.1 | async-start | bytes 262144 | tf_op jit(solution)/shard_map/all_to_all | solution.py:346
  33.5 11.0 %collective-permute-start.3 = (bf16[2,64,512]{2,1,0:T(8,128)(2,1)S(1)}, bf16[2,64,512]{2,1,0:T(8,128)(2,1)S(1)}, u32[]{:S(2)}, u32[]{:S(2)}) collective-permute-start(bf16[2,64,512]{2,1,0:T(8,128)(2,1)S(1)} %copy-done.6), channel_id=1, source_target_pairs={{0,2},{2,0},{4,6},{6,4},{8,10},{10,8},{12,14},{14,12},{1,3},{3,1},... | collective-permute-start | bytes 393224 | tf_op jit(solution)/shard_map/ppermute | solution.py:363
  35.4 13.5 %collective-permute-start.4 = (bf16[2,64,512]{2,1,0:T(8,128)(2,1)S(1)}, bf16[2,64,512]{2,1,0:T(8,128)(2,1)S(1)}, u32[]{:S(2)}, u32[]{:S(2)}) collective-permute-start(bf16[2,64,512]{2,1,0:T(8,128)(2,1)S(1)} %copy-done.5), channel_id=1, source_target_pairs={{0,6},{2,4},{4,2},{6,0},{8,14},{10,12},{12,10},{14,8},{1,7},{3,5},... | collective-permute-start | bytes 393224 | tf_op jit(solution)/shard_map/ppermute | solution.py:363
  36.9 12.2 %collective-permute-start.5 = (bf16[2,64,512]{2,1,0:T(8,128)(2,1)S(1)}, bf16[2,64,512]{2,1,0:T(8,128)(2,1)S(1)}, u32[]{:S(2)}, u32[]{:S(2)}) collective-permute-start(bf16[2,64,512]{2,1,0:T(8,128)(2,1)S(1)} %copy-done.4), channel_id=1, source_target_pairs={{0,4},{2,6},{4,0},{6,2},{8,12},{10,14},{12,8},{14,10},{1,5},{3,7},... | collective-permute-start | bytes 393224 | tf_op jit(solution)/shard_map/ppermute | solution.py:363
  37.0 12.1 %collective-permute-start.6 = (bf16[2,64,512]{2,1,0:T(8,128)(2,1)S(1)}, bf16[2,64,512]{2,1,0:T(8,128)(2,1)S(1)}, u32[]{:S(2)}, u32[]{:S(2)}) collective-permute-start(bf16[2,64,512]{2,1,0:T(8,128)(2,1)S(1)} %copy-done.3), channel_id=1, source_target_pairs={{0,10},{2,8},{4,14},{6,12},{8,2},{10,0},{12,6},{14,4},{1,11},{3,9}... | collective-permute-start | bytes 393224 | tf_op jit(solution)/shard_map/ppermute | solution.py:363
  40.7 11.9 %collective-permute-start.7 = (bf16[2,64,512]{2,1,0:T(8,128)(2,1)S(1)}, bf16[2,64,512]{2,1,0:T(8,128)(2,1)S(1)}, u32[]{:S(2)}, u32[]{:S(2)}) collective-permute-start(bf16[2,64,512]{2,1,0:T(8,128)(2,1)S(1)} %copy-done.2), channel_id=1, source_target_pairs={{0,8},{2,10},{4,12},{6,14},{8,0},{10,2},{12,4},{14,6},{1,9},{3,11}... | collective-permute-start | bytes 393224 | tf_op jit(solution)/shard_map/ppermute | solution.py:363
  55.3 12.2 %collective-permute-start.11 = (bf16[512,128]{1,0:T(8,128)(2,1)S(1)}, bf16[512,128]{1,0:T(8,128)(2,1)S(1)}, u32[]{:S(2)}, u32[]{:S(2)}) collective-permute-start(bf16[512,128]{1,0:T(8,128)(2,1)S(1)} %get-tuple-element.41.refs_0_.refs_1_), channel_id=1, source_target_pairs={{0,8},{2,10},{4,12},{6,14},{8,0},{10,2},{12,4},{14,6},{1,9},{3,11}... | collective-permute-start | bytes 393224 | tf_op jit(solution)/shard_map/ppermute | solution.py:363
  55.3 15.6 %collective-permute-start.9 = (bf16[512,128]{1,0:T(8,128)(2,1)S(1)}, bf16[512,128]{1,0:T(8,128)(2,1)S(1)}, u32[]{:S(2)}, u32[]{:S(2)}) collective-permute-start(bf16[512,128]{1,0:T(8,128)(2,1)S(1)} %get-tuple-element.41.refs_0_.refs_1_), channel_id=1, source_target_pairs={{0,4},{2,6},{4,0},{6,2},{8,12},{10,14},{12,8},{14,10},{1,5},{3,7},... | collective-permute-start | bytes 393224 | tf_op jit(solution)/shard_map/ppermute | solution.py:363
  58.7 12.9 %collective-permute-start.8 = (bf16[512,128]{1,0:T(8,128)(2,1)S(1)}, bf16[512,128]{1,0:T(8,128)(2,1)S(1)}, u32[]{:S(2)}, u32[]{:S(2)}) collective-permute-start(bf16[512,128]{1,0:T(8,128)(2,1)S(1)} %get-tuple-element.41.refs_0_.refs_1_), channel_id=1, source_target_pairs={{0,2},{2,0},{4,6},{6,4},{8,10},{10,8},{12,14},{14,12},{1,3},{3,1},... | collective-permute-start | bytes 393224 | tf_op jit(solution)/shard_map/ppermute | solution.py:363
  62.4 9.2 %collective-permute-start.19 = (bf16[512,128]{1,0:T(8,128)(2,1)S(1)}, bf16[512,128]{1,0:T(8,128)(2,1)S(1)}, u32[]{:S(2)}, u32[]{:S(2)}) collective-permute-start(bf16[512,128]{1,0:T(8,128)(2,1)S(1)} %get-tuple-element.46.refs_9_), channel_id=1, source_target_pairs={{0,8},{2,10},{4,12},{6,14},{8,0},{10,2},{12,4},{14,6},{1,9},{3,11}... | collective-permute-start | bytes 393224 | tf_op jit(solution)/shard_map/ppermute | solution.py:363
  62.5 19.4 %all-to-all-start.2 = ((bf16[8,72,128]{2,1,0:T(8,128)(2,1)}), bf16[8,72,128]{2,1,0:T(8,128)(2,1)S(1)}, u32[]{:S(2)}, u32[]{:S(2)}) async-start(bf16[8,72,128]{2,1,0:T(8,128)(2,1)} %get-tuple-element.45), calls=%async_computation.2 | async-start | bytes 294912 | tf_op jit(solution)/shard_map/all_to_all | solution.py:346
  67.5 7.5 %collective-permute-start.12 = (bf16[512,128]{1,0:T(8,128)(2,1)S(1)}, bf16[512,128]{1,0:T(8,128)(2,1)S(1)}, u32[]{:S(2)}, u32[]{:S(2)}) collective-permute-start(bf16[512,128]{1,0:T(8,128)(2,1)S(1)} %collective-permute-done.11.refs_4_.refs_5_), channel_id=1, source_target_pairs={{0,2},{2,0},{4,6},{6,4},{8,10},{10,8},{12,14},{14,12},{1,3},{3,1},... | collective-permute-start | bytes 393224 | tf_op jit(solution)/shard_map/ppermute | solution.py:363
  69.5 7.0 %collective-permute-start.13 = (bf16[512,128]{1,0:T(8,128)(2,1)S(1)}, bf16[512,128]{1,0:T(8,128)(2,1)S(1)}, u32[]{:S(2)}, u32[]{:S(2)}) collective-permute-start(bf16[512,128]{1,0:T(8,128)(2,1)S(1)} %collective-permute-done.11.refs_4_.refs_5_), channel_id=1, source_target_pairs={{0,4},{2,6},{4,0},{6,2},{8,12},{10,14},{12,8},{14,10},{1,5},{3,7},... | collective-permute-start | bytes 393224 | tf_op jit(solution)/shard_map/ppermute | solution.py:363
  71.0 7.0 %collective-permute-start.10 = (bf16[512,128]{1,0:T(8,128)(2,1)S(1)}, bf16[512,128]{1,0:T(8,128)(2,1)S(1)}, u32[]{:S(2)}, u32[]{:S(2)}) collective-permute-start(bf16[512,128]{1,0:T(8,128)(2,1)S(1)} %collective-permute-done.9.refs_2_.refs_3_), channel_id=1, source_target_pairs={{0,2},{2,0},{4,6},{6,4},{8,10},{10,8},{12,14},{14,12},{1,3},{3,1},... | collective-permute-start | bytes 393224 | tf_op jit(solution)/shard_map/ppermute | solution.py:363
  71.5 7.8 %collective-permute-start.17 = (bf16[512,128]{1,0:T(8,128)(2,1)S(1)}, bf16[512,128]{1,0:T(8,128)(2,1)S(1)}, u32[]{:S(2)}, u32[]{:S(2)}) collective-permute-start(bf16[512,128]{1,0:T(8,128)(2,1)S(1)} %get-tuple-element.46.refs_9_), channel_id=1, source_target_pairs={{0,4},{2,6},{4,0},{6,2},{8,12},{10,14},{12,8},{14,10},{1,5},{3,7},... | collective-permute-start | bytes 393224 | tf_op jit(solution)/shard_map/ppermute | solution.py:363
  71.6 9.2 %collective-permute-start.20 = (bf16[512,128]{1,0:T(8,128)(2,1)S(1)}, bf16[512,128]{1,0:T(8,128)(2,1)S(1)}, u32[]{:S(2)}, u32[]{:S(2)}) collective-permute-start(bf16[512,128]{1,0:T(8,128)(2,1)S(1)} %collective-permute-done.19.refs_13_), channel_id=1, source_target_pairs={{0,2},{2,0},{4,6},{6,4},{8,10},{10,8},{12,14},{14,12},{1,3},{3,1},... | collective-permute-start | bytes 393224 | tf_op jit(solution)/shard_map/ppermute | solution.py:363
  75.0 6.9 %collective-permute-start.14 = (bf16[512,128]{1,0:T(8,128)(2,1)S(1)}, bf16[512,128]{1,0:T(8,128)(2,1)S(1)}, u32[]{:S(2)}, u32[]{:S(2)}) collective-permute-start(bf16[512,128]{1,0:T(8,128)(2,1)S(1)} %collective-permute-done.12.refs_5_.refs_6_), channel_id=1, source_target_pairs={{0,4},{2,6},{4,0},{6,2},{8,12},{10,14},{12,8},{14,10},{1,5},{3,7},... | collective-permute-start | bytes 393224 | tf_op jit(solution)/shard_map/ppermute | solution.py:363
  76.5 8.7 %collective-permute-start.16 = (bf16[512,128]{1,0:T(8,128)(2,1)S(1)}, bf16[512,128]{1,0:T(8,128)(2,1)S(1)}, u32[]{:S(2)}, u32[]{:S(2)}) collective-permute-start(bf16[512,128]{1,0:T(8,128)(2,1)S(1)} %get-tuple-element.46.refs_9_), channel_id=1, source_target_pairs={{0,2},{2,0},{4,6},{6,4},{8,10},{10,8},{12,14},{14,12},{1,3},{3,1},... | collective-permute-start | bytes 393224 | tf_op jit(solution)/shard_map/ppermute | solution.py:363
  78.0 7.2 %collective-permute-start.21 = (bf16[512,128]{1,0:T(8,128)(2,1)S(1)}, bf16[512,128]{1,0:T(8,128)(2,1)S(1)}, u32[]{:S(2)}, u32[]{:S(2)}) collective-permute-start(bf16[512,128]{1,0:T(8,128)(2,1)S(1)} %collective-permute-done.19.refs_13_), channel_id=1, source_target_pairs={{0,4},{2,6},{4,0},{6,2},{8,12},{10,14},{12,8},{14,10},{1,5},{3,7},... | collective-permute-start | bytes 393224 | tf_op jit(solution)/shard_map/ppermute | solution.py:363
  79.3 5.9 %collective-permute-start.18 = (bf16[512,128]{1,0:T(8,128)(2,1)S(1)}, bf16[512,128]{1,0:T(8,128)(2,1)S(1)}, u32[]{:S(2)}, u32[]{:S(2)}) collective-permute-start(bf16[512,128]{1,0:T(8,128)(2,1)S(1)} %collective-permute-done.17.refs_11_), channel_id=1, source_target_pairs={{0,2},{2,0},{4,6},{6,4},{8,10},{10,8},{12,14},{14,12},{1,3},{3,1},... | collective-permute-start | bytes 393224 | tf_op jit(solution)/shard_map/ppermute | solution.py:363
  80.8 5.0 %collective-permute-start.22 = (bf16[512,128]{1,0:T(8,128)(2,1)S(1)}, bf16[512,128]{1,0:T(8,128)(2,1)S(1)}, u32[]{:S(2)}, u32[]{:S(2)}) collective-permute-start(bf16[512,128]{1,0:T(8,128)(2,1)S(1)} %collective-permute-done.20.refs_14_), channel_id=1, source_target_pairs={{0,4},{2,6},{4,0},{6,2},{8,12},{10,14},{12,8},{14,10},{1,5},{3,7},... | collective-permute-start | bytes 393224 | tf_op jit(solution)/shard_map/ppermute | solution.py:363
  81.9 3.3 %collective-permute-start.15 = (f32[72,128]{1,0:T(8,128)S(1)}, f32[72,128]{1,0:T(8,128)S(1)}, u32[]{:S(2)}, u32[]{:S(2)}) collective-permute-start(f32[72,128]{1,0:T(8,128)S(1)} %convert_reduce_fusion.mine_ref), channel_id=1, source_target_pairs={{0,1},{1,0},{2,3},{3,2},{4,5},{5,4},{6,7},{7,6},{8,9},{9,8},{10,11... | collective-permute-start | bytes 110600 | tf_op jit(solution)/shard_map/ppermute | solution.py:351
  (1 other events, 23.4 us)

commit v6 on v5

--- a/solution.py
+++ b/solution.py
@@ -252,7 +252,8 @@
 
 
 def sparse_body(ways, piece_ref, numbers_ref, left_ref, move_ref, level_ref, *refs):
-    right_refs, out_ref = refs[:-1], refs[-1]
+    *right_refs, out_hbm, out_ref, sem = refs
+    copies = []
     low = (left_ref[...].astype(F32) + move_ref[...].astype(F32)).astype(BF16)
     _, begin, end = standing_numbers(numbers_ref[...], low.shape[0])
     base = lax.axis_index("narrow") * piece_ref.shape[2]
@@ -267,14 +268,23 @@
         out_ref[0, :, at] = (real * share).astype(BF16)
         out_ref[1, :, at] = (imag * share).astype(BF16)
 
-    for way, right_ref in zip(ways, right_refs):
+    for index, (way, right_ref) in enumerate(zip(ways, right_refs)):
         one(right_ref[...], device_at(*way))
+        part = right_ref.shape[0]
+        at = pl.ds(pl.multiple_of(device_at(*way) * part, part), part)
+        copies.append(pltpu.make_async_copy(out_ref.at[:, :, at], out_hbm.at[:, :, at], sem.at[index]))
+        copies[-1].start()
     if not ways:
         block = column_block(right_refs[0].shape[0])
 
         @pl.loop(0, right_refs[0].shape[0] // block)
         def _(step):
             one(right_refs[0][pl.ds(pl.multiple_of(step * block, block), block), :], step)
+
+        copies.append(pltpu.make_async_copy(out_ref, out_hbm, sem.at[0]))
+        copies[-1].start()
+    for copy in copies:
+        copy.wait()
 
 
 def join_body(ways, header_ref, move_ref, rows_ref, mine_ref, *refs):
@@ -368,7 +378,7 @@
     return ((me // NEAR) ^ far) * NEAR + ((me % NEAR) ^ near)
 
 
-PART_ORDER = ((3, 0), (3, 1), (0, 1), (1, 1), (1, 0), (2, 1), (2, 0), (0, 0))
+PART_ORDER = ((3, 0), (3, 1), (1, 1), (1, 0), (0, 1), (2, 1), (2, 0), (0, 0))
 
 
 def part_ways():
@@ -420,7 +430,10 @@
         partial(prep_body, ways),
         "prep",
         [shape((count, rows + PAD, width), BF16), pltpu.VMEM((PAD, width), BF16), pltpu.VMEM(level.shape, F32)]
-        + [shape((2, rows, part), pieces.dtype)] * len(ways),
+        + [
+            pltpu.VMEM((2, rows, part), pieces.dtype) if way == (0, 0) else shape((2, rows, part), pieces.dtype)
+            for way in ways
+        ],
         [midpoint_factor, destination[None], first_offset[None], valid_length[None], level] + [pieces] * bool(ways),
         keep=False,
     )
@@ -475,6 +488,8 @@
         "sparse_pass",
         shape(pieces.shape, BF16),
         [pieces, numbers, left_mine, move_mine, level, *lows],
+        [pltpu.VMEM(pieces.shape, BF16), pltpu.SemaphoreType.DMA((len(lows),))],
+        ANY,
         keep=False,
     )
     new_offset, new_midpoint = call(

time: 88.4 us -> 88.3 us (level)
  transfers between devices with their start and end apart: 26 -> 26, of which waited for: 10 -> 9; matrix products, arithmetic and copies ran while one was open for 0% -> 0% of each run, Pallas kernels for 16% -> 16%
where the time goes in v6:
time: 88.3 us; the launch traced here: 87.8 us
  starting transfers between devices  45.3 us (51%)
  waiting for transfers between devices  23.5 us (27%)
  Pallas kernels  18.2 us (21%)
    ppermute x21, starting transfers between devices, shift(): return lax.ppermute(value, 'wide', pairs)  29.3 us
    pallas_call x7, Pallas kernels, call(): pl.pallas_call(body, in_specs=[VMEM] * len(arrays), out_specs=out_specs o...  18.2 us
    all_to_all x3, starting transfers between devices, exchange(): lax.all_to_all(blocks, 'wide', split_axis=0, concat_axis=0, tiled=True)  15.8 us
    ppermute x21, waiting for transfers between devices, shift(): return lax.ppermute(value, 'wide', pairs)  14.3 us
    all_to_all x3, waiting for transfers between devices, exchange(): lax.all_to_all(blocks, 'wide', split_axis=0, concat_axis=0, tiled=True)  7.96 us
  transfers between devices with their start and end apart: 26, of which 9 were waited for; matrix products, arithmetic and copies ran while one was open for 0% of the time, Pallas kernels for 16%

profile of v6, /device:TPU:0, one launch (start us, length us, event | category | flops | bytes accessed | tf_op | source)
XLA Modules:
  0.0 87.8 jit_solution(9123178463942009355)
XLA Ops:
  0.6 2.3 %shard_map.94 = (bf16[8,72,128]{2,1,0:T(8,128)(2,1)}, bf16[8,128]{1,0:T(8,128)(2,1)S(1)}, f32[1,4096]{1,0:T(1,128)S(1)}, bf16[2,64,512]{2,1,0:T(8,128)(2,1)}, bf...) custom-call(f32[64,128]{1,0:T(8,128)} %rows_ref.3, ...), custom_call_target="tpu_custom_call" | custom-call | tf_op jit(solution)/shard_map/pallas_call | solution.py:339
  3.0 7.4 %all-to-all-start = ((bf16[8,72,128]{2,1,0:T(8,128)(2,1)}), bf16[8,72,128]{2,1,0:T(8,128)(2,1)S(1)}, u32[]{:S(2)}, u32[]{:S(2)}) async-start(bf16[8,72,128]{2,1,0:T(8,128)(2,1)} %get-tuple-element.27), calls=%async_computation | async-start | bytes 294912 | tf_op jit(solution)/shard_map/all_to_all | solution.py:356
  10.4 3.8 %collective-permute-start.1 = (bf16[2,64,512]{2,1,0:T(8,128)(2,1)}, bf16[2,64,512]{2,1,0:T(8,128)(2,1)S(1)}, u32[]{:S(2)}, u32[]{:S(2)}) collective-permute-start(bf16[2,64,512]{2,1,0:T(8,128)(2,1)} %get-tuple-element.33), channel_id=1, source_target_pairs={{0,12},{2,14},{4,8},{6,10},{8,4},{10,6},{12,0},{14,2},{1,13},{3,15... | collective-permute-start | bytes 393224 | tf_op jit(solution)/shard_map/ppermute | solution.py:373
  14.2 1.5 %collective-permute-start.2 = (bf16[2,64,512]{2,1,0:T(8,128)(2,1)}, bf16[2,64,512]{2,1,0:T(8,128)(2,1)S(1)}, u32[]{:S(2)}, u32[]{:S(2)}) collective-permute-start(bf16[2,64,512]{2,1,0:T(8,128)(2,1)} %get-tuple-element.34), channel_id=1, source_target_pairs={{0,14},{2,12},{4,10},{6,8},{8,6},{10,4},{12,2},{14,0},{1,15},{3,13... | collective-permute-start | bytes 393224 | tf_op jit(solution)/shard_map/ppermute | solution.py:373
  15.7 8.0 %all-to-all-done.header_ref = bf16[8,72,128]{2,1,0:T(8,128)(2,1)S(1)} async-done(((bf16[8,72,128]{2,1,0:T(8,128)(2,1)}), bf16[8,72,128]{2,1,0:T(8,128)(2,1)S(1)}, u32[]{:S(2)}, u32[]{:S(2)}) %all-to-all-start) | async-done | bytes 147488 | tf_op jit(solution)/shard_map/all_to_all | solution.py:356
  23.7 4.3 %shard_map.95 = (f32[72,128]{1,0:T(8,128)S(1)}, bf16[64,128]{1,0:T(8,128)(2,1)S(1)}, f32[512,128]{1,0:T(8,128)S(1)}) custom-call(bf16[2,64,4096]{2,1,0:T(8,128)(2,1)} %piece_ref.3, bf16[8,72,128]{2,1,0:T(8,128)(2,1)S(1)} %all-to-all-done.header_ref, bf16[8,128]{1,0:T(8,128)(2,1)S(1)} %get-tuple-element.26.numbers_ref, f32[4096,128]{1,0:T(8,128)} %right_ref.1, ...), custom_call_target="tpu_custom_call" | custom-call | tf_op jit(solution)/shard_map/pallas_call | solution.py:339
  28.0 1.2 %collective-permute-done.refs_0_ = f32[72,128]{1,0:T(8,128)S(1)} collective-permute-done((f32[72,128]{1,0:T(8,128)S(1)}, f32[72,128]{1,0:T(8,128)S(1)}, u32[]{:S(2)}, u32[]{:S(2)}) %collective-permute-start) | collective-permute-done | bytes 36896 | tf_op jit(solution)/shard_map/ppermute | solution.py:361
  29.2 0.8 shard_map.96
  30.0 3.4 %all-to-all-start.1 = ((bf16[8,64,128]{2,1,0:T(8,128)(2,1)}), bf16[8,64,128]{2,1,0:T(8,128)(2,1)S(1)}, u32[]{:S(2)}, u32[]{:S(2)}) async-start(bf16[8,64,128]{2,1,0:T(8,128)(2,1)} %get-tuple-element.42), calls=%async_computation.1 | async-start | bytes 262144 | tf_op jit(solution)/shard_map/all_to_all | solution.py:356
  33.4 2.8 %collective-permute-start.3 = (bf16[2,64,512]{2,1,0:T(8,128)(2,1)S(1)}, bf16[2,64,512]{2,1,0:T(8,128)(2,1)S(1)}, u32[]{:S(2)}, u32[]{:S(2)}) collective-permute-start(bf16[2,64,512]{2,1,0:T(8,128)(2,1)S(1)} %copy-done.5), channel_id=1, source_target_pairs={{0,6},{2,4},{4,2},{6,0},{8,14},{10,12},{12,10},{14,8},{1,7},{3,5},... | collective-permute-start | bytes 393224 | tf_op jit(solution)/shard_map/ppermute | solution.py:373
  36.2 0.5 collective-permute-start.4
  37.0 3.7 %collective-permute-start.6 = (bf16[2,64,512]{2,1,0:T(8,128)(2,1)S(1)}, bf16[2,64,512]{2,1,0:T(8,128)(2,1)S(1)}, u32[]{:S(2)}, u32[]{:S(2)}) collective-permute-start(bf16[2,64,512]{2,1,0:T(8,128)(2,1)S(1)} %copy-done.2), channel_id=1, source_target_pairs={{0,10},{2,8},{4,14},{6,12},{8,2},{10,0},{12,6},{14,4},{1,11},{3,9}... | collective-permute-start | bytes 393224 | tf_op jit(solution)/shard_map/ppermute | solution.py:373
  41.2 7.3 %collective-permute-done.3.refs_2_ = bf16[2,64,512]{2,1,0:T(8,128)(2,1)S(1)} collective-permute-done((bf16[2,64,512]{2,1,0:T(8,128)(2,1)S(1)}, bf16[2,64,512]{2,1,0:T(8,128)(2,1)S(1)}, u32[]{:S(2)}, u32[]{:S(2)}) %collective-permute-start.3) | collective-permute-done | bytes 131104 | tf_op jit(solution)/shard_map/ppermute | solution.py:373
  49.1 3.5 %collective-permute-done.7.refs_6_ = bf16[2,64,512]{2,1,0:T(8,128)(2,1)S(1)} collective-permute-done((bf16[2,64,512]{2,1,0:T(8,128)(2,1)S(1)}, bf16[2,64,512]{2,1,0:T(8,128)(2,1)S(1)}, u32[]{:S(2)}, u32[]{:S(2)}) %collective-permute-start.7) | collective-permute-done | bytes 131104 | tf_op jit(solution)/shard_map/ppermute | solution.py:373
  52.6 2.6 %shard_map.97 = (f32[512,128]{1,0:T(8,128)S(1)}, bf16[512,128]{1,0:T(8,128)(2,1)S(1)}, bf16[512,128]{1,0:T(8,128)(2,1)S(1)}) custom-call(bf16[8,72,128]{2,1,0:T(8,128)(2,1)S(1)} %all-to-all-done.header_ref, f32[512,128]{1,0:T(8,128)S(1)} %get-tuple-element.32.right_ref, f32[1,4096]{1,0:T(1,128)S(1)} %get-tuple-element.28.level_ref, ...), custom_call_target="tpu_custom_call" | custom-call | tf_op jit(solution)/shard_map/pallas_call | solution.py:339
  55.3 3.4 %collective-permute-start.9 = (bf16[512,128]{1,0:T(8,128)(2,1)S(1)}, bf16[512,128]{1,0:T(8,128)(2,1)S(1)}, u32[]{:S(2)}, u32[]{:S(2)}) collective-permute-start(bf16[512,128]{1,0:T(8,128)(2,1)S(1)} %get-tuple-element.41.refs_0_.refs_1_), channel_id=1, source_target_pairs={{0,4},{2,6},{4,0},{6,2},{8,12},{10,14},{12,8},{14,10},{1,5},{3,7},... | collective-permute-start | bytes 393224 | tf_op jit(solution)/shard_map/ppermute | solution.py:373
  58.6 0.6 collective-permute-start.8
  59.2 3.1 %shard_map.99 = (bf16[512,128]{1,0:T(8,128)(2,1)S(1)}, bf16[8,72,128]{2,1,0:T(8,128)(2,1)}) custom-call(bf16[8,72,128]{2,1,0:T(8,128)(2,1)S(1)} %all-to-all-done.header_ref, f32[512,128]{1,0:T(8,128)S(1)} %get-tuple-element.43.right_ref, f32[1,4096]{1,0:T(1,128)S(1)} %get-tuple-element.28.level_ref, bf16[2,64,512]{2,1,0:T(8,128)(2,1)S(1)} %collective-permute-done.1.refs_0_, ...), custom_call_target="tpu_custom_call" | custom-call | tf_op jit(solution)/shard_map/pallas_call | solution.py:339
  62.4 5.0 %all-to-all-start.2 = ((bf16[8,72,128]{2,1,0:T(8,128)(2,1)}), bf16[8,72,128]{2,1,0:T(8,128)(2,1)S(1)}, u32[]{:S(2)}, u32[]{:S(2)}) async-start(bf16[8,72,128]{2,1,0:T(8,128)(2,1)} %get-tuple-element.45), calls=%async_computation.2 | async-start | bytes 294912 | tf_op jit(solution)/shard_map/all_to_all | solution.py:356
  67.4 2.0 %collective-permute-start.12 = (bf16[512,128]{1,0:T(8,128)(2,1)S(1)}, bf16[512,128]{1,0:T(8,128)(2,1)S(1)}, u32[]{:S(2)}, u32[]{:S(2)}) collective-permute-start(bf16[512,128]{1,0:T(8,128)(2,1)S(1)} %collective-permute-done.11.refs_4_.refs_5_), channel_id=1, source_target_pairs={{0,2},{2,0},{4,6},{6,4},{8,10},{10,8},{12,14},{14,12},{1,3},{3,1},... | collective-permute-start | bytes 393224 | tf_op jit(solution)/shard_map/ppermute | solution.py:373
  69.5 1.5 %collective-permute-start.13 = (bf16[512,128]{1,0:T(8,128)(2,1)S(1)}, bf16[512,128]{1,0:T(8,128)(2,1)S(1)}, u32[]{:S(2)}, u32[]{:S(2)}) collective-permute-start(bf16[512,128]{1,0:T(8,128)(2,1)S(1)} %collective-permute-done.11.refs_4_.refs_5_), channel_id=1, source_target_pairs={{0,4},{2,6},{4,0},{6,2},{8,12},{10,14},{12,8},{14,10},{1,5},{3,7},... | collective-permute-start | bytes 393224 | tf_op jit(solution)/shard_map/ppermute | solution.py:373
  70.9 0.6 collective-permute-start.10
  71.6 2.0 %collective-permute-start.20 = (bf16[512,128]{1,0:T(8,128)(2,1)S(1)}, bf16[512,128]{1,0:T(8,128)(2,1)S(1)}, u32[]{:S(2)}, u32[]{:S(2)}) collective-permute-start(bf16[512,128]{1,0:T(8,128)(2,1)S(1)} %collective-permute-done.19.refs_13_), channel_id=1, source_target_pairs={{0,2},{2,0},{4,6},{6,4},{8,10},{10,8},{12,14},{14,12},{1,3},{3,1},... | collective-permute-start | bytes 393224 | tf_op jit(solution)/shard_map/ppermute | solution.py:373
  73.5 1.4 %collective-permute-done.12.refs_5_.refs_6_ = bf16[512,128]{1,0:T(8,128)(2,1)S(1)} collective-permute-done((bf16[512,128]{1,0:T(8,128)(2,1)S(1)}, bf16[512,128]{1,0:T(8,128)(2,1)S(1)}, u32[]{:S(2)}, u32[]{:S(2)}) %collective-permute-start.12) | collective-permute-done | bytes 131104 | tf_op jit(solution)/shard_map/ppermute | solution.py:373
  74.9 1.6 %collective-permute-start.14 = (bf16[512,128]{1,0:T(8,128)(2,1)S(1)}, bf16[512,128]{1,0:T(8,128)(2,1)S(1)}, u32[]{:S(2)}, u32[]{:S(2)}) collective-permute-start(bf16[512,128]{1,0:T(8,128)(2,1)S(1)} %collective-permute-done.12.refs_5_.refs_6_), channel_id=1, source_target_pairs={{0,4},{2,6},{4,0},{6,2},{8,12},{10,14},{12,8},{14,10},{1,5},{3,7},... | collective-permute-start | bytes 393224 | tf_op jit(solution)/shard_map/ppermute | solution.py:373
  76.5 1.0 %collective-permute-start.16 = (bf16[512,128]{1,0:T(8,128)(2,1)S(1)}, bf16[512,128]{1,0:T(8,128)(2,1)S(1)}, u32[]{:S(2)}, u32[]{:S(2)}) collective-permute-start(bf16[512,128]{1,0:T(8,128)(2,1)S(1)} %get-tuple-element.46.refs_9_), channel_id=1, source_target_pairs={{0,2},{2,0},{4,6},{6,4},{8,10},{10,8},{12,14},{14,12},{1,3},{3,1},... | collective-permute-start | bytes 393224 | tf_op jit(solution)/shard_map/ppermute | solution.py:373
  77.9 1.4 %collective-permute-start.21 = (bf16[512,128]{1,0:T(8,128)(2,1)S(1)}, bf16[512,128]{1,0:T(8,128)(2,1)S(1)}, u32[]{:S(2)}, u32[]{:S(2)}) collective-permute-start(bf16[512,128]{1,0:T(8,128)(2,1)S(1)} %collective-permute-done.19.refs_13_), channel_id=1, source_target_pairs={{0,4},{2,6},{4,0},{6,2},{8,12},{10,14},{12,8},{14,10},{1,5},{3,7},... | collective-permute-start | bytes 393224 | tf_op jit(solution)/shard_map/ppermute | solution.py:373
  79.3 1.0 %collective-permute-start.18 = (bf16[512,128]{1,0:T(8,128)(2,1)S(1)}, bf16[512,128]{1,0:T(8,128)(2,1)S(1)}, u32[]{:S(2)}, u32[]{:S(2)}) collective-permute-start(bf16[512,128]{1,0:T(8,128)(2,1)S(1)} %collective-permute-done.17.refs_11_), channel_id=1, source_target_pairs={{0,2},{2,0},{4,6},{6,4},{8,10},{10,8},{12,14},{14,12},{1,3},{3,1},... | collective-permute-start | bytes 393224 | tf_op jit(solution)/shard_map/ppermute | solution.py:373
  80.7 1.1 %collective-permute-start.22 = (bf16[512,128]{1,0:T(8,128)(2,1)S(1)}, bf16[512,128]{1,0:T(8,128)(2,1)S(1)}, u32[]{:S(2)}, u32[]{:S(2)}) collective-permute-start(bf16[512,128]{1,0:T(8,128)(2,1)S(1)} %collective-permute-done.20.refs_14_), channel_id=1, source_target_pairs={{0,4},{2,6},{4,0},{6,2},{8,12},{10,14},{12,8},{14,10},{1,5},{3,7},... | collective-permute-start | bytes 393224 | tf_op jit(solution)/shard_map/ppermute | solution.py:373
  81.9 3.0 %shard_map.98 = bf16[2,64,4096]{2,1,0:T(8,128)(2,1)} custom-call(bf16[2,64,4096]{2,1,0:T(8,128)(2,1)} %piece_ref.3, bf16[8,128]{1,0:T(8,128)(2,1)S(1)} %get-tuple-element.26.numbers_ref, bf16[64,128]{1,0:T(8,128)(2,1)S(1)} %get-tuple-element.29.left_ref, bf16[64,128]{1,0:T(8,128)(2,1)S(1)} %get-tuple-element.31.move_ref, ...), custom_call_target="tpu_custom_call" | custom-call | tf_op jit(solution)/shard_map/pallas_call | solution.py:339
  84.9 0.8 collective-permute-done.22.refs_16_
  85.7 2.1 %shard_map.100 = (f32[4096,128]{1,0:T(8,128)}, f32[64,128]{1,0:T(8,128)}) custom-call(bf16[8,72,128]{2,1,0:T(8,128)(2,1)S(1)} %all-to-all-done.header_ref, bf16[8,64,128]{2,1,0:T(8,128)(2,1)S(1)} %all-to-all-done.1.move_ref, f32[64,128]{1,0:T(8,128)S(1)} %copy-done, f32[72,128]{1,0:T(8,128)S(1)} %convert_reduce_fusion.mine_ref, ...), custom_call_target="tpu_custom_call" | custom-call | tf_op jit(solution)/shard_map/pallas_call | solution.py:339
  (40 shorter events, 2.5 us)
Async XLA Ops:
  2.9 30.5 %copy-start.5 = (bf16[2,64,512]{2,1,0:T(8,128)(2,1)S(1)}, bf16[2,64,512]{2,1,0:T(8,128)(2,1)}, u32[]{:S(2)}) copy-start(bf16[2,64,512]{2,1,0:T(8,128)(2,1)} %get-tuple-element.35) | copy-start | bytes 393220
  3.0 33.3 %copy-start.4 = (bf16[2,64,512]{2,1,0:T(8,128)(2,1)S(1)}, bf16[2,64,512]{2,1,0:T(8,128)(2,1)}, u32[]{:S(2)}) copy-start(bf16[2,64,512]{2,1,0:T(8,128)(2,1)} %get-tuple-element.36) | copy-start | bytes 393220
  3.0 33.8 %copy-start.3 = (bf16[2,64,512]{2,1,0:T(8,128)(2,1)S(1)}, bf16[2,64,512]{2,1,0:T(8,128)(2,1)}, u32[]{:S(2)}) copy-start(bf16[2,64,512]{2,1,0:T(8,128)(2,1)} %get-tuple-element.37) | copy-start | bytes 393220
  3.0 34.0 %copy-start.2 = (bf16[2,64,512]{2,1,0:T(8,128)(2,1)S(1)}, bf16[2,64,512]{2,1,0:T(8,128)(2,1)}, u32[]{:S(2)}) copy-start(bf16[2,64,512]{2,1,0:T(8,128)(2,1)} %get-tuple-element.38) | copy-start | bytes 393220
  3.0 37.7 %copy-start.1 = (bf16[2,64,512]{2,1,0:T(8,128)(2,1)S(1)}, bf16[2,64,512]{2,1,0:T(8,128)(2,1)}, u32[]{:S(2)}) copy-start(bf16[2,64,512]{2,1,0:T(8,128)(2,1)} %get-tuple-element.39) | copy-start | bytes 393220
  3.0 20.7 %all-to-all-start = ((bf16[8,72,128]{2,1,0:T(8,128)(2,1)}), bf16[8,72,128]{2,1,0:T(8,128)(2,1)S(1)}, u32[]{:S(2)}, u32[]{:S(2)}) async-start(bf16[8,72,128]{2,1,0:T(8,128)(2,1)} %get-tuple-element.27), calls=%async_computation | async-start | bytes 294912 | tf_op jit(solution)/shard_map/all_to_all | solution.py:356
  10.4 26.6 %collective-permute-start.1 = (bf16[2,64,512]{2,1,0:T(8,128)(2,1)}, bf16[2,64,512]{2,1,0:T(8,128)(2,1)S(1)}, u32[]{:S(2)}, u32[]{:S(2)}) collective-permute-start(bf16[2,64,512]{2,1,0:T(8,128)(2,1)} %get-tuple-element.33), channel_id=1, source_target_pairs={{0,12},{2,14},{4,8},{6,10},{8,4},{10,6},{12,0},{14,2},{1,13},{3,15... | collective-permute-start | bytes 393224 | tf_op jit(solution)/shard_map/ppermute | solution.py:373
  14.2 26.4 %collective-permute-start.2 = (bf16[2,64,512]{2,1,0:T(8,128)(2,1)}, bf16[2,64,512]{2,1,0:T(8,128)(2,1)S(1)}, u32[]{:S(2)}, u32[]{:S(2)}) collective-permute-start(bf16[2,64,512]{2,1,0:T(8,128)(2,1)} %get-tuple-element.34), channel_id=1, source_target_pairs={{0,14},{2,12},{4,10},{6,8},{8,6},{10,4},{12,2},{14,0},{1,15},{3,13... | collective-permute-start | bytes 393224 | tf_op jit(solution)/shard_map/ppermute | solution.py:373
  27.9 1.3 %collective-permute-start = (f32[72,128]{1,0:T(8,128)S(1)}, f32[72,128]{1,0:T(8,128)S(1)}, u32[]{:S(2)}, u32[]{:S(2)}) collective-permute-start(f32[72,128]{1,0:T(8,128)S(1)} %get-tuple-element.30.mine_ref), channel_id=1, source_target_pairs={{0,1},{1,0},{2,3},{3,2},{4,5},{5,4},{6,7},{7,6},{8,9},{9,8},{10,11... | collective-permute-start | bytes 110600 | tf_op jit(solution)/shard_map/ppermute | solution.py:361
  30.0 29.2 %all-to-all-start.1 = ((bf16[8,64,128]{2,1,0:T(8,128)(2,1)}), bf16[8,64,128]{2,1,0:T(8,128)(2,1)S(1)}, u32[]{:S(2)}, u32[]{:S(2)}) async-start(bf16[8,64,128]{2,1,0:T(8,128)(2,1)} %get-tuple-element.42), calls=%async_computation.1 | async-start | bytes 262144 | tf_op jit(solution)/shard_map/all_to_all | solution.py:356
  33.4 15.1 %collective-permute-start.3 = (bf16[2,64,512]{2,1,0:T(8,128)(2,1)S(1)}, bf16[2,64,512]{2,1,0:T(8,128)(2,1)S(1)}, u32[]{:S(2)}, u32[]{:S(2)}) collective-permute-start(bf16[2,64,512]{2,1,0:T(8,128)(2,1)S(1)} %copy-done.5), channel_id=1, source_target_pairs={{0,6},{2,4},{4,2},{6,0},{8,14},{10,12},{12,10},{14,8},{1,7},{3,5},... | collective-permute-start | bytes 393224 | tf_op jit(solution)/shard_map/ppermute | solution.py:373
  36.2 12.8 %collective-permute-start.4 = (bf16[2,64,512]{2,1,0:T(8,128)(2,1)S(1)}, bf16[2,64,512]{2,1,0:T(8,128)(2,1)S(1)}, u32[]{:S(2)}, u32[]{:S(2)}) collective-permute-start(bf16[2,64,512]{2,1,0:T(8,128)(2,1)S(1)} %copy-done.4), channel_id=1, source_target_pairs={{0,4},{2,6},{4,0},{6,2},{8,12},{10,14},{12,8},{14,10},{1,5},{3,7},... | collective-permute-start | bytes 393224 | tf_op jit(solution)/shard_map/ppermute | solution.py:373
  36.8 12.3 %collective-permute-start.5 = (bf16[2,64,512]{2,1,0:T(8,128)(2,1)S(1)}, bf16[2,64,512]{2,1,0:T(8,128)(2,1)S(1)}, u32[]{:S(2)}, u32[]{:S(2)}) collective-permute-start(bf16[2,64,512]{2,1,0:T(8,128)(2,1)S(1)} %copy-done.3), channel_id=1, source_target_pairs={{0,2},{2,0},{4,6},{6,4},{8,10},{10,8},{12,14},{14,12},{1,3},{3,1},... | collective-permute-start | bytes 393224 | tf_op jit(solution)/shard_map/ppermute | solution.py:373
  37.0 12.1 %collective-permute-start.6 = (bf16[2,64,512]{2,1,0:T(8,128)(2,1)S(1)}, bf16[2,64,512]{2,1,0:T(8,128)(2,1)S(1)}, u32[]{:S(2)}, u32[]{:S(2)}) collective-permute-start(bf16[2,64,512]{2,1,0:T(8,128)(2,1)S(1)} %copy-done.2), channel_id=1, source_target_pairs={{0,10},{2,8},{4,14},{6,12},{8,2},{10,0},{12,6},{14,4},{1,11},{3,9}... | collective-permute-start | bytes 393224 | tf_op jit(solution)/shard_map/ppermute | solution.py:373
  40.7 11.9 %collective-permute-start.7 = (bf16[2,64,512]{2,1,0:T(8,128)(2,1)S(1)}, bf16[2,64,512]{2,1,0:T(8,128)(2,1)S(1)}, u32[]{:S(2)}, u32[]{:S(2)}) collective-permute-start(bf16[2,64,512]{2,1,0:T(8,128)(2,1)S(1)} %copy-done.1), channel_id=1, source_target_pairs={{0,8},{2,10},{4,12},{6,14},{8,0},{10,2},{12,4},{14,6},{1,9},{3,11}... | collective-permute-start | bytes 393224 | tf_op jit(solution)/shard_map/ppermute | solution.py:373
  55.2 12.3 %collective-permute-start.11 = (bf16[512,128]{1,0:T(8,128)(2,1)S(1)}, bf16[512,128]{1,0:T(8,128)(2,1)S(1)}, u32[]{:S(2)}, u32[]{:S(2)}) collective-permute-start(bf16[512,128]{1,0:T(8,128)(2,1)S(1)} %get-tuple-element.41.refs_0_.refs_1_), channel_id=1, source_target_pairs={{0,8},{2,10},{4,12},{6,14},{8,0},{10,2},{12,4},{14,6},{1,9},{3,11}... | collective-permute-start | bytes 393224 | tf_op jit(solution)/shard_map/ppermute | solution.py:373
  55.3 15.7 %collective-permute-start.9 = (bf16[512,128]{1,0:T(8,128)(2,1)S(1)}, bf16[512,128]{1,0:T(8,128)(2,1)S(1)}, u32[]{:S(2)}, u32[]{:S(2)}) collective-permute-start(bf16[512,128]{1,0:T(8,128)(2,1)S(1)} %get-tuple-element.41.refs_0_.refs_1_), channel_id=1, source_target_pairs={{0,4},{2,6},{4,0},{6,2},{8,12},{10,14},{12,8},{14,10},{1,5},{3,7},... | collective-permute-start | bytes 393224 | tf_op jit(solution)/shard_map/ppermute | solution.py:373
  58.6 12.9 %collective-permute-start.8 = (bf16[512,128]{1,0:T(8,128)(2,1)S(1)}, bf16[512,128]{1,0:T(8,128)(2,1)S(1)}, u32[]{:S(2)}, u32[]{:S(2)}) collective-permute-start(bf16[512,128]{1,0:T(8,128)(2,1)S(1)} %get-tuple-element.41.refs_0_.refs_1_), channel_id=1, source_target_pairs={{0,2},{2,0},{4,6},{6,4},{8,10},{10,8},{12,14},{14,12},{1,3},{3,1},... | collective-permute-start | bytes 393224 | tf_op jit(solution)/shard_map/ppermute | solution.py:373
  62.3 23.3 %copy-start = (f32[64,128]{1,0:T(8,128)S(1)}, f32[64,128]{1,0:T(8,128)}, u32[]{:S(2)}) copy-start(f32[64,128]{1,0:T(8,128)} %rows_ref.3) | copy-start | bytes 98308
  62.3 9.2 %collective-permute-start.19 = (bf16[512,128]{1,0:T(8,128)(2,1)S(1)}, bf16[512,128]{1,0:T(8,128)(2,1)S(1)}, u32[]{:S(2)}, u32[]{:S(2)}) collective-permute-start(bf16[512,128]{1,0:T(8,128)(2,1)S(1)} %get-tuple-element.46.refs_9_), channel_id=1, source_target_pairs={{0,8},{2,10},{4,12},{6,14},{8,0},{10,2},{12,4},{14,6},{1,9},{3,11}... | collective-permute-start | bytes 393224 | tf_op jit(solution)/shard_map/ppermute | solution.py:373
  62.4 19.4 %all-to-all-start.2 = ((bf16[8,72,128]{2,1,0:T(8,128)(2,1)}), bf16[8,72,128]{2,1,0:T(8,128)(2,1)S(1)}, u32[]{:S(2)}, u32[]{:S(2)}) async-start(bf16[8,72,128]{2,1,0:T(8,128)(2,1)} %get-tuple-element.45), calls=%async_computation.2 | async-start | bytes 294912 | tf_op jit(solution)/shard_map/all_to_all | solution.py:356
  67.4 7.4 %collective-permute-start.12 = (bf16[512,128]{1,0:T(8,128)(2,1)S(1)}, bf16[512,128]{1,0:T(8,128)(2,1)S(1)}, u32[]{:S(2)}, u32[]{:S(2)}) collective-permute-start(bf16[512,128]{1,0:T(8,128)(2,1)S(1)} %collective-permute-done.11.refs_4_.refs_5_), channel_id=1, source_target_pairs={{0,2},{2,0},{4,6},{6,4},{8,10},{10,8},{12,14},{14,12},{1,3},{3,1},... | collective-permute-start | bytes 393224 | tf_op jit(solution)/shard_map/ppermute | solution.py:373
  69.5 7.0 %collective-permute-start.13 = (bf16[512,128]{1,0:T(8,128)(2,1)S(1)}, bf16[512,128]{1,0:T(8,128)(2,1)S(1)}, u32[]{:S(2)}, u32[]{:S(2)}) collective-permute-start(bf16[512,128]{1,0:T(8,128)(2,1)S(1)} %collective-permute-done.11.refs_4_.refs_5_), channel_id=1, source_target_pairs={{0,4},{2,6},{4,0},{6,2},{8,12},{10,14},{12,8},{14,10},{1,5},{3,7},... | collective-permute-start | bytes 393224 | tf_op jit(solution)/shard_map/ppermute | solution.py:373
  70.9 7.0 %collective-permute-start.10 = (bf16[512,128]{1,0:T(8,128)(2,1)S(1)}, bf16[512,128]{1,0:T(8,128)(2,1)S(1)}, u32[]{:S(2)}, u32[]{:S(2)}) collective-permute-start(bf16[512,128]{1,0:T(8,128)(2,1)S(1)} %collective-permute-done.9.refs_2_.refs_3_), channel_id=1, source_target_pairs={{0,2},{2,0},{4,6},{6,4},{8,10},{10,8},{12,14},{14,12},{1,3},{3,1},... | collective-permute-start | bytes 393224 | tf_op jit(solution)/shard_map/ppermute | solution.py:373
  71.5 7.8 %collective-permute-start.17 = (bf16[512,128]{1,0:T(8,128)(2,1)S(1)}, bf16[512,128]{1,0:T(8,128)(2,1)S(1)}, u32[]{:S(2)}, u32[]{:S(2)}) collective-permute-start(bf16[512,128]{1,0:T(8,128)(2,1)S(1)} %get-tuple-element.46.refs_9_), channel_id=1, source_target_pairs={{0,4},{2,6},{4,0},{6,2},{8,12},{10,14},{12,8},{14,10},{1,5},{3,7},... | collective-permute-start | bytes 393224 | tf_op jit(solution)/shard_map/ppermute | solution.py:373
  71.6 9.1 %collective-permute-start.20 = (bf16[512,128]{1,0:T(8,128)(2,1)S(1)}, bf16[512,128]{1,0:T(8,128)(2,1)S(1)}, u32[]{:S(2)}, u32[]{:S(2)}) collective-permute-start(bf16[512,128]{1,0:T(8,128)(2,1)S(1)} %collective-permute-done.19.refs_13_), channel_id=1, source_target_pairs={{0,2},{2,0},{4,6},{6,4},{8,10},{10,8},{12,14},{14,12},{1,3},{3,1},... | collective-permute-start | bytes 393224 | tf_op jit(solution)/shard_map/ppermute | solution.py:373
  74.9 7.0 %collective-permute-start.14 = (bf16[512,128]{1,0:T(8,128)(2,1)S(1)}, bf16[512,128]{1,0:T(8,128)(2,1)S(1)}, u32[]{:S(2)}, u32[]{:S(2)}) collective-permute-start(bf16[512,128]{1,0:T(8,128)(2,1)S(1)} %collective-permute-done.12.refs_5_.refs_6_), channel_id=1, source_target_pairs={{0,4},{2,6},{4,0},{6,2},{8,12},{10,14},{12,8},{14,10},{1,5},{3,7},... | collective-permute-start | bytes 393224 | tf_op jit(solution)/shard_map/ppermute | solution.py:373
  76.5 8.4 %collective-permute-start.16 = (bf16[512,128]{1,0:T(8,128)(2,1)S(1)}, bf16[512,128]{1,0:T(8,128)(2,1)S(1)}, u32[]{:S(2)}, u32[]{:S(2)}) collective-permute-start(bf16[512,128]{1,0:T(8,128)(2,1)S(1)} %get-tuple-element.46.refs_9_), channel_id=1, source_target_pairs={{0,2},{2,0},{4,6},{6,4},{8,10},{10,8},{12,14},{14,12},{1,3},{3,1},... | collective-permute-start | bytes 393224 | tf_op jit(solution)/shard_map/ppermute | solution.py:373
  77.9 7.0 %collective-permute-start.21 = (bf16[512,128]{1,0:T(8,128)(2,1)S(1)}, bf16[512,128]{1,0:T(8,128)(2,1)S(1)}, u32[]{:S(2)}, u32[]{:S(2)}) collective-permute-start(bf16[512,128]{1,0:T(8,128)(2,1)S(1)} %collective-permute-done.19.refs_13_), channel_id=1, source_target_pairs={{0,4},{2,6},{4,0},{6,2},{8,12},{10,14},{12,8},{14,10},{1,5},{3,7},... | collective-permute-start | bytes 393224 | tf_op jit(solution)/shard_map/ppermute | solution.py:373
  79.3 5.6 %collective-permute-start.18 = (bf16[512,128]{1,0:T(8,128)(2,1)S(1)}, bf16[512,128]{1,0:T(8,128)(2,1)S(1)}, u32[]{:S(2)}, u32[]{:S(2)}) collective-permute-start(bf16[512,128]{1,0:T(8,128)(2,1)S(1)} %collective-permute-done.17.refs_11_), channel_id=1, source_target_pairs={{0,2},{2,0},{4,6},{6,4},{8,10},{10,8},{12,14},{14,12},{1,3},{3,1},... | collective-permute-start | bytes 393224 | tf_op jit(solution)/shard_map/ppermute | solution.py:373
  80.7 5.0 %collective-permute-start.22 = (bf16[512,128]{1,0:T(8,128)(2,1)S(1)}, bf16[512,128]{1,0:T(8,128)(2,1)S(1)}, u32[]{:S(2)}, u32[]{:S(2)}) collective-permute-start(bf16[512,128]{1,0:T(8,128)(2,1)S(1)} %collective-permute-done.20.refs_14_), channel_id=1, source_target_pairs={{0,4},{2,6},{4,0},{6,2},{8,12},{10,14},{12,8},{14,10},{1,5},{3,7},... | collective-permute-start | bytes 393224 | tf_op jit(solution)/shard_map/ppermute | solution.py:373
  81.8 3.0 %collective-permute-start.15 = (f32[72,128]{1,0:T(8,128)S(1)}, f32[72,128]{1,0:T(8,128)S(1)}, u32[]{:S(2)}, u32[]{:S(2)}) collective-permute-start(f32[72,128]{1,0:T(8,128)S(1)} %convert_reduce_fusion.mine_ref), channel_id=1, source_target_pairs={{0,1},{1,0},{2,3},{3,2},{4,5},{5,4},{6,7},{7,6},{8,9},{9,8},{10,11... | collective-permute-start | bytes 110600 | tf_op jit(solution)/shard_map/ppermute | solution.py:361
